TPU v7x, 128 devices: a whole 4x4x4 slice. The times are simulated.
128 devices in a mesh: ctx: 8 (over x_hi, y), exp: 16 (over z, x_lo, core).
Axes of the slice: x: 4 (x_hi: 2, x_lo: 2; x = x_hi * 2 + x_lo), y: 4, z: 4, core: 2. Of those that a mesh axis runs over, the one named last changes fastest.
Arguments:
- queries: bfloat16 [16384, 2048], P('ctx', 'exp'), may hold values from -6 to 6
- keys: bfloat16 [16384, 2048], P('ctx', 'exp'), may hold values from -6 to 6
- values: bfloat16 [16384, 2048], P('ctx', 'exp'), may hold values from -6 to 6
- gate_input: bfloat16 [16384, 2048], P(('ctx', 'exp')), may hold values from -6 to 6
- route_ids: int32 [16384, 2], P(('ctx', 'exp')), may hold values from 0 to 31, all different within a row; in each aligned block of 128 rows (0 to 127, 128 to 255, ...) at most 16 rows name the same one
- route_gates: float32 [16384, 2], P(('ctx', 'exp')), may hold values from 0.1 to 1
- w_gate: bfloat16 [32, 2048, 512], P('exp'), may hold values from -0.125 to 0.125
- w_up: bfloat16 [32, 2048, 512], P('exp'), may hold values from -0.125 to 0.125
- w_down: bfloat16 [32, 512, 2048], P('exp'), may hold values from -0.25 to 0.25
- out_grad: bfloat16 [16384, 2048], P(('ctx', 'exp')), may hold values from -6 to 6
Outputs:
- normed: bfloat16 [16384, 2048], P(('ctx', 'exp'))
- mixed: bfloat16 [16384, 2048], P(('ctx', 'exp'))
- normed_grad: bfloat16 [16384, 2048], P(('ctx', 'exp'))
- w_gate_grad: bfloat16 [32, 2048, 512], P('exp', 'ctx')
- w_up_grad: bfloat16 [32, 2048, 512], P('exp', 'ctx')
- w_down_grad: bfloat16 [32, 512, 2048], P('exp', None, 'ctx')
Inputs may be any that keep to these rules, and one draw needn't show every extreme that they name: `route_ids`: each position names two different experts. Within the 128 positions of one aligned block no expert is named by more than 16 routes, and in every draw some expert is named by exactly 16 routes of some block.
All inputs are finite; a program needn't handle non-finite values.
Results may differ from a plain program's by a relative error of at most 0.013.
Values may be sent and summed in bfloat16 or wider, within the bound.
No kernel may reach another device: no remote copies, remote signals or barrier semaphores. Data moves between devices by JAX's collectives and lax.ppermute only.
A program may use at most 128 MiB of HBM per device.

v0:
```python
import math

import jax
import jax.numpy as jnp
from jax import lax
from jax.experimental import pallas as pl
from jax.experimental.pallas import tpu as pltpu
from jax.sharding import PartitionSpec as P


HEAD_DIM = 128
EXPERTS = 32
CAP = 16
N_EXP = 16
TOK = 128
ROWS = N_EXP * CAP
TQ = 512
TK = 256
F32 = jnp.float32
BF16 = jnp.bfloat16


def vmem():
    return pl.BlockSpec(memory_space=pltpu.VMEM)


def smem():
    return pl.BlockSpec(memory_space=pltpu.SMEM)


def mm(a, b, ca, cb):
    return lax.dot_general(a, b, (((ca,), (cb,)), ((), ())), preferred_element_type=F32)


def half_silu(scores):
    h = scores * (0.5 / math.sqrt(HEAD_DIM))
    return h + h * jnp.tanh(h)


def attend_tile(q, key_t, value, masked_from):
    w = half_silu(mm(q, key_t, 1, 0))
    if masked_from is not None:
        row = lax.broadcasted_iota(jnp.int32, w.shape, 0)
        col = lax.broadcasted_iota(jnp.int32, w.shape, 1)
        w = jnp.where(row >= col + masked_from, w, 0.0)
    return mm(w.astype(BF16), value, 1, 0)


def add_block(q_ref, turned, value, acc, rows):
    def q_step(i, carry):
        rows_i = pl.ds(pl.multiple_of(i * TQ, TQ), TQ)
        q = q_ref[rows_i, :]
        part = acc[rows_i, :]
        for j in range(rows // TK):
            rows_j = pl.ds(j * TK, TK)
            part = part + attend_tile(q, turned[:, rows_j], value[rows_j, :], None)
        acc[rows_i, :] = part
        return carry

    lax.fori_loop(0, rows // TQ, q_step, 0)


def attend_own(q, kv):
    rows = q.shape[0]

    def kernel(q_ref, kv, acc, turned):
        turned[...] = kv[0].T
        for i in range(rows // TQ):
            rows_i = pl.ds(i * TQ, TQ)
            part = jnp.zeros((TQ, HEAD_DIM), F32)
            for j in range((i + 1) * TQ // TK):
                rows_j = pl.ds(j * TK, TK)
                gap = j * TK - i * TQ
                part = part + attend_tile(
                    q_ref[rows_i, :], turned[:, rows_j], kv[1, rows_j, :], gap if gap >= 0 else None
                )
            acc[rows_i, :] = part

    return pl.pallas_call(
        kernel,
        out_shape=jax.ShapeDtypeStruct((rows, HEAD_DIM), F32),
        in_specs=[vmem()] * 2,
        out_specs=vmem(),
        scratch_shapes=[pltpu.VMEM((HEAD_DIM, rows), BF16)],
        name="attend_own",
    )(q, kv)


def attend(flags, q, kvs, base, extra, out_type):
    rows = q.shape[0]
    count = len(kvs)
    given = [v for v in (base, extra) if v is not None]

    def kernel(*refs):
        flags_ref, q_ref = refs[0], refs[1]
        kv_refs = refs[2 : 2 + count]
        base_ref = refs[2 + count] if base is not None else None
        extra_ref = refs[1 + count + len(given)] if extra is not None else None
        out, acc, turned, value = refs[-4:]
        acc[...] = jnp.zeros_like(acc) if base is None else base_ref[...]

        def one(n, carry):
            @pl.when(flags_ref[n] != 0)
            def _():
                for m, kv in enumerate(kv_refs):

                    @pl.when(n == m)
                    def _(kv=kv):
                        turned[...] = kv[0].T
                        value[...] = kv[1]

                add_block(q_ref, turned, value, acc, rows)

            return carry

        lax.fori_loop(0, count, one, 0)
        total = acc[...]
        if extra is not None:
            total = total + extra_ref[...].astype(F32)
        out[...] = total.astype(out_type)

    return pl.pallas_call(
        kernel,
        out_shape=jax.ShapeDtypeStruct((rows, HEAD_DIM), out_type),
        in_specs=[smem()] + [vmem()] * (1 + count + len(given)),
        out_specs=vmem(),
        scratch_shapes=[
            pltpu.VMEM((rows, HEAD_DIM), F32),
            pltpu.VMEM((HEAD_DIM, rows), BF16),
            pltpu.VMEM((rows, HEAD_DIM), BF16),
        ],
    )(flags, q, *kvs, *given)


def route_kernel(ids_ref, gates_ref, grad_ref, pick0_ref, pick1_ref, send_ref):
    ids = ids_ref[...]
    expert = lax.broadcasted_iota(jnp.int32, (EXPERTS, TOK), 0)
    one0 = (expert == ids[0:1, :]).astype(F32)
    one1 = (expert == ids[1:2, :]).astype(F32)
    earlier = lax.broadcasted_iota(jnp.int32, (TOK, TOK), 0) < lax.broadcasted_iota(
        jnp.int32, (TOK, TOK), 1
    )
    counts = mm((one0 + one1).astype(BF16), earlier.astype(F32).astype(BF16), 1, 0)
    slot0 = jnp.sum(one0 * counts, axis=0, keepdims=True).astype(jnp.int32)
    slot1 = jnp.sum(one1 * (counts + one0), axis=0, keepdims=True).astype(jnp.int32)
    row = lax.broadcasted_iota(jnp.int32, (EXPERTS * CAP, TOK), 0)
    pick0 = (row == ids[0:1, :] * CAP + slot0).astype(F32).astype(BF16)
    pick1 = (row == ids[1:2, :] * CAP + slot1).astype(F32).astype(BF16)
    pick0_ref[...] = pick0
    pick1_ref[...] = pick1
    grad = grad_ref[...].astype(F32)
    scaled0 = (gates_ref[:, 0:1] * grad).astype(BF16)
    scaled1 = (gates_ref[:, 1:2] * grad).astype(BF16)
    sent = mm(pick0, scaled0, 1, 0) + mm(pick1, scaled1, 1, 0)
    send_ref[...] = sent.astype(BF16).reshape(send_ref.shape)


def norm_kernel(tok_ref, gate_ref, pick0_ref, pick1_ref, normed_ref, send_ref):
    heads = [tok_ref[h].astype(F32) for h in range(tok_ref.shape[0])]
    width = HEAD_DIM * len(heads)
    total = heads[0]
    for h in heads[1:]:
        total = total + h
    mean = jnp.sum(total, axis=1, keepdims=True) * (1.0 / width)
    squares = None
    for h in heads:
        c = h - mean
        squares = c * c if squares is None else squares + c * c
    variance = jnp.sum(squares, axis=1, keepdims=True) * (1.0 / width)
    scale = lax.rsqrt(variance + 1e-05)
    for n, h in enumerate(heads):
        cols = slice(n * HEAD_DIM, (n + 1) * HEAD_DIM)
        normed_ref[:, cols] = ((h - mean) * scale * gate_ref[:, cols].astype(F32)).astype(BF16)
    pick = pick0_ref[...] + pick1_ref[...]
    send_ref[...] = mm(pick, normed_ref[...], 1, 0).astype(BF16).reshape(send_ref.shape)


def hidden_grad_kernel(grad_ref, down_ref, out_ref):
    grads = grad_ref[...].reshape(ROWS, grad_ref.shape[2])
    out_ref[0] = mm(grads, down_ref[0], 1, 1)


def expert_in_kernel(in_ref, hg_ref, gate_ref, up_ref, hidden_ref, gg_ref, ug_ref):
    rows = in_ref[...].reshape(ROWS, in_ref.shape[2])
    gate_pre = mm(rows, gate_ref[0], 1, 0)
    up_pre = mm(rows, up_ref[0], 1, 0)
    sigma = jax.nn.sigmoid(gate_pre)
    silu = gate_pre * sigma
    hidden_grad = hg_ref[0]
    hidden_ref[0] = (silu * up_pre).astype(BF16)
    gg_ref[0] = (hidden_grad * up_pre * (sigma * (1.0 + gate_pre * (1.0 - sigma)))).astype(BF16)
    ug_ref[0] = (hidden_grad * silu).astype(BF16)


def weight_grad(order, source, act, groups, turned):
    cols = source.shape[2] // 8
    hid = act.shape[2]
    piece = (hid, cols) if turned else (cols, hid)

    def kernel(order_ref, src, act_ref, *outs):
        for e in range(2):
            side = act_ref[e].T if turned else act_ref[e]
            done = 0
            for out, count in zip(outs, groups):
                for n in range(count):
                    at = pl.ds(pl.multiple_of(order_ref[done] * cols, cols), cols)
                    rows = src[:, e * CAP : (e + 1) * CAP, at].reshape(ROWS, cols)
                    grad = mm(side, rows, 1, 0) if turned else mm(rows, side, 0, 0)
                    out[n, e] = grad.astype(BF16)
                    done += 1

    return pl.pallas_call(
        kernel,
        out_shape=tuple(jax.ShapeDtypeStruct((c, 2, *piece), BF16) for c in groups),
        in_specs=[smem(), vmem(), vmem()],
        out_specs=(vmem(),) * len(groups),
    )(order, source, act)


def expert_back_kernel(hidden_ref, down_ref, gg_ref, ug_ref, gate_ref, up_ref, out_ref):
    step = pl.program_id(0)
    shape = out_ref.shape

    @pl.when(step < 2)
    def _():
        out_ref[...] = mm(hidden_ref[0], down_ref[0], 1, 0).astype(BF16).reshape(shape)

    @pl.when(step >= 2)
    def _():
        total = mm(gg_ref[0], gate_ref[0], 1, 1) + mm(ug_ref[0], up_ref[0], 1, 1)
        out_ref[...] = total.astype(BF16).reshape(shape)


def pair_sum_kernel(keep_ref, got_ref, *outs):
    for n, out in enumerate(outs):
        out[...] = (keep_ref[n].astype(F32) + got_ref[n].astype(F32)).astype(out.dtype)


def mixed_kernel(back_ref, pick0_ref, pick1_ref, gates_ref, out_ref):
    back = back_ref[:, 0:2].reshape(EXPERTS * CAP, back_ref.shape[3])
    first = mm(pick0_ref[...], back, 0, 0) * gates_ref[:, 0:1]
    second = mm(pick1_ref[...], back, 0, 0) * gates_ref[:, 1:2]
    out_ref[...] = (first + second).astype(BF16)


def normed_grad_kernel(back_ref, pick0_ref, pick1_ref, out_ref):
    back = back_ref[:, 2:4].reshape(EXPERTS * CAP, back_ref.shape[3])
    pick = pick0_ref[...] + pick1_ref[...]
    out_ref[...] = mm(pick, back, 0, 0).astype(BF16)


def move_y(value, distance, keep=lambda hi, y: True):
    pairs = [
        (hi * 4 + y, hi * 4 + (y + distance) % 4)
        for hi in range(2)
        for y in range(4)
        if keep(hi, y)
    ]
    return lax.ppermute(value, "ctx", pairs)


def move_x(value, both=True):
    pairs = [(y, 4 + y) for y in range(4)]
    if both:
        pairs += [(4 + y, y) for y in range(4)]
    return lax.ppermute(value, "ctx", pairs)


def exchange(value):
    return lax.all_to_all(value, "exp", split_axis=0, concat_axis=0, tiled=True)


def step(queries, keys, values, gate_input, route_ids, route_gates, w_gate, w_up, w_down, out_grad):
    width = gate_input.shape[1]
    hid = w_gate.shape[2]
    ctx = lax.axis_index("ctx")
    hi, y = ctx // 4, ctx % 4
    full = jax.ShapeDtypeStruct
    down_x = [(n, 4 + n) for n in range(4)]
    up_x = [(4 + n, n) for n in range(4)]

    kv = jnp.stack([keys, values])
    lent_q = lax.ppermute(queries, "ctx", up_x)
    from_x = lax.ppermute(kv, "ctx", down_x)
    from_y1 = move_y(kv, 1, lambda hi, y: hi == 0 or y < 3)
    from_y2 = move_y(kv, 2, lambda hi, y: hi == 0 or y < 2)
    from_y3 = move_y(kv, 3, lambda hi, y: y == 0)
    from_xy = move_y(from_x, 3, lambda hi, y: hi == 1)
    from_xx = lax.ppermute(from_y2, "ctx", down_x)

    pick0, pick1, send_grads = pl.pallas_call(
        route_kernel,
        out_shape=(
            full((EXPERTS * CAP, TOK), BF16),
            full((EXPERTS * CAP, TOK), BF16),
            full((N_EXP, 2 * CAP, width), BF16),
        ),
        in_specs=[vmem()] * 3,
        out_specs=(vmem(),) * 3,
        name="route",
    )(route_ids.T, route_gates, out_grad)
    recv_grads = exchange(send_grads)

    flag = lambda *conds: jnp.stack([c.astype(jnp.int32) for c in conds])
    low, high = hi == 0, hi == 1
    acc = attend_own(queries, kv)
    lent = attend(flag(low, low), lent_q, [kv, from_y1], None, None, BF16)
    returned = lax.ppermute(lent, "ctx", down_x)
    acc = attend(flag(y >= 1, y >= 2, y >= 3), queries, [from_y1, from_y2, from_y3], acc, None, F32)
    attended = attend(flag(high, high), queries, [from_xx, from_xy], acc, returned, BF16)

    expert_block = pl.BlockSpec((N_EXP, CAP, width), lambda e: (0, e, 0))
    in_weight = pl.BlockSpec((1, width, hid), lambda e: (e, 0, 0))
    out_weight = pl.BlockSpec((1, hid, width), lambda e: (e, 0, 0))
    act_block = pl.BlockSpec((1, ROWS, hid), lambda e: (e, 0, 0))
    attended, recv_grads = lax.optimization_barrier((attended, recv_grads))
    token_heads = exchange(attended.reshape(N_EXP, TOK, HEAD_DIM))
    hidden_grad = pl.pallas_call(
        hidden_grad_kernel,
        grid=(2,),
        out_shape=full((2, ROWS, hid), F32),
        in_specs=[expert_block, out_weight],
        out_specs=act_block,
        name="hidden_grad",
    )(recv_grads, w_down)
    normed, send_inputs = pl.pallas_call(
        norm_kernel,
        out_shape=(full((TOK, width), BF16), full((N_EXP, 2 * CAP, width), BF16)),
        in_specs=[vmem()] * 4,
        out_specs=(vmem(),) * 2,
        name="norm",
    )(token_heads, gate_input, pick0, pick1)
    recv_inputs = exchange(send_inputs)

    act = full((2, ROWS, hid), BF16)
    hidden, gate_grad, up_grad = pl.pallas_call(
        expert_in_kernel,
        grid=(2,),
        out_shape=(act, act, act),
        in_specs=[expert_block, act_block, in_weight, in_weight],
        out_specs=(act_block,) * 3,
        name="expert_in",
    )(recv_inputs, hidden_grad, w_gate, w_up)

    turn = jnp.arange(4, dtype=jnp.int32)
    x_order = jnp.concatenate([(1 - hi) * 4 + (y + turn) % 4, hi * 4 + (y + turn) % 4])
    far = (turn + 1) % 4
    y_order = jnp.stack(
        [hi * 4 + (y + far) % 4, (1 - hi) * 4 + (y + far) % 4], axis=1
    ).reshape(8)
    up_send, up_keep = weight_grad(x_order, recv_inputs, up_grad, (4, 4), False)
    up_got = move_x(up_send)
    ga = weight_grad(y_order, recv_inputs, gate_grad, (2, 2, 2, 2), False)
    got_g = []
    for n in range(3):
        got_g.append(move_y(ga[n], n + 1))
    do = weight_grad(y_order, recv_grads, hidden, (2, 2, 2, 2), True)
    held = lax.optimization_barrier((*do[:3], *got_g))
    got_g = held[3:]
    got_d = []
    for n in range(3):
        got_d.append(move_y(held[n], n + 1))

    early = lambda shape: pl.BlockSpec((1, *shape), lambda n: (jnp.minimum(n, 1), 0, 0))
    late = lambda shape: pl.BlockSpec((1, *shape), lambda n: (jnp.maximum(n - 2, 0), 0, 0))
    expert_back = pl.pallas_call(
        expert_back_kernel,
        grid=(4,),
        out_shape=full((N_EXP, 4, CAP, width), BF16),
        in_specs=[
            early((ROWS, hid)),
            early((hid, width)),
            late((ROWS, hid)),
            late((ROWS, hid)),
            late((width, hid)),
            late((width, hid)),
        ],
        out_specs=pl.BlockSpec((N_EXP, 1, CAP, width), lambda n: (0, n, 0, 0)),
        name="expert_back",
    )(hidden, w_down, gate_grad, up_grad, w_gate, w_up)
    back = exchange(expert_back)

    token = full((TOK, width), BF16)
    mixed = pl.pallas_call(
        mixed_kernel, out_shape=token, in_specs=[vmem()] * 4, out_specs=vmem(), name="mixed"
    )(back, pick0, pick1, route_gates)
    normed_grad = pl.pallas_call(
        normed_grad_kernel, out_shape=token, in_specs=[vmem()] * 3, out_specs=vmem(), name="ngrad"
    )(back, pick0, pick1)

    wide = lambda v: v.astype(F32)

    def over_row(own, got):
        sums = wide(own) + wide(got[0]) + wide(got[1]) + wide(got[2])
        return sums[0], sums[1].astype(BF16)

    gate_part, gate_send = over_row(ga[3], got_g)
    gate_got = move_x(gate_send)
    gate_sum = (gate_part + wide(gate_got)).astype(BF16)
    quarter = up_keep.shape[1:]
    up_part, *up_rest = pl.pallas_call(
        pair_sum_kernel,
        out_shape=(full(quarter, F32),) + (full(quarter, BF16),) * 3,
        in_specs=[vmem()] * 2,
        out_specs=(vmem(),) * 4,
        name="pair_sum",
    )(up_keep, up_got)
    got_u = []
    for n in (1, 2, 3):
        got_u.append(move_y(up_rest[n - 1], n))
    up_sum = (up_part + wide(got_u[0]) + wide(got_u[1]) + wide(got_u[2])).astype(BF16)
    down_part, down_send = over_row(do[3], got_d)
    down_got = move_x(down_send)
    down_sum = (down_part + wide(down_got)).astype(BF16)
    return (normed, mixed, normed_grad, gate_sum, up_sum, down_sum)


def solution(mesh):
    in_specs = (
        P("ctx", "exp"),
        P("ctx", "exp"),
        P("ctx", "exp"),
        P(("ctx", "exp"), None),
        P(("ctx", "exp"), None),
        P(("ctx", "exp"), None),
        P("exp", None, None),
        P("exp", None, None),
        P("exp", None, None),
        P(("ctx", "exp"), None),
    )
    out_specs = (
        P(("ctx", "exp"), None),
        P(("ctx", "exp"), None),
        P(("ctx", "exp"), None),
        P("exp", "ctx", None),
        P("exp", "ctx", None),
        P("exp", None, "ctx"),
    )
    return jax.shard_map(step, mesh=mesh, in_specs=in_specs, out_specs=out_specs, check_vma=False)
```

profile of v0, /device:TPU:0, one launch (start us, length us, event | category | flops | bytes accessed | tf_op | source)
XLA Modules:
  0.0 328.8 jit_solution(2844865321215552948)
XLA Ops:
  0.6 1.3 pad_maximum_fusion.kv.refs_2_
  2.0 5.2 %collective-permute-start = (bf16[2,2048,128]{2,1,0:T(8,128)(2,1)S(1)}, bf16[2,2048,128]{2,1,0:T(8,128)(2,1)}, u32[]{:S(2)}, u32[]{:S(2)}) collective-permute-start(bf16[2,2048,128]{2,1,0:T(8,128)(2,1)S(1)} %pad_maximum_fusion.kv.refs_2_), channel_id=1, source_target_pairs={{0,32},{16,48},{32,0},{48,16},{64,96},{80,112},{1,33},{17,49},{33,... | collective-permute-start | bytes 3145736 | tf_op jit(solution)/shard_map/ppermute | solution.py:259
  7.2 6.9 %collective-permute-start.2 = (bf16[2,2048,128]{2,1,0:T(8,128)(2,1)S(1)}, bf16[2,2048,128]{2,1,0:T(8,128)(2,1)}, u32[]{:S(2)}, u32[]{:S(2)}) collective-permute-start(bf16[2,2048,128]{2,1,0:T(8,128)(2,1)S(1)} %pad_maximum_fusion.kv.refs_2_), channel_id=1, source_target_pairs={{0,64},{16,80},{32,96},{48,112},{1,65},{17,81},{33,97},{49,113},{2... | collective-permute-start | bytes 3145736 | tf_op jit(solution)/shard_map/ppermute | solution.py:284
  14.1 0.7 copy.18.gates_ref
  14.8 3.9 %route.1 = (bf16[512,128]{1,0:T(8,128)(2,1)}, bf16[512,128]{1,0:T(8,128)(2,1)}, bf16[16,32,2048]{2,1,0:T(8,128)(2,1)}) custom-call(s32[2,128]{1,0:T(2,128)} %bitcast.28, f32[128,2]{1,0:T(8,128)} %copy.18.gates_ref, bf16[128,2048]{1,0:T(8,128)(2,1)} %grad_ref.1), custom_call_target="tpu_custom_call" | custom-call | tf_op jit(solution)/shard_map/route/pallas_call | solution.py:291
  18.7 5.4 %all-to-all-start = ((bf16[16,32,2048]{2,1,0:T(8,128)(2,1)}), bf16[16,32,2048]{2,1,0:T(8,128)(2,1)S(1)}, u32[]{:S(2)}, u32[]{:S(2)}) async-start(bf16[16,32,2048]{2,1,0:T(8,128)(2,1)} %get-tuple-element.36), calls=%async_computation | async-start | bytes 4194304 | tf_op jit(solution)/shard_map/all_to_all | solution.py:270
  24.2 2.6 collective-permute-start.4
  26.8 1.3 collective-permute-start.6
  28.1 5.5 %collective-permute-start.5 = (bf16[2,2048,128]{2,1,0:T(8,128)(2,1)S(1)}, bf16[2,2048,128]{2,1,0:T(8,128)(2,1)}, u32[]{:S(2)}, u32[]{:S(2)}) collective-permute-start(bf16[2,2048,128]{2,1,0:T(8,128)(2,1)S(1)} %pad_maximum_fusion.kv.refs_2_), channel_id=1, source_target_pairs={{0,48},{64,112},{1,49},{65,113},{2,50},{66,114},{3,51},{67,115},{4... | collective-permute-start | bytes 3145736 | tf_op jit(solution)/shard_map/ppermute | solution.py:259
  33.5 7.8 %collective-permute-start.1 = (bf16[2,2048,128]{2,1,0:T(8,128)(2,1)}, bf16[2,2048,128]{2,1,0:T(8,128)(2,1)}, u32[]{:S(2)}, u32[]{:S(2)}) collective-permute-start(bf16[2,2048,128]{2,1,0:T(8,128)(2,1)} %collective-permute-done.refs_3_), channel_id=1, source_target_pairs={{0,64},{16,80},{32,96},{48,112},{1,65},{17,81},{33,97},{49,113},{2... | collective-permute-start | bytes 3145736 | tf_op jit(solution)/shard_map/ppermute | solution.py:289
  41.4 1.6 collective-permute-start.3
  43.0 0.6 add_convert_fusion.3.refs_0_
  43.6 16.2 %collective-permute-done.6.refs_1_ = bf16[2048,128]{1,0:T(8,128)(2,1)} collective-permute-done((bf16[2048,128]{1,0:T(8,128)(2,1)}, bf16[2048,128]{1,0:T(8,128)(2,1)}, u32[]{:S(2)}, u32[]{:S(2)}) %collective-permute-start.6) | collective-permute-done | bytes 524320 | tf_op jit(solution)/shard_map/ppermute | solution.py:283
  59.8 13.8 %shard_map.146 = bf16[2048,128]{1,0:T(8,128)(2,1)} custom-call(s32[2]{0:T(128)} %add_convert_fusion.3.refs_0_, bf16[2048,128]{1,0:T(8,128)(2,1)} %collective-permute-done.6.refs_1_, bf16[2,2048,128]{2,1,0:T(8,128)(2,1)} %copy-done.2, bf16[2,2048,128]{2,1,0:T(8,128)(2,1)} %collective-permute-done.4.refs_2_.refs_3_), custom_call_target="tpu_custom_call" | custom-call | tf_op jit(solution)/shard_map/pallas_call | solution.py:122
  73.7 2.1 collective-permute-start.7
  75.7 5.6 %attend_own.1.refs_5_ = f32[2048,128]{1,0:T(8,128)} custom-call(bf16[2048,128]{1,0:T(8,128)(2,1)} %refs_1_.3, bf16[2,2048,128]{2,1,0:T(8,128)(2,1)} %copy-done.2), custom_call_target="tpu_custom_call" | custom-call | tf_op jit(solution)/shard_map/attend_own/pallas_call | solution.py:79
  81.3 0.6 add_convert_fusion.1.refs_0_
  81.9 0.6 add_convert_fusion.2.refs_0_
  82.5 3.5 %shard_map.145.refs_4_ = f32[2048,128]{1,0:T(8,128)} custom-call(s32[3]{0:T(128)} %add_convert_fusion.2.refs_0_, bf16[2048,128]{1,0:T(8,128)(2,1)} %refs_1_.3, bf16[2,2048,128]{2,1,0:T(8,128)(2,1)} %collective-permute-done.4.refs_2_.refs_3_, bf16[2,2048,128]{2,1,0:T(8,128)(2,1)} %collective-permute-done.refs_3_, ...), custom_call_target="tpu_custom_call" | custom-call | tf_op jit(solution)/shard_map/pallas_call | solution.py:122
  86.0 5.5 %collective-permute-done.7.refs_5_ = bf16[2048,128]{1,0:T(8,128)(2,1)} collective-permute-done((bf16[2048,128]{1,0:T(8,128)(2,1)}, bf16[2048,128]{1,0:T(8,128)(2,1)}, u32[]{:S(2)}, u32[]{:S(2)}) %collective-permute-start.7) | collective-permute-done | bytes 524320 | tf_op jit(solution)/shard_map/ppermute | solution.py:308
  91.6 3.1 shard_map.147
  94.7 16.3 %all_to_all.20.tok_ref = bf16[16,128,128]{2,1,0:T(8,128)(2,1)} all-to-all(bf16[16,128,128]{2,1,0:T(8,128)(2,1)} %bitcast.25), channel_id=1, replica_groups=mesh['ctx'=8,'exp'=16] {'exp'}, dimensions={0} | all-to-all | bytes 1048576 | tf_op jit(solution)/shard_map/all_to_all | solution.py:270
  111.0 3.7 %norm.1 = (bf16[128,2048]{1,0:T(8,128)(2,1)}, bf16[16,32,2048]{2,1,0:T(8,128)(2,1)}) custom-call(bf16[16,128,128]{2,1,0:T(8,128)(2,1)} %all_to_all.20.tok_ref, bf16[128,2048]{1,0:T(8,128)(2,1)} %gate_ref.3, bf16[512,128]{1,0:T(8,128)(2,1)} %get-tuple-element.38.pick0_ref, bf16[512,128]{1,0:T(8,128)(2,1)} %get-tuple-element.39.pick1_ref), custom_call_target="tpu_custom_call" | custom-call | tf_op jit(solution)/shard_map/norm/pallas_call | solution.py:326
  114.7 3.7 %all-to-all-start.2 = ((bf16[16,32,2048]{2,1,0:T(8,128)(2,1)}), bf16[16,32,2048]{2,1,0:T(8,128)(2,1)S(1)}, u32[]{:S(2)}, u32[]{:S(2)}) async-start(bf16[16,32,2048]{2,1,0:T(8,128)(2,1)} %get-tuple-element.41), calls=%async_computation.2 | async-start | bytes 4194304 | tf_op jit(solution)/shard_map/all_to_all | solution.py:270
  118.5 4.5 %hidden_grad.1.hg_ref = f32[2,256,512]{2,1,0:T(8,128)} custom-call(bf16[16,32,2048]{2,1,0:T(8,128)(2,1)} %copy-done.1, bf16[2,512,2048]{2,1,0:T(8,128)(2,1)} %down_ref.3), custom_call_target="tpu_custom_call" | custom-call | tf_op jit(solution)/shard_map/hidden_grad/pallas_call | solution.py:318
  122.9 23.3 %all-to-all-done.2.in_ref.src = bf16[16,32,2048]{2,1,0:T(8,128)(2,1)S(1)} async-done(((bf16[16,32,2048]{2,1,0:T(8,128)(2,1)}), bf16[16,32,2048]{2,1,0:T(8,128)(2,1)S(1)}, u32[]{:S(2)}, u32[]{:S(2)}) %all-to-all-start.2) | async-done | bytes 2097184 | tf_op jit(solution)/shard_map/all_to_all | solution.py:270
  146.2 1.3 copy-done
  147.5 6.6 %expert_in.1 = (bf16[2,256,512]{2,1,0:T(8,128)(2,1)}, bf16[2,256,512]{2,1,0:T(8,128)(2,1)}, bf16[2,256,512]{2,1,0:T(8,128)(2,1)}) custom-call(bf16[16,32,2048]{2,1,0:T(8,128)(2,1)} %copy-done, f32[2,256,512]{2,1,0:T(8,128)} %hidden_grad.1.hg_ref, bf16[2,2048,512]{2,1,0:T(8,128)(2,1)} %gate_ref.5, bf16[2,2048,512]{2,1,0:T(8,128)(2,1)} %up_ref.3), custom_call_target="tpu_custom_call" | custom-call | tf_op jit(solution)/shard_map/expert_in/pallas_call | solution.py:336
  154.1 10.0 %expert_back.1 = bf16[16,4,16,2048]{3,2,1,0:T(8,128)(2,1)} custom-call(bf16[2,256,512]{2,1,0:T(8,128)(2,1)} %get-tuple-element.43.hidden_ref.act_ref, bf16[2,512,2048]{2,1,0:T(8,128)(2,1)} %down_ref.3, bf16[2,256,512]{2,1,0:T(8,128)(2,1)} %get-tuple-element.44.gg_ref.act_ref, bf16[2,256,512]{2,1,0:T(8,128)(2,1)} %get-tuple-element.45.ug_ref.act_ref, ...), custom_call_target="tpu_custom_call" | custom-call | tf_op jit(solution)/shard_map/expert_back/pallas_call | solution.py:366
  164.1 4.5 %all-to-all-start.3 = ((bf16[16,4,16,2048]{3,2,1,0:T(8,128)(2,1)}), bf16[16,4,16,2048]{3,2,1,0:T(8,128)(2,1)}, u32[]{:S(2)}, u32[]{:S(2)}) async-start(bf16[16,4,16,2048]{3,2,1,0:T(8,128)(2,1)} %expert_back.1), calls=%async_computation.3 | async-start | bytes 8388608 | tf_op jit(solution)/shard_map/all_to_all | solution.py:270
  168.7 0.1 pad_add_fusion
  168.8 0.6 reshape.104.order_ref
  169.4 4.6 %shard_map.148 = (bf16[2,2,256,512]{3,2,1,0:T(8,128)(2,1)}, bf16[2,2,256,512]{3,2,1,0:T(8,128)(2,1)}, bf16[2,2,256,512]{3,2,1,0:T(8,128)(2,1)}, bf16[2,2,256,512]{3,2,1,0:T(8,128)(2,1)}) custom-call(s32[8]{0:T(128)} %reshape.104.order_ref, bf16[16,32,2048]{2,1,0:T(8,128)(2,1)} %copy-done, bf16[2,256,512]{2,1,0:T(8,128)(2,1)} %get-tuple-element.44.gg_ref.act_ref), custom_call_target="tpu_custom_call" | custom-call | tf_op jit(solution)/shard_map/pallas_call | solution.py:212
  173.9 8.3 %collective-permute-start.10 = (bf16[2,2,256,512]{3,2,1,0:T(8,128)(2,1)}, bf16[2,2,256,512]{3,2,1,0:T(8,128)(2,1)S(1)}, u32[]{:S(2)}, u32[]{:S(2)}) collective-permute-start(bf16[2,2,256,512]{3,2,1,0:T(8,128)(2,1)} %get-tuple-element.52), channel_id=1, source_target_pairs={{0,48},{16,0},{32,16},{48,32},{64,112},{80,64},{96,80},{112,96},{1... | collective-permute-start | bytes 3145736 | tf_op jit(solution)/shard_map/ppermute | solution.py:259
  182.3 1.5 collective-permute-start.9
  183.7 0.6 pad_add_fusion.1.order_ref
  184.3 4.8 %shard_map.150 = (bf16[4,2,256,512]{3,2,1,0:T(8,128)(2,1)}, bf16[4,2,256,512]{3,2,1,0:T(8,128)(2,1)}) custom-call(s32[8]{0:T(128)} %pad_add_fusion.1.order_ref, bf16[16,32,2048]{2,1,0:T(8,128)(2,1)} %copy-done, bf16[2,256,512]{2,1,0:T(8,128)(2,1)} %get-tuple-element.45.ug_ref.act_ref), custom_call_target="tpu_custom_call" | custom-call | tf_op jit(solution)/shard_map/pallas_call | solution.py:212
  189.2 8.7 %collective-permute-start.12 = (bf16[4,2,256,512]{3,2,1,0:T(8,128)(2,1)}, bf16[4,2,256,512]{3,2,1,0:T(8,128)(2,1)}, u32[]{:S(2)}, u32[]{:S(2)}) collective-permute-start(bf16[4,2,256,512]{3,2,1,0:T(8,128)(2,1)} %get-tuple-element.57), channel_id=1, source_target_pairs={{0,64},{16,80},{32,96},{48,112},{64,0},{80,16},{96,32},{112,48},{1... | collective-permute-start | bytes 6291464 | tf_op jit(solution)/shard_map/ppermute | solution.py:266
  197.9 4.6 %shard_map.149 = (bf16[2,2,512,256]{3,2,1,0:T(8,128)(2,1)}, bf16[2,2,512,256]{3,2,1,0:T(8,128)(2,1)}, bf16[2,2,512,256]{3,2,1,0:T(8,128)(2,1)}, bf16[2,2,512,256]{3,2,1,0:T(8,128)(2,1)}) custom-call(s32[8]{0:T(128)} %reshape.104.order_ref, bf16[16,32,2048]{2,1,0:T(8,128)(2,1)} %copy-done.1, bf16[2,256,512]{2,1,0:T(8,128)(2,1)} %get-tuple-element.43.hidden_ref.act_ref), custom_call_target="tpu_custom_call" | custom-call | tf_op jit(solution)/shard_map/pallas_call | solution.py:212
  202.5 25.4 %collective-permute-done.10 = bf16[2,2,256,512]{3,2,1,0:T(8,128)(2,1)S(1)} collective-permute-done((bf16[2,2,256,512]{3,2,1,0:T(8,128)(2,1)}, bf16[2,2,256,512]{3,2,1,0:T(8,128)(2,1)S(1)}, u32[]{:S(2)}, u32[]{:S(2)}) %collective-permute-start.10) | collective-permute-done | bytes 1048608 | tf_op jit(solution)/shard_map/ppermute | solution.py:259
  227.9 3.3 %collective-permute-done.8 = bf16[2,2,256,512]{3,2,1,0:T(8,128)(2,1)S(1)} collective-permute-done((bf16[2,2,256,512]{3,2,1,0:T(8,128)(2,1)}, bf16[2,2,256,512]{3,2,1,0:T(8,128)(2,1)S(1)}, u32[]{:S(2)}, u32[]{:S(2)}) %collective-permute-start.8) | collective-permute-done | bytes 1048608 | tf_op jit(solution)/shard_map/ppermute | solution.py:259
  231.2 1.8 collective-permute-start.17
  233.0 1.5 collective-permute-start.18
  234.5 2.5 convert_add_fusion.1
  237.0 0.1 fusion.4
  237.0 9.5 %collective-permute-start.11 = (bf16[2,256,512]{2,1,0:T(8,128)(2,1)S(1)}, bf16[2,256,512]{2,1,0:T(8,128)(2,1)}, u32[]{:S(2)}, u32[]{:S(2)}) collective-permute-start(bf16[2,256,512]{2,1,0:T(8,128)(2,1)S(1)} %fusion.4), channel_id=1, source_target_pairs={{0,64},{16,80},{32,96},{48,112},{64,0},{80,16},{96,32},{112,48},{1... | collective-permute-start | bytes 1572872 | tf_op jit(solution)/shard_map/ppermute | solution.py:266
  246.5 32.7 %collective-permute-done.16 = bf16[2,2,512,256]{3,2,1,0:T(8,128)(2,1)S(1)} collective-permute-done((bf16[2,2,512,256]{3,2,1,0:T(8,128)(2,1)}, bf16[2,2,512,256]{3,2,1,0:T(8,128)(2,1)S(1)}, u32[]{:S(2)}, u32[]{:S(2)}) %collective-permute-start.16) | collective-permute-done | bytes 1048608 | tf_op jit(solution)/shard_map/ppermute | solution.py:259
  279.2 0.6 collective-permute-done.18
  279.8 0.5 convert_add_fusion
  280.3 1.3 copy-done.3
  281.6 0.1 fusion.5
  281.7 7.7 %collective-permute-start.19 = (bf16[2,512,256]{2,1,0:T(8,128)(2,1)S(1)}, bf16[2,512,256]{2,1,0:T(8,128)(2,1)}, u32[]{:S(2)}, u32[]{:S(2)}) collective-permute-start(bf16[2,512,256]{2,1,0:T(8,128)(2,1)S(1)} %fusion.5), channel_id=1, source_target_pairs={{0,64},{16,80},{32,96},{48,112},{64,0},{80,16},{96,32},{112,48},{1... | collective-permute-start | bytes 1572872 | tf_op jit(solution)/shard_map/ppermute | solution.py:266
  289.4 3.8 %pair_sum.1 = (f32[2,256,512]{2,1,0:T(8,128)}, bf16[2,256,512]{2,1,0:T(8,128)(2,1)}, bf16[2,256,512]{2,1,0:T(8,128)(2,1)}, bf16[2,256,512]{2,1,0:T(8,128)(2,1)}) custom-call(bf16[4,2,256,512]{3,2,1,0:T(8,128)(2,1)} %get-tuple-element.56.keep_ref, bf16[4,2,256,512]{3,2,1,0:T(8,128)(2,1)} %collective-permute-done.12.got_ref), custom_call_target="tpu_custom_call" | custom-call | tf_op jit(solution)/shard_map/pair_sum/pallas_call | solution.py:401
  293.2 1.6 collective-permute-start.13
  294.8 2.5 collective-permute-start.14
  297.3 0.8 collective-permute-start.15
  298.1 2.0 fusion.3
  300.1 0.6 collective-permute-done.19
  300.7 2.0 fusion.1
  302.6 5.3 %collective-permute-done.13 = bf16[2,256,512]{2,1,0:T(8,128)(2,1)S(1)} collective-permute-done((bf16[2,256,512]{2,1,0:T(8,128)(2,1)}, bf16[2,256,512]{2,1,0:T(8,128)(2,1)S(1)}, u32[]{:S(2)}, u32[]{:S(2)}) %collective-permute-start.13) | collective-permute-done | bytes 524320 | tf_op jit(solution)/shard_map/ppermute | solution.py:259
  307.9 12.4 %collective-permute-done.14 = bf16[2,256,512]{2,1,0:T(8,128)(2,1)S(1)} collective-permute-done((bf16[2,256,512]{2,1,0:T(8,128)(2,1)}, bf16[2,256,512]{2,1,0:T(8,128)(2,1)S(1)}, u32[]{:S(2)}, u32[]{:S(2)}) %collective-permute-start.14) | collective-permute-done | bytes 524320 | tf_op jit(solution)/shard_map/ppermute | solution.py:259
  320.3 1.1 add_convert_fusion
  321.4 3.5 %ngrad.1 = bf16[128,2048]{1,0:T(8,128)(2,1)} custom-call(bf16[16,4,16,2048]{3,2,1,0:T(8,128)(2,1)} %all-to-all-done.3.back_ref, bf16[512,128]{1,0:T(8,128)(2,1)} %get-tuple-element.38.pick0_ref, bf16[512,128]{1,0:T(8,128)(2,1)} %get-tuple-element.39.pick1_ref), custom_call_target="tpu_custom_call" | custom-call | tf_op jit(solution)/shard_map/ngrad/pallas_call | solution.py:387
  324.9 3.8 %mixed.1 = bf16[128,2048]{1,0:T(8,128)(2,1)} custom-call(bf16[16,4,16,2048]{3,2,1,0:T(8,128)(2,1)} %all-to-all-done.3.back_ref, bf16[512,128]{1,0:T(8,128)(2,1)} %get-tuple-element.38.pick0_ref, bf16[512,128]{1,0:T(8,128)(2,1)} %get-tuple-element.39.pick1_ref, f32[128,2]{1,0:T(8,128)} %copy.18.gates_ref), custom_call_target="tpu_custom_call" | custom-call | tf_op jit(solution)/shard_map/mixed/pallas_call | solution.py:384
  (37 shorter events, 0.1 us)
Async XLA Ops:
  0.6 13.5 %copy-start.10 = (f32[128,2]{0,1:T(2,128)S(1)}, f32[128,2]{0,1:T(2,128)}, u32[]{:S(2)}) copy-start(f32[128,2]{0,1:T(2,128)} %param.15) | copy-start | bytes 3076
  2.0 26.1 %copy-start.2 = (bf16[2,2048,128]{2,1,0:T(8,128)(2,1)}, bf16[2,2048,128]{2,1,0:T(8,128)(2,1)S(1)}, u32[]{:S(2)}) copy-start(bf16[2,2048,128]{2,1,0:T(8,128)(2,1)S(1)} %pad_maximum_fusion.kv.refs_2_) | copy-start | bytes 3145732
  2.0 31.5 %collective-permute-start = (bf16[2,2048,128]{2,1,0:T(8,128)(2,1)S(1)}, bf16[2,2048,128]{2,1,0:T(8,128)(2,1)}, u32[]{:S(2)}, u32[]{:S(2)}) collective-permute-start(bf16[2,2048,128]{2,1,0:T(8,128)(2,1)S(1)} %pad_maximum_fusion.kv.refs_2_), channel_id=1, source_target_pairs={{0,32},{16,48},{32,0},{48,16},{64,96},{80,112},{1,33},{17,49},{33,... | collective-permute-start | bytes 3145736 | tf_op jit(solution)/shard_map/ppermute | solution.py:259
  7.2 34.1 %collective-permute-start.2 = (bf16[2,2048,128]{2,1,0:T(8,128)(2,1)S(1)}, bf16[2,2048,128]{2,1,0:T(8,128)(2,1)}, u32[]{:S(2)}, u32[]{:S(2)}) collective-permute-start(bf16[2,2048,128]{2,1,0:T(8,128)(2,1)S(1)} %pad_maximum_fusion.kv.refs_2_), channel_id=1, source_target_pairs={{0,64},{16,80},{32,96},{48,112},{1,65},{17,81},{33,97},{49,113},{2... | collective-permute-start | bytes 3145736 | tf_op jit(solution)/shard_map/ppermute | solution.py:284
  18.7 76.0 %all-to-all-start = ((bf16[16,32,2048]{2,1,0:T(8,128)(2,1)}), bf16[16,32,2048]{2,1,0:T(8,128)(2,1)S(1)}, u32[]{:S(2)}, u32[]{:S(2)}) async-start(bf16[16,32,2048]{2,1,0:T(8,128)(2,1)} %get-tuple-element.36), calls=%async_computation | async-start | bytes 4194304 | tf_op jit(solution)/shard_map/all_to_all | solution.py:270
  24.2 35.7 %collective-permute-start.4 = (bf16[2,2048,128]{2,1,0:T(8,128)(2,1)S(1)}, bf16[2,2048,128]{2,1,0:T(8,128)(2,1)}, u32[]{:S(2)}, u32[]{:S(2)}) collective-permute-start(bf16[2,2048,128]{2,1,0:T(8,128)(2,1)S(1)} %pad_maximum_fusion.kv.refs_2_), channel_id=1, source_target_pairs={{0,16},{16,32},{32,48},{48,0},{64,80},{80,96},{96,112},{1,17},{17,... | collective-permute-start | bytes 3145736 | tf_op jit(solution)/shard_map/ppermute | solution.py:259
  26.8 33.1 %collective-permute-start.6 = (bf16[2048,128]{1,0:T(8,128)(2,1)}, bf16[2048,128]{1,0:T(8,128)(2,1)}, u32[]{:S(2)}, u32[]{:S(2)}) collective-permute-start(bf16[2048,128]{1,0:T(8,128)(2,1)} %refs_1_.3), channel_id=1, source_target_pairs={{64,0},{80,16},{96,32},{112,48},{65,1},{81,17},{97,33},{113,49},{6... | collective-permute-start | bytes 1572872 | tf_op jit(solution)/shard_map/ppermute | solution.py:283
  28.1 54.4 %collective-permute-start.5 = (bf16[2,2048,128]{2,1,0:T(8,128)(2,1)S(1)}, bf16[2,2048,128]{2,1,0:T(8,128)(2,1)}, u32[]{:S(2)}, u32[]{:S(2)}) collective-permute-start(bf16[2,2048,128]{2,1,0:T(8,128)(2,1)S(1)} %pad_maximum_fusion.kv.refs_2_), channel_id=1, source_target_pairs={{0,48},{64,112},{1,49},{65,113},{2,50},{66,114},{3,51},{67,115},{4... | collective-permute-start | bytes 3145736 | tf_op jit(solution)/shard_map/ppermute | solution.py:259
  33.5 58.0 %collective-permute-start.1 = (bf16[2,2048,128]{2,1,0:T(8,128)(2,1)}, bf16[2,2048,128]{2,1,0:T(8,128)(2,1)}, u32[]{:S(2)}, u32[]{:S(2)}) collective-permute-start(bf16[2,2048,128]{2,1,0:T(8,128)(2,1)} %collective-permute-done.refs_3_), channel_id=1, source_target_pairs={{0,64},{16,80},{32,96},{48,112},{1,65},{17,81},{33,97},{49,113},{2... | collective-permute-start | bytes 3145736 | tf_op jit(solution)/shard_map/ppermute | solution.py:289
  41.4 50.2 %collective-permute-start.3 = (bf16[2,2048,128]{2,1,0:T(8,128)(2,1)}, bf16[2,2048,128]{2,1,0:T(8,128)(2,1)}, u32[]{:S(2)}, u32[]{:S(2)}) collective-permute-start(bf16[2,2048,128]{2,1,0:T(8,128)(2,1)} %collective-permute-done.2), channel_id=1, source_target_pairs={{64,112},{80,64},{96,80},{112,96},{65,113},{81,65},{97,81},{113,97... | collective-permute-start | bytes 3145736 | tf_op jit(solution)/shard_map/ppermute | solution.py:259
  73.7 17.9 %collective-permute-start.7 = (bf16[2048,128]{1,0:T(8,128)(2,1)}, bf16[2048,128]{1,0:T(8,128)(2,1)}, u32[]{:S(2)}, u32[]{:S(2)}) collective-permute-start(bf16[2048,128]{1,0:T(8,128)(2,1)} %shard_map.146), channel_id=1, source_target_pairs={{0,64},{16,80},{32,96},{48,112},{1,65},{17,81},{33,97},{49,113},{2... | collective-permute-start | bytes 1572872 | tf_op jit(solution)/shard_map/ppermute | solution.py:308
  94.7 20.0 %copy-start.1 = (bf16[16,32,2048]{2,1,0:T(8,128)(2,1)}, bf16[16,32,2048]{2,1,0:T(8,128)(2,1)S(1)}, u32[]{:S(2)}) copy-start(bf16[16,32,2048]{2,1,0:T(8,128)(2,1)S(1)} %all-to-all-done.grad_ref.src) | copy-start | bytes 6291460
  114.7 31.5 %all-to-all-start.2 = ((bf16[16,32,2048]{2,1,0:T(8,128)(2,1)}), bf16[16,32,2048]{2,1,0:T(8,128)(2,1)S(1)}, u32[]{:S(2)}, u32[]{:S(2)}) async-start(bf16[16,32,2048]{2,1,0:T(8,128)(2,1)} %get-tuple-element.41), calls=%async_computation.2 | async-start | bytes 4194304 | tf_op jit(solution)/shard_map/all_to_all | solution.py:270
  146.2 1.3 copy-start
  164.1 157.3 %all-to-all-start.3 = ((bf16[16,4,16,2048]{3,2,1,0:T(8,128)(2,1)}), bf16[16,4,16,2048]{3,2,1,0:T(8,128)(2,1)}, u32[]{:S(2)}, u32[]{:S(2)}) async-start(bf16[16,4,16,2048]{3,2,1,0:T(8,128)(2,1)} %expert_back.1), calls=%async_computation.3 | async-start | bytes 8388608 | tf_op jit(solution)/shard_map/all_to_all | solution.py:270
  173.9 53.9 %collective-permute-start.10 = (bf16[2,2,256,512]{3,2,1,0:T(8,128)(2,1)}, bf16[2,2,256,512]{3,2,1,0:T(8,128)(2,1)S(1)}, u32[]{:S(2)}, u32[]{:S(2)}) collective-permute-start(bf16[2,2,256,512]{3,2,1,0:T(8,128)(2,1)} %get-tuple-element.52), channel_id=1, source_target_pairs={{0,48},{16,0},{32,16},{48,32},{64,112},{80,64},{96,80},{112,96},{1... | collective-permute-start | bytes 3145736 | tf_op jit(solution)/shard_map/ppermute | solution.py:259
  182.3 48.9 %collective-permute-start.8 = (bf16[2,2,256,512]{3,2,1,0:T(8,128)(2,1)}, bf16[2,2,256,512]{3,2,1,0:T(8,128)(2,1)S(1)}, u32[]{:S(2)}, u32[]{:S(2)}) collective-permute-start(bf16[2,2,256,512]{3,2,1,0:T(8,128)(2,1)} %get-tuple-element.50), channel_id=1, source_target_pairs={{0,16},{16,32},{32,48},{48,0},{64,80},{80,96},{96,112},{112,64},{1... | collective-permute-start | bytes 3145736 | tf_op jit(solution)/shard_map/ppermute | solution.py:259
  182.3 48.9 %collective-permute-start.9 = (bf16[2,2,256,512]{3,2,1,0:T(8,128)(2,1)}, bf16[2,2,256,512]{3,2,1,0:T(8,128)(2,1)}, u32[]{:S(2)}, u32[]{:S(2)}) collective-permute-start(bf16[2,2,256,512]{3,2,1,0:T(8,128)(2,1)} %get-tuple-element.51), channel_id=1, source_target_pairs={{0,32},{16,48},{32,0},{48,16},{64,96},{80,112},{96,64},{112,80},{1... | collective-permute-start | bytes 3145736 | tf_op jit(solution)/shard_map/ppermute | solution.py:259
  184.3 50.2 %copy-start.6 = (bf16[2,2,256,512]{3,2,1,0:T(8,128)(2,1)S(1)}, bf16[2,2,256,512]{3,2,1,0:T(8,128)(2,1)}, u32[]{:S(2)}) copy-start(bf16[2,2,256,512]{3,2,1,0:T(8,128)(2,1)} %get-tuple-element.46) | copy-start | bytes 3145732
  189.2 100.2 %collective-permute-start.12 = (bf16[4,2,256,512]{3,2,1,0:T(8,128)(2,1)}, bf16[4,2,256,512]{3,2,1,0:T(8,128)(2,1)}, u32[]{:S(2)}, u32[]{:S(2)}) collective-permute-start(bf16[4,2,256,512]{3,2,1,0:T(8,128)(2,1)} %get-tuple-element.57), channel_id=1, source_target_pairs={{0,64},{16,80},{32,96},{48,112},{64,0},{80,16},{96,32},{112,48},{1... | collective-permute-start | bytes 6291464 | tf_op jit(solution)/shard_map/ppermute | solution.py:266
  227.9 6.6 %copy-start.7 = (bf16[2,2,256,512]{3,2,1,0:T(8,128)(2,1)}, bf16[2,2,256,512]{3,2,1,0:T(8,128)(2,1)S(1)}, u32[]{:S(2)}) copy-start(bf16[2,2,256,512]{3,2,1,0:T(8,128)(2,1)S(1)} %collective-permute-done.10) | copy-start | bytes 3145732
  231.2 3.3 %copy-start.8 = (bf16[2,2,256,512]{3,2,1,0:T(8,128)(2,1)}, bf16[2,2,256,512]{3,2,1,0:T(8,128)(2,1)S(1)}, u32[]{:S(2)}) copy-start(bf16[2,2,256,512]{3,2,1,0:T(8,128)(2,1)S(1)} %collective-permute-done.8) | copy-start | bytes 3145732
  231.2 48.0 %collective-permute-start.16 = (bf16[2,2,512,256]{3,2,1,0:T(8,128)(2,1)}, bf16[2,2,512,256]{3,2,1,0:T(8,128)(2,1)S(1)}, u32[]{:S(2)}, u32[]{:S(2)}) collective-permute-start(bf16[2,2,512,256]{3,2,1,0:T(8,128)(2,1)} %get-tuple-element.63), channel_id=1, source_target_pairs={{0,16},{16,32},{32,48},{48,0},{64,80},{80,96},{96,112},{112,64},{1... | collective-permute-start | bytes 3145736 | tf_op jit(solution)/shard_map/ppermute | solution.py:259
  231.2 48.0 %collective-permute-start.17 = (bf16[2,2,512,256]{3,2,1,0:T(8,128)(2,1)}, bf16[2,2,512,256]{3,2,1,0:T(8,128)(2,1)S(1)}, u32[]{:S(2)}, u32[]{:S(2)}) collective-permute-start(bf16[2,2,512,256]{3,2,1,0:T(8,128)(2,1)} %get-tuple-element.64), channel_id=1, source_target_pairs={{0,32},{16,48},{32,0},{48,16},{64,96},{80,112},{96,64},{112,80},{1... | collective-permute-start | bytes 3145736 | tf_op jit(solution)/shard_map/ppermute | solution.py:259
  233.0 46.8 %collective-permute-start.18 = (bf16[2,2,512,256]{3,2,1,0:T(8,128)(2,1)}, bf16[2,2,512,256]{3,2,1,0:T(8,128)(2,1)S(1)}, u32[]{:S(2)}, u32[]{:S(2)}) collective-permute-start(bf16[2,2,512,256]{3,2,1,0:T(8,128)(2,1)} %get-tuple-element.65), channel_id=1, source_target_pairs={{0,48},{16,0},{32,16},{48,32},{64,112},{80,64},{96,80},{112,96},{1... | collective-permute-start | bytes 3145736 | tf_op jit(solution)/shard_map/ppermute | solution.py:259
  234.5 45.4 %copy-start.9 = (bf16[2,2,512,256]{3,2,1,0:T(8,128)(2,1)S(1)}, bf16[2,2,512,256]{3,2,1,0:T(8,128)(2,1)}, u32[]{:S(2)}) copy-start(bf16[2,2,512,256]{3,2,1,0:T(8,128)(2,1)} %get-tuple-element.62) | copy-start | bytes 3145732
  237.0 61.0 %collective-permute-start.11 = (bf16[2,256,512]{2,1,0:T(8,128)(2,1)S(1)}, bf16[2,256,512]{2,1,0:T(8,128)(2,1)}, u32[]{:S(2)}, u32[]{:S(2)}) collective-permute-start(bf16[2,256,512]{2,1,0:T(8,128)(2,1)S(1)} %fusion.4), channel_id=1, source_target_pairs={{0,64},{16,80},{32,96},{48,112},{64,0},{80,16},{96,32},{112,48},{1... | collective-permute-start | bytes 1572872 | tf_op jit(solution)/shard_map/ppermute | solution.py:266
  280.3 1.3 copy-start.3
  281.7 19.0 %collective-permute-start.19 = (bf16[2,512,256]{2,1,0:T(8,128)(2,1)S(1)}, bf16[2,512,256]{2,1,0:T(8,128)(2,1)}, u32[]{:S(2)}, u32[]{:S(2)}) collective-permute-start(bf16[2,512,256]{2,1,0:T(8,128)(2,1)S(1)} %fusion.5), channel_id=1, source_target_pairs={{0,64},{16,80},{32,96},{48,112},{64,0},{80,16},{96,32},{112,48},{1... | collective-permute-start | bytes 1572872 | tf_op jit(solution)/shard_map/ppermute | solution.py:266
  293.2 7.4 %copy-start.4 = (f32[2,2,512,256]{3,2,1,0:T(8,128)S(1)}, f32[2,2,512,256]{3,2,1,0:T(8,128)}, u32[]{:S(2)}) copy-start(f32[2,2,512,256]{3,2,1,0:T(8,128)} %copy-done.3) | copy-start | bytes 6291460
  293.2 14.7 %collective-permute-start.13 = (bf16[2,256,512]{2,1,0:T(8,128)(2,1)}, bf16[2,256,512]{2,1,0:T(8,128)(2,1)S(1)}, u32[]{:S(2)}, u32[]{:S(2)}) collective-permute-start(bf16[2,256,512]{2,1,0:T(8,128)(2,1)} %get-tuple-element.59), channel_id=1, source_target_pairs={{0,16},{16,32},{32,48},{48,0},{64,80},{80,96},{96,112},{112,64},{1... | collective-permute-start | bytes 1572872 | tf_op jit(solution)/shard_map/ppermute | solution.py:259
  294.8 25.5 %collective-permute-start.14 = (bf16[2,256,512]{2,1,0:T(8,128)(2,1)}, bf16[2,256,512]{2,1,0:T(8,128)(2,1)S(1)}, u32[]{:S(2)}, u32[]{:S(2)}) collective-permute-start(bf16[2,256,512]{2,1,0:T(8,128)(2,1)} %get-tuple-element.60), channel_id=1, source_target_pairs={{0,32},{16,48},{32,0},{48,16},{64,96},{80,112},{96,64},{112,80},{1... | collective-permute-start | bytes 1572872 | tf_op jit(solution)/shard_map/ppermute | solution.py:259
  297.3 23.0 %copy-start.5 = (f32[2,256,512]{2,1,0:T(8,128)S(1)}, f32[2,256,512]{2,1,0:T(8,128)}, u32[]{:S(2)}) copy-start(f32[2,256,512]{2,1,0:T(8,128)} %get-tuple-element.58) | copy-start | bytes 3145732
  297.3 23.0 %collective-permute-start.15 = (bf16[2,256,512]{2,1,0:T(8,128)(2,1)}, bf16[2,256,512]{2,1,0:T(8,128)(2,1)S(1)}, u32[]{:S(2)}, u32[]{:S(2)}) collective-permute-start(bf16[2,256,512]{2,1,0:T(8,128)(2,1)} %get-tuple-element.61), channel_id=1, source_target_pairs={{0,48},{16,0},{32,16},{48,32},{64,112},{80,64},{96,80},{112,96},{1... | collective-permute-start | bytes 1572872 | tf_op jit(solution)/shard_map/ppermute | solution.py:259
where the time goes:
time: 330 us; the launch traced here: 329 us
  waiting for transfers between devices  125 us (38%)
  starting transfers between devices  90.6 us (27%)
  Pallas kernels  79.9 us (24%)
  blocking collectives  16.3 us (5%)
  other arithmetic  11.8 us (4%)
  local copies, waits for them, and re-layouts  4.04 us (1%)
    ppermute x13, waiting for transfers between devices, move_y(): return lax.ppermute(value, 'ctx', pairs)  79.7 us
    ppermute x13, starting transfers between devices, move_y(): return lax.ppermute(value, 'ctx', pairs)  32.8 us
    ppermute x3, starting transfers between devices, move_x(): return lax.ppermute(value, 'ctx', pairs)  26 us
    all_to_all x3, waiting for transfers between devices, exchange(): return lax.all_to_all(value, 'exp', split_axis=0, concat_axis=0, tiled=True)  23.3 us
    pallas_call x3, Pallas kernels, attend(): pl.pallas_call(kernel, out_shape=jax.ShapeDtypeStruct((rows, HEAD_DIM), o...  20.5 us
    all_to_all x1, blocking collectives, exchange(): return lax.all_to_all(value, 'exp', split_axis=0, concat_axis=0, tiled=True)  16.3 us
    ppermute x1, waiting for transfers between devices, step(): lent_q = lax.ppermute(queries, 'ctx', up_x)  16.2 us
    pallas_call x3, Pallas kernels, weight_grad(): pl.pallas_call(kernel, out_shape=tuple((jax.ShapeDtypeStruct((c, 2, *piec...  14 us
  transfers between devices with their start and end apart: 23, of which 10 were waited for; matrix products, arithmetic and copies ran while one was open for 4% of the time, Pallas kernels for 16%

commit v1 on v0

--- a/solution.py
+++ b/solution.py
@@ -86,18 +86,16 @@
     )(q, kv)
 
 
-def attend(flags, q, kvs, base, extra, out_type):
+def attend(flags, q, kvs, base, out_type):
     rows = q.shape[0]
     count = len(kvs)
-    given = [v for v in (base, extra) if v is not None]
 
     def kernel(*refs):
         flags_ref, q_ref = refs[0], refs[1]
         kv_refs = refs[2 : 2 + count]
-        base_ref = refs[2 + count] if base is not None else None
-        extra_ref = refs[1 + count + len(given)] if extra is not None else None
+        base_ref = refs[2 + count]
         out, acc, turned, value = refs[-4:]
-        acc[...] = jnp.zeros_like(acc) if base is None else base_ref[...]
+        acc[...] = base_ref[...]
 
         def one(n, carry):
             @pl.when(flags_ref[n] != 0)
@@ -114,22 +112,19 @@
             return carry
 
         lax.fori_loop(0, count, one, 0)
-        total = acc[...]
-        if extra is not None:
-            total = total + extra_ref[...].astype(F32)
-        out[...] = total.astype(out_type)
+        out[...] = acc[...].astype(out_type)
 
     return pl.pallas_call(
         kernel,
         out_shape=jax.ShapeDtypeStruct((rows, HEAD_DIM), out_type),
-        in_specs=[smem()] + [vmem()] * (1 + count + len(given)),
+        in_specs=[smem()] + [vmem()] * (2 + count),
         out_specs=vmem(),
         scratch_shapes=[
             pltpu.VMEM((rows, HEAD_DIM), F32),
             pltpu.VMEM((HEAD_DIM, rows), BF16),
             pltpu.VMEM((rows, HEAD_DIM), BF16),
         ],
-    )(flags, q, *kvs, *given)
+    )(flags, q, *kvs, base)
 
 
 def route_kernel(ids_ref, gates_ref, grad_ref, pick0_ref, pick1_ref, send_ref):
@@ -277,15 +272,15 @@
     hi, y = ctx // 4, ctx % 4
     full = jax.ShapeDtypeStruct
     down_x = [(n, 4 + n) for n in range(4)]
-    up_x = [(4 + n, n) for n in range(4)]
+    in_high = lambda hi, y: hi == 1
 
     kv = jnp.stack([keys, values])
-    lent_q = lax.ppermute(queries, "ctx", up_x)
+    from_y1 = move_y(kv, 1, lambda hi, y: y < 3)
     from_x = lax.ppermute(kv, "ctx", down_x)
-    from_y1 = move_y(kv, 1, lambda hi, y: hi == 0 or y < 3)
     from_y2 = move_y(kv, 2, lambda hi, y: hi == 0 or y < 2)
     from_y3 = move_y(kv, 3, lambda hi, y: y == 0)
-    from_xy = move_y(from_x, 3, lambda hi, y: hi == 1)
+    from_xy1 = move_y(from_x, 1, in_high)
+    from_xy3 = move_y(from_x, 3, in_high)
     from_xx = lax.ppermute(from_y2, "ctx", down_x)
 
     pick0, pick1, send_grads = pl.pallas_call(
@@ -302,12 +297,17 @@
     recv_grads = exchange(send_grads)
 
     flag = lambda *conds: jnp.stack([c.astype(jnp.int32) for c in conds])
-    low, high = hi == 0, hi == 1
+    high = hi == 1
     acc = attend_own(queries, kv)
-    lent = attend(flag(low, low), lent_q, [kv, from_y1], None, None, BF16)
-    returned = lax.ppermute(lent, "ctx", down_x)
-    acc = attend(flag(y >= 1, y >= 2, y >= 3), queries, [from_y1, from_y2, from_y3], acc, None, F32)
-    attended = attend(flag(high, high), queries, [from_xx, from_xy], acc, returned, BF16)
+    stages = (
+        (flag(y >= 1, high), [from_y1, from_x], F32),
+        (flag(y >= 2, y >= 3), [from_y2, from_y3], F32),
+        (flag(high, high), [from_xy1, from_xy3], F32),
+        (flag(high), [from_xx], BF16),
+    )
+    for flags, blocks, kind in stages:
+        acc = attend(flags, queries, blocks, acc, kind)
+    attended = acc
 
     expert_block = pl.BlockSpec((N_EXP, CAP, width), lambda e: (0, e, 0))
     in_weight = pl.BlockSpec((1, width, hid), lambda e: (e, 0, 0))
@@ -348,12 +348,12 @@
     y_order = jnp.stack(
         [hi * 4 + (y + far) % 4, (1 - hi) * 4 + (y + far) % 4], axis=1
     ).reshape(8)
-    up_send, up_keep = weight_grad(x_order, recv_inputs, up_grad, (4, 4), False)
-    up_got = move_x(up_send)
     ga = weight_grad(y_order, recv_inputs, gate_grad, (2, 2, 2, 2), False)
     got_g = []
     for n in range(3):
         got_g.append(move_y(ga[n], n + 1))
+    up_send, up_keep = weight_grad(x_order, recv_inputs, up_grad, (4, 4), False)
+    up_got = move_x(up_send)
     do = weight_grad(y_order, recv_grads, hidden, (2, 2, 2, 2), True)
     held = lax.optimization_barrier((*do[:3], *got_g))
     got_g = held[3:]

time: 330 us -> 324 us (0.982)
  starting transfers between devices: 90.6 us -> 121 us
  waiting for transfers between devices: 125 us -> 97.6 us
  Pallas kernels: 79.9 us -> 71.9 us
    ppermute x3, starting transfers between devices: 26 us -> 58.3 us  [move_x(): return lax.ppermute(value, 'ctx', pairs)]
    ppermute x2 -> x0, waiting for transfers between devices: 21.8 us -> none  [the longest x1 16.2 us: step(): lent_q = lax.ppermute(queries, 'ctx', up_x)]
    ppermute x13 -> x14, waiting for transfers between devices: 79.7 us -> 65.3 us  [move_y(): return lax.ppermute(value, 'ctx', pairs)]
    pallas_call x3 -> x4, Pallas kernels: 20.5 us -> 12.4 us  [attend(): pl.pallas_call(kernel, out_shape=jax.ShapeDtypeStruct((rows, HEAD_DIM), o...]
    ppermute x1, waiting for transfers between devices: 0.01 us -> 7.3 us  [step(): from_xx = lax.ppermute(from_y2, 'ctx', down_x)]
    ppermute x2 -> x0, starting transfers between devices: 3.37 us -> none  [the longest x1 2.07 us: step(): returned = lax.ppermute(lent, 'ctx', down_x)]
    ppermute x13 -> x14, starting transfers between devices: 32.8 us -> 35.7 us  [move_y(): return lax.ppermute(value, 'ctx', pairs)]
  transfers between devices with their start and end apart: 23 -> 22, of which waited for: 10 -> 10; matrix products, arithmetic and copies ran while one was open for 4% -> 4% of each run, Pallas kernels for 16% -> 14%
where the time goes in v1:
time: 324 us; the launch traced here: 323 us
  starting transfers between devices  121 us (37%)
  waiting for transfers between devices  97.6 us (30%)
  Pallas kernels  71.9 us (22%)
  blocking collectives  16.3 us (5%)
  other arithmetic  11.8 us (4%)
  local copies, waits for them, and re-layouts  4.06 us (1%)
    ppermute x14, waiting for transfers between devices, move_y(): return lax.ppermute(value, 'ctx', pairs)  65.3 us
    ppermute x3, starting transfers between devices, move_x(): return lax.ppermute(value, 'ctx', pairs)  58.3 us
    ppermute x14, starting transfers between devices, move_y(): return lax.ppermute(value, 'ctx', pairs)  35.7 us
    all_to_all x3, waiting for transfers between devices, exchange(): return lax.all_to_all(value, 'exp', split_axis=0, concat_axis=0, tiled=True)  23.3 us
    all_to_all x1, blocking collectives, exchange(): return lax.all_to_all(value, 'exp', split_axis=0, concat_axis=0, tiled=True)  16.3 us
    pallas_call x3, Pallas kernels, weight_grad(): pl.pallas_call(kernel, out_shape=tuple((jax.ShapeDtypeStruct((c, 2, *piec...  14.1 us
    all_to_all x3, starting transfers between devices, exchange(): return lax.all_to_all(value, 'exp', split_axis=0, concat_axis=0, tiled=True)  13.7 us
    pallas_call x4, Pallas kernels, attend(): pl.pallas_call(kernel, out_shape=jax.ShapeDtypeStruct((rows, HEAD_DIM), o...  12.4 us
  transfers between devices with their start and end apart: 22, of which 10 were waited for; matrix products, arithmetic and copies ran while one was open for 4% of the time, Pallas kernels for 14%

profile of v1, /device:TPU:0, one launch (start us, length us, event | category | flops | bytes accessed | tf_op | source)
XLA Modules:
  0.0 323.1 jit_solution(5852672467879792997)
XLA Ops:
  0.6 1.3 pad_maximum_fusion.kv
  2.0 6.0 %collective-permute-start.2 = (bf16[2,2048,128]{2,1,0:T(8,128)(2,1)S(1)}, bf16[2,2048,128]{2,1,0:T(8,128)(2,1)}, u32[]{:S(2)}, u32[]{:S(2)}) collective-permute-start(bf16[2,2048,128]{2,1,0:T(8,128)(2,1)S(1)} %pad_maximum_fusion.kv), channel_id=1, source_target_pairs={{0,64},{16,80},{32,96},{48,112},{1,65},{17,81},{33,97},{49,113},{2... | collective-permute-start | bytes 3145736 | tf_op jit(solution)/shard_map/ppermute | solution.py:279
  8.0 5.1 %collective-permute-start = (bf16[2,2048,128]{2,1,0:T(8,128)(2,1)S(1)}, bf16[2,2048,128]{2,1,0:T(8,128)(2,1)}, u32[]{:S(2)}, u32[]{:S(2)}) collective-permute-start(bf16[2,2048,128]{2,1,0:T(8,128)(2,1)S(1)} %pad_maximum_fusion.kv), channel_id=1, source_target_pairs={{0,32},{16,48},{32,0},{48,16},{64,96},{80,112},{1,33},{17,49},{33,... | collective-permute-start | bytes 3145736 | tf_op jit(solution)/shard_map/ppermute | solution.py:254
  13.1 0.7 copy.18.gates_ref
  13.9 3.9 %route.1 = (bf16[512,128]{1,0:T(8,128)(2,1)}, bf16[512,128]{1,0:T(8,128)(2,1)}, bf16[16,32,2048]{2,1,0:T(8,128)(2,1)}) custom-call(s32[2,128]{1,0:T(2,128)} %bitcast.27, f32[128,2]{1,0:T(8,128)} %copy.18.gates_ref, bf16[128,2048]{1,0:T(8,128)(2,1)} %grad_ref.1), custom_call_target="tpu_custom_call" | custom-call | tf_op jit(solution)/shard_map/route/pallas_call | solution.py:286
  17.8 5.4 %all-to-all-start = ((bf16[16,32,2048]{2,1,0:T(8,128)(2,1)}), bf16[16,32,2048]{2,1,0:T(8,128)(2,1)S(1)}, u32[]{:S(2)}, u32[]{:S(2)}) async-start(bf16[16,32,2048]{2,1,0:T(8,128)(2,1)} %get-tuple-element.36), calls=%async_computation | async-start | bytes 4194304 | tf_op jit(solution)/shard_map/all_to_all | solution.py:265
  23.2 3.6 %collective-permute-start.6 = (bf16[2,2048,128]{2,1,0:T(8,128)(2,1)S(1)}, bf16[2,2048,128]{2,1,0:T(8,128)(2,1)}, u32[]{:S(2)}, u32[]{:S(2)}) collective-permute-start(bf16[2,2048,128]{2,1,0:T(8,128)(2,1)S(1)} %pad_maximum_fusion.kv), channel_id=1, source_target_pairs={{0,16},{16,32},{32,48},{64,80},{80,96},{96,112},{1,17},{17,33},{33... | collective-permute-start | bytes 3145736 | tf_op jit(solution)/shard_map/ppermute | solution.py:254
  26.8 2.3 collective-permute-start.5
  29.1 1.5 collective-permute-done.2.refs_3_
  30.6 1.7 collective-permute-start.3
  32.2 1.6 collective-permute-start.4
  33.9 3.7 %collective-permute-done.refs_2_ = bf16[2,2048,128]{2,1,0:T(8,128)(2,1)} collective-permute-done((bf16[2,2048,128]{2,1,0:T(8,128)(2,1)S(1)}, bf16[2,2048,128]{2,1,0:T(8,128)(2,1)}, u32[]{:S(2)}, u32[]{:S(2)}) %collective-permute-start) | collective-permute-done | bytes 1048608 | tf_op jit(solution)/shard_map/ppermute | solution.py:254
  37.5 7.1 %collective-permute-start.1 = (bf16[2,2048,128]{2,1,0:T(8,128)(2,1)}, bf16[2,2048,128]{2,1,0:T(8,128)(2,1)}, u32[]{:S(2)}, u32[]{:S(2)}) collective-permute-start(bf16[2,2048,128]{2,1,0:T(8,128)(2,1)} %collective-permute-done.refs_2_), channel_id=1, source_target_pairs={{0,64},{16,80},{32,96},{48,112},{1,65},{17,81},{33,97},{49,113},{2... | collective-permute-start | bytes 3145736 | tf_op jit(solution)/shard_map/ppermute | solution.py:284
  44.7 5.6 %attend_own.1.refs_4_ = f32[2048,128]{1,0:T(8,128)} custom-call(bf16[2048,128]{1,0:T(8,128)(2,1)} %refs_1_.7, bf16[2,2048,128]{2,1,0:T(8,128)(2,1)} %copy-done.4), custom_call_target="tpu_custom_call" | custom-call | tf_op jit(solution)/shard_map/attend_own/pallas_call | solution.py:79
  50.3 0.6 pad_add_fusion.1.refs_0_
  50.9 0.6 pad_add_fusion.2.refs_0_
  51.5 0.6 add_convert_fusion.1.refs_0_
  52.1 5.7 %collective-permute-done.6.refs_2_ = bf16[2,2048,128]{2,1,0:T(8,128)(2,1)} collective-permute-done((bf16[2,2048,128]{2,1,0:T(8,128)(2,1)S(1)}, bf16[2,2048,128]{2,1,0:T(8,128)(2,1)}, u32[]{:S(2)}, u32[]{:S(2)}) %collective-permute-start.6) | collective-permute-done | bytes 1048608 | tf_op jit(solution)/shard_map/ppermute | solution.py:254
  57.8 3.2 shard_map.145.refs_4_
  60.9 3.2 %shard_map.146.refs_4_ = f32[2048,128]{1,0:T(8,128)} custom-call(s32[2]{0:T(128)} %add_convert_fusion.1.refs_0_, bf16[2048,128]{1,0:T(8,128)(2,1)} %refs_1_.7, bf16[2,2048,128]{2,1,0:T(8,128)(2,1)} %collective-permute-done.refs_2_, bf16[2,2048,128]{2,1,0:T(8,128)(2,1)} %collective-permute-done.5.refs_3_, f32[2048,128]{1,0:T(8,128)} %shard_map.145.refs_4_), custom_call_target="tpu_custom_call" | custom-call | tf_op jit(solution)/shard_map/pallas_call | solution.py:117
  64.2 0.0 collective-permute-done.3.refs_2_
  64.2 3.2 shard_map.147.refs_3_
  67.3 7.3 %collective-permute-done.1.refs_2_ = bf16[2,2048,128]{2,1,0:T(8,128)(2,1)} collective-permute-done((bf16[2,2048,128]{2,1,0:T(8,128)(2,1)}, bf16[2,2048,128]{2,1,0:T(8,128)(2,1)}, u32[]{:S(2)}, u32[]{:S(2)}) %collective-permute-start.1) | collective-permute-done | bytes 1048608 | tf_op jit(solution)/shard_map/ppermute | solution.py:284
  74.6 2.8 shard_map.148
  77.4 16.3 %all_to_all.20.tok_ref = bf16[16,128,128]{2,1,0:T(8,128)(2,1)} all-to-all(bf16[16,128,128]{2,1,0:T(8,128)(2,1)} %bitcast.24), channel_id=1, replica_groups=mesh['ctx'=8,'exp'=16] {'exp'}, dimensions={0} | all-to-all | bytes 1048576 | tf_op jit(solution)/shard_map/all_to_all | solution.py:265
  93.7 3.7 %norm.1 = (bf16[128,2048]{1,0:T(8,128)(2,1)}, bf16[16,32,2048]{2,1,0:T(8,128)(2,1)}) custom-call(bf16[16,128,128]{2,1,0:T(8,128)(2,1)} %all_to_all.20.tok_ref, bf16[128,2048]{1,0:T(8,128)(2,1)} %gate_ref.3, bf16[512,128]{1,0:T(8,128)(2,1)} %get-tuple-element.38.pick0_ref, bf16[512,128]{1,0:T(8,128)(2,1)} %get-tuple-element.39.pick1_ref), custom_call_target="tpu_custom_call" | custom-call | tf_op jit(solution)/shard_map/norm/pallas_call | solution.py:326
  97.4 3.7 %all-to-all-start.2 = ((bf16[16,32,2048]{2,1,0:T(8,128)(2,1)}), bf16[16,32,2048]{2,1,0:T(8,128)(2,1)S(1)}, u32[]{:S(2)}, u32[]{:S(2)}) async-start(bf16[16,32,2048]{2,1,0:T(8,128)(2,1)} %get-tuple-element.41), calls=%async_computation.2 | async-start | bytes 4194304 | tf_op jit(solution)/shard_map/all_to_all | solution.py:265
  101.2 4.5 %hidden_grad.1.hg_ref = f32[2,256,512]{2,1,0:T(8,128)} custom-call(bf16[16,32,2048]{2,1,0:T(8,128)(2,1)} %copy-done.1, bf16[2,512,2048]{2,1,0:T(8,128)(2,1)} %down_ref.3), custom_call_target="tpu_custom_call" | custom-call | tf_op jit(solution)/shard_map/hidden_grad/pallas_call | solution.py:318
  105.6 23.3 %all-to-all-done.2.in_ref.src = bf16[16,32,2048]{2,1,0:T(8,128)(2,1)S(1)} async-done(((bf16[16,32,2048]{2,1,0:T(8,128)(2,1)}), bf16[16,32,2048]{2,1,0:T(8,128)(2,1)S(1)}, u32[]{:S(2)}, u32[]{:S(2)}) %all-to-all-start.2) | async-done | bytes 2097184 | tf_op jit(solution)/shard_map/all_to_all | solution.py:265
  128.9 1.3 copy-done
  130.2 6.6 %expert_in.1 = (bf16[2,256,512]{2,1,0:T(8,128)(2,1)}, bf16[2,256,512]{2,1,0:T(8,128)(2,1)}, bf16[2,256,512]{2,1,0:T(8,128)(2,1)}) custom-call(bf16[16,32,2048]{2,1,0:T(8,128)(2,1)} %copy-done, f32[2,256,512]{2,1,0:T(8,128)} %hidden_grad.1.hg_ref, bf16[2,2048,512]{2,1,0:T(8,128)(2,1)} %gate_ref.5, bf16[2,2048,512]{2,1,0:T(8,128)(2,1)} %up_ref.3), custom_call_target="tpu_custom_call" | custom-call | tf_op jit(solution)/shard_map/expert_in/pallas_call | solution.py:336
  136.8 10.0 %expert_back.1 = bf16[16,4,16,2048]{3,2,1,0:T(8,128)(2,1)} custom-call(bf16[2,256,512]{2,1,0:T(8,128)(2,1)} %get-tuple-element.43.hidden_ref.act_ref, bf16[2,512,2048]{2,1,0:T(8,128)(2,1)} %down_ref.3, bf16[2,256,512]{2,1,0:T(8,128)(2,1)} %get-tuple-element.44.gg_ref.act_ref, bf16[2,256,512]{2,1,0:T(8,128)(2,1)} %get-tuple-element.45.ug_ref.act_ref, ...), custom_call_target="tpu_custom_call" | custom-call | tf_op jit(solution)/shard_map/expert_back/pallas_call | solution.py:366
  146.8 4.5 %all-to-all-start.3 = ((bf16[16,4,16,2048]{3,2,1,0:T(8,128)(2,1)}), bf16[16,4,16,2048]{3,2,1,0:T(8,128)(2,1)}, u32[]{:S(2)}, u32[]{:S(2)}) async-start(bf16[16,4,16,2048]{3,2,1,0:T(8,128)(2,1)} %expert_back.1), calls=%async_computation.3 | async-start | bytes 8388608 | tf_op jit(solution)/shard_map/all_to_all | solution.py:265
  151.4 0.1 pad_add_fusion
  151.4 0.6 reshape.104.order_ref
  152.0 4.7 %shard_map.149 = (bf16[2,2,256,512]{3,2,1,0:T(8,128)(2,1)}, bf16[2,2,256,512]{3,2,1,0:T(8,128)(2,1)}, bf16[2,2,256,512]{3,2,1,0:T(8,128)(2,1)}, bf16[2,2,256,512]{3,2,1,0:T(8,128)(2,1)}) custom-call(s32[8]{0:T(128)} %reshape.104.order_ref, bf16[16,32,2048]{2,1,0:T(8,128)(2,1)} %copy-done, bf16[2,256,512]{2,1,0:T(8,128)(2,1)} %get-tuple-element.44.gg_ref.act_ref), custom_call_target="tpu_custom_call" | custom-call | tf_op jit(solution)/shard_map/pallas_call | solution.py:207
  156.7 1.5 collective-permute-start.7
  158.2 10.9 %collective-permute-start.8 = (bf16[2,2,256,512]{3,2,1,0:T(8,128)(2,1)}, bf16[2,2,256,512]{3,2,1,0:T(8,128)(2,1)S(1)}, u32[]{:S(2)}, u32[]{:S(2)}) collective-permute-start(bf16[2,2,256,512]{3,2,1,0:T(8,128)(2,1)} %get-tuple-element.51), channel_id=1, source_target_pairs={{0,32},{16,48},{32,0},{48,16},{64,96},{80,112},{96,64},{112,80},{1... | collective-permute-start | bytes 3145736 | tf_op jit(solution)/shard_map/ppermute | solution.py:254
  169.1 0.6 pad_add_fusion.3.order_ref
  169.7 4.8 %shard_map.151 = (bf16[4,2,256,512]{3,2,1,0:T(8,128)(2,1)}, bf16[4,2,256,512]{3,2,1,0:T(8,128)(2,1)}) custom-call(s32[8]{0:T(128)} %pad_add_fusion.3.order_ref, bf16[16,32,2048]{2,1,0:T(8,128)(2,1)} %copy-done, bf16[2,256,512]{2,1,0:T(8,128)(2,1)} %get-tuple-element.45.ug_ref.act_ref), custom_call_target="tpu_custom_call" | custom-call | tf_op jit(solution)/shard_map/pallas_call | solution.py:207
  174.6 20.0 %collective-permute-start.11 = (bf16[4,2,256,512]{3,2,1,0:T(8,128)(2,1)}, bf16[4,2,256,512]{3,2,1,0:T(8,128)(2,1)}, u32[]{:S(2)}, u32[]{:S(2)}) collective-permute-start(bf16[4,2,256,512]{3,2,1,0:T(8,128)(2,1)} %get-tuple-element.57), channel_id=1, source_target_pairs={{0,64},{16,80},{32,96},{48,112},{64,0},{80,16},{96,32},{112,48},{1... | collective-permute-start | bytes 6291464 | tf_op jit(solution)/shard_map/ppermute | solution.py:261
  194.5 4.6 %shard_map.150 = (bf16[2,2,512,256]{3,2,1,0:T(8,128)(2,1)}, bf16[2,2,512,256]{3,2,1,0:T(8,128)(2,1)}, bf16[2,2,512,256]{3,2,1,0:T(8,128)(2,1)}, bf16[2,2,512,256]{3,2,1,0:T(8,128)(2,1)}) custom-call(s32[8]{0:T(128)} %reshape.104.order_ref, bf16[16,32,2048]{2,1,0:T(8,128)(2,1)} %copy-done.1, bf16[2,256,512]{2,1,0:T(8,128)(2,1)} %get-tuple-element.43.hidden_ref.act_ref), custom_call_target="tpu_custom_call" | custom-call | tf_op jit(solution)/shard_map/pallas_call | solution.py:207
  199.1 15.9 %collective-permute-done.8 = bf16[2,2,256,512]{3,2,1,0:T(8,128)(2,1)S(1)} collective-permute-done((bf16[2,2,256,512]{3,2,1,0:T(8,128)(2,1)}, bf16[2,2,256,512]{3,2,1,0:T(8,128)(2,1)S(1)}, u32[]{:S(2)}, u32[]{:S(2)}) %collective-permute-start.8) | collective-permute-done | bytes 1048608 | tf_op jit(solution)/shard_map/ppermute | solution.py:254
  215.1 3.6 %collective-permute-start.16 = (bf16[2,2,512,256]{3,2,1,0:T(8,128)(2,1)}, bf16[2,2,512,256]{3,2,1,0:T(8,128)(2,1)S(1)}, u32[]{:S(2)}, u32[]{:S(2)}) collective-permute-start(bf16[2,2,512,256]{3,2,1,0:T(8,128)(2,1)} %get-tuple-element.64), channel_id=1, source_target_pairs={{0,32},{16,48},{32,0},{48,16},{64,96},{80,112},{96,64},{112,80},{1... | collective-permute-start | bytes 3145736 | tf_op jit(solution)/shard_map/ppermute | solution.py:254
  218.7 2.5 convert_add_fusion.1
  221.2 0.1 fusion.4
  221.3 20.3 %collective-permute-start.10 = (bf16[2,256,512]{2,1,0:T(8,128)(2,1)S(1)}, bf16[2,256,512]{2,1,0:T(8,128)(2,1)}, u32[]{:S(2)}, u32[]{:S(2)}) collective-permute-start(bf16[2,256,512]{2,1,0:T(8,128)(2,1)S(1)} %fusion.4), channel_id=1, source_target_pairs={{0,64},{16,80},{32,96},{48,112},{64,0},{80,16},{96,32},{112,48},{1... | collective-permute-start | bytes 1572872 | tf_op jit(solution)/shard_map/ppermute | solution.py:261
  241.6 22.8 %collective-permute-done.16 = bf16[2,2,512,256]{3,2,1,0:T(8,128)(2,1)S(1)} collective-permute-done((bf16[2,2,512,256]{3,2,1,0:T(8,128)(2,1)}, bf16[2,2,512,256]{3,2,1,0:T(8,128)(2,1)S(1)}, u32[]{:S(2)}, u32[]{:S(2)}) %collective-permute-start.16) | collective-permute-done | bytes 1048608 | tf_op jit(solution)/shard_map/ppermute | solution.py:254
  264.5 0.5 convert_add_fusion
  264.9 1.3 copy-done.2
  266.2 0.1 fusion.5
  266.3 18.0 %collective-permute-start.18 = (bf16[2,512,256]{2,1,0:T(8,128)(2,1)S(1)}, bf16[2,512,256]{2,1,0:T(8,128)(2,1)}, u32[]{:S(2)}, u32[]{:S(2)}) collective-permute-start(bf16[2,512,256]{2,1,0:T(8,128)(2,1)S(1)} %fusion.5), channel_id=1, source_target_pairs={{0,64},{16,80},{32,96},{48,112},{64,0},{80,16},{96,32},{112,48},{1... | collective-permute-start | bytes 1572872 | tf_op jit(solution)/shard_map/ppermute | solution.py:261
  284.3 3.8 %pair_sum.1 = (f32[2,256,512]{2,1,0:T(8,128)}, bf16[2,256,512]{2,1,0:T(8,128)(2,1)}, bf16[2,256,512]{2,1,0:T(8,128)(2,1)}, bf16[2,256,512]{2,1,0:T(8,128)(2,1)}) custom-call(bf16[4,2,256,512]{3,2,1,0:T(8,128)(2,1)} %get-tuple-element.56.keep_ref, bf16[4,2,256,512]{3,2,1,0:T(8,128)(2,1)} %collective-permute-done.11.got_ref), custom_call_target="tpu_custom_call" | custom-call | tf_op jit(solution)/shard_map/pair_sum/pallas_call | solution.py:401
  288.1 1.2 collective-permute-start.12
  289.3 2.4 collective-permute-start.13
  291.7 1.8 collective-permute-start.14
  293.5 2.0 fusion.3
  295.5 0.1 collective-permute-done.18
  295.6 2.0 fusion.1
  297.6 4.7 %collective-permute-done.12 = bf16[2,256,512]{2,1,0:T(8,128)(2,1)S(1)} collective-permute-done((bf16[2,256,512]{2,1,0:T(8,128)(2,1)}, bf16[2,256,512]{2,1,0:T(8,128)(2,1)S(1)}, u32[]{:S(2)}, u32[]{:S(2)}) %collective-permute-start.12) | collective-permute-done | bytes 524320 | tf_op jit(solution)/shard_map/ppermute | solution.py:254
  302.3 12.4 %collective-permute-done.13 = bf16[2,256,512]{2,1,0:T(8,128)(2,1)S(1)} collective-permute-done((bf16[2,256,512]{2,1,0:T(8,128)(2,1)}, bf16[2,256,512]{2,1,0:T(8,128)(2,1)S(1)}, u32[]{:S(2)}, u32[]{:S(2)}) %collective-permute-start.13) | collective-permute-done | bytes 524320 | tf_op jit(solution)/shard_map/ppermute | solution.py:254
  314.7 1.1 add_convert_fusion
  315.8 3.5 %ngrad.1 = bf16[128,2048]{1,0:T(8,128)(2,1)} custom-call(bf16[16,4,16,2048]{3,2,1,0:T(8,128)(2,1)} %all-to-all-done.3.back_ref, bf16[512,128]{1,0:T(8,128)(2,1)} %get-tuple-element.38.pick0_ref, bf16[512,128]{1,0:T(8,128)(2,1)} %get-tuple-element.39.pick1_ref), custom_call_target="tpu_custom_call" | custom-call | tf_op jit(solution)/shard_map/ngrad/pallas_call | solution.py:387
  319.3 3.8 %mixed.1 = bf16[128,2048]{1,0:T(8,128)(2,1)} custom-call(bf16[16,4,16,2048]{3,2,1,0:T(8,128)(2,1)} %all-to-all-done.3.back_ref, bf16[512,128]{1,0:T(8,128)(2,1)} %get-tuple-element.38.pick0_ref, bf16[512,128]{1,0:T(8,128)(2,1)} %get-tuple-element.39.pick1_ref, f32[128,2]{1,0:T(8,128)} %copy.18.gates_ref), custom_call_target="tpu_custom_call" | custom-call | tf_op jit(solution)/shard_map/mixed/pallas_call | solution.py:384
  (36 shorter events, 0.1 us)
Async XLA Ops:
  0.6 12.5 %copy-start.10 = (f32[128,2]{0,1:T(2,128)S(1)}, f32[128,2]{0,1:T(2,128)}, u32[]{:S(2)}) copy-start(f32[128,2]{0,1:T(2,128)} %param.15) | copy-start | bytes 3076
  2.0 24.8 %copy-start.4 = (bf16[2,2048,128]{2,1,0:T(8,128)(2,1)}, bf16[2,2048,128]{2,1,0:T(8,128)(2,1)S(1)}, u32[]{:S(2)}) copy-start(bf16[2,2048,128]{2,1,0:T(8,128)(2,1)S(1)} %pad_maximum_fusion.kv) | copy-start | bytes 3145732
  2.0 28.6 %collective-permute-start.2 = (bf16[2,2048,128]{2,1,0:T(8,128)(2,1)S(1)}, bf16[2,2048,128]{2,1,0:T(8,128)(2,1)}, u32[]{:S(2)}, u32[]{:S(2)}) collective-permute-start(bf16[2,2048,128]{2,1,0:T(8,128)(2,1)S(1)} %pad_maximum_fusion.kv), channel_id=1, source_target_pairs={{0,64},{16,80},{32,96},{48,112},{1,65},{17,81},{33,97},{49,113},{2... | collective-permute-start | bytes 3145736 | tf_op jit(solution)/shard_map/ppermute | solution.py:279
  8.0 29.5 %collective-permute-start = (bf16[2,2048,128]{2,1,0:T(8,128)(2,1)S(1)}, bf16[2,2048,128]{2,1,0:T(8,128)(2,1)}, u32[]{:S(2)}, u32[]{:S(2)}) collective-permute-start(bf16[2,2048,128]{2,1,0:T(8,128)(2,1)S(1)} %pad_maximum_fusion.kv), channel_id=1, source_target_pairs={{0,32},{16,48},{32,0},{48,16},{64,96},{80,112},{1,33},{17,49},{33,... | collective-permute-start | bytes 3145736 | tf_op jit(solution)/shard_map/ppermute | solution.py:254
  17.8 59.7 %all-to-all-start = ((bf16[16,32,2048]{2,1,0:T(8,128)(2,1)}), bf16[16,32,2048]{2,1,0:T(8,128)(2,1)S(1)}, u32[]{:S(2)}, u32[]{:S(2)}) async-start(bf16[16,32,2048]{2,1,0:T(8,128)(2,1)} %get-tuple-element.36), calls=%async_computation | async-start | bytes 4194304 | tf_op jit(solution)/shard_map/all_to_all | solution.py:265
  23.2 34.5 %collective-permute-start.6 = (bf16[2,2048,128]{2,1,0:T(8,128)(2,1)S(1)}, bf16[2,2048,128]{2,1,0:T(8,128)(2,1)}, u32[]{:S(2)}, u32[]{:S(2)}) collective-permute-start(bf16[2,2048,128]{2,1,0:T(8,128)(2,1)S(1)} %pad_maximum_fusion.kv), channel_id=1, source_target_pairs={{0,16},{16,32},{32,48},{64,80},{80,96},{96,112},{1,17},{17,33},{33... | collective-permute-start | bytes 3145736 | tf_op jit(solution)/shard_map/ppermute | solution.py:254
  26.8 34.1 %collective-permute-start.5 = (bf16[2,2048,128]{2,1,0:T(8,128)(2,1)S(1)}, bf16[2,2048,128]{2,1,0:T(8,128)(2,1)}, u32[]{:S(2)}, u32[]{:S(2)}) collective-permute-start(bf16[2,2048,128]{2,1,0:T(8,128)(2,1)S(1)} %pad_maximum_fusion.kv), channel_id=1, source_target_pairs={{0,48},{64,112},{1,49},{65,113},{2,50},{66,114},{3,51},{67,115},{4... | collective-permute-start | bytes 3145736 | tf_op jit(solution)/shard_map/ppermute | solution.py:254
  30.6 33.6 %collective-permute-start.3 = (bf16[2,2048,128]{2,1,0:T(8,128)(2,1)}, bf16[2,2048,128]{2,1,0:T(8,128)(2,1)}, u32[]{:S(2)}, u32[]{:S(2)}) collective-permute-start(bf16[2,2048,128]{2,1,0:T(8,128)(2,1)} %collective-permute-done.2.refs_3_), channel_id=1, source_target_pairs={{64,80},{80,96},{96,112},{112,64},{65,81},{81,97},{97,113},{113,65... | collective-permute-start | bytes 3145736 | tf_op jit(solution)/shard_map/ppermute | solution.py:254
  32.2 31.9 %collective-permute-start.4 = (bf16[2,2048,128]{2,1,0:T(8,128)(2,1)}, bf16[2,2048,128]{2,1,0:T(8,128)(2,1)}, u32[]{:S(2)}, u32[]{:S(2)}) collective-permute-start(bf16[2,2048,128]{2,1,0:T(8,128)(2,1)} %collective-permute-done.2.refs_3_), channel_id=1, source_target_pairs={{64,112},{80,64},{96,80},{112,96},{65,113},{81,65},{97,81},{113,97... | collective-permute-start | bytes 3145736 | tf_op jit(solution)/shard_map/ppermute | solution.py:254
  37.5 37.1 %collective-permute-start.1 = (bf16[2,2048,128]{2,1,0:T(8,128)(2,1)}, bf16[2,2048,128]{2,1,0:T(8,128)(2,1)}, u32[]{:S(2)}, u32[]{:S(2)}) collective-permute-start(bf16[2,2048,128]{2,1,0:T(8,128)(2,1)} %collective-permute-done.refs_2_), channel_id=1, source_target_pairs={{0,64},{16,80},{32,96},{48,112},{1,65},{17,81},{33,97},{49,113},{2... | collective-permute-start | bytes 3145736 | tf_op jit(solution)/shard_map/ppermute | solution.py:284
  77.4 20.0 %copy-start.1 = (bf16[16,32,2048]{2,1,0:T(8,128)(2,1)}, bf16[16,32,2048]{2,1,0:T(8,128)(2,1)S(1)}, u32[]{:S(2)}) copy-start(bf16[16,32,2048]{2,1,0:T(8,128)(2,1)S(1)} %all-to-all-done.grad_ref.src) | copy-start | bytes 6291460
  97.4 31.5 %all-to-all-start.2 = ((bf16[16,32,2048]{2,1,0:T(8,128)(2,1)}), bf16[16,32,2048]{2,1,0:T(8,128)(2,1)S(1)}, u32[]{:S(2)}, u32[]{:S(2)}) async-start(bf16[16,32,2048]{2,1,0:T(8,128)(2,1)} %get-tuple-element.41), calls=%async_computation.2 | async-start | bytes 4194304 | tf_op jit(solution)/shard_map/all_to_all | solution.py:265
  128.9 1.3 copy-start
  146.8 169.0 %all-to-all-start.3 = ((bf16[16,4,16,2048]{3,2,1,0:T(8,128)(2,1)}), bf16[16,4,16,2048]{3,2,1,0:T(8,128)(2,1)}, u32[]{:S(2)}, u32[]{:S(2)}) async-start(bf16[16,4,16,2048]{3,2,1,0:T(8,128)(2,1)} %expert_back.1), calls=%async_computation.3 | async-start | bytes 8388608 | tf_op jit(solution)/shard_map/all_to_all | solution.py:265
  156.7 42.4 %collective-permute-start.7 = (bf16[2,2,256,512]{3,2,1,0:T(8,128)(2,1)}, bf16[2,2,256,512]{3,2,1,0:T(8,128)(2,1)S(1)}, u32[]{:S(2)}, u32[]{:S(2)}) collective-permute-start(bf16[2,2,256,512]{3,2,1,0:T(8,128)(2,1)} %get-tuple-element.50), channel_id=1, source_target_pairs={{0,16},{16,32},{32,48},{48,0},{64,80},{80,96},{96,112},{112,64},{1... | collective-permute-start | bytes 3145736 | tf_op jit(solution)/shard_map/ppermute | solution.py:254
  158.2 56.9 %collective-permute-start.8 = (bf16[2,2,256,512]{3,2,1,0:T(8,128)(2,1)}, bf16[2,2,256,512]{3,2,1,0:T(8,128)(2,1)S(1)}, u32[]{:S(2)}, u32[]{:S(2)}) collective-permute-start(bf16[2,2,256,512]{3,2,1,0:T(8,128)(2,1)} %get-tuple-element.51), channel_id=1, source_target_pairs={{0,32},{16,48},{32,0},{48,16},{64,96},{80,112},{96,64},{112,80},{1... | collective-permute-start | bytes 3145736 | tf_op jit(solution)/shard_map/ppermute | solution.py:254
  169.1 46.0 %collective-permute-start.9 = (bf16[2,2,256,512]{3,2,1,0:T(8,128)(2,1)}, bf16[2,2,256,512]{3,2,1,0:T(8,128)(2,1)}, u32[]{:S(2)}, u32[]{:S(2)}) collective-permute-start(bf16[2,2,256,512]{3,2,1,0:T(8,128)(2,1)} %get-tuple-element.52), channel_id=1, source_target_pairs={{0,48},{16,0},{32,16},{48,32},{64,112},{80,64},{96,80},{112,96},{1... | collective-permute-start | bytes 3145736 | tf_op jit(solution)/shard_map/ppermute | solution.py:254
  169.7 49.0 %copy-start.6 = (bf16[2,2,256,512]{3,2,1,0:T(8,128)(2,1)S(1)}, bf16[2,2,256,512]{3,2,1,0:T(8,128)(2,1)}, u32[]{:S(2)}) copy-start(bf16[2,2,256,512]{3,2,1,0:T(8,128)(2,1)} %get-tuple-element.46) | copy-start | bytes 3145732
  174.6 109.7 %collective-permute-start.11 = (bf16[4,2,256,512]{3,2,1,0:T(8,128)(2,1)}, bf16[4,2,256,512]{3,2,1,0:T(8,128)(2,1)}, u32[]{:S(2)}, u32[]{:S(2)}) collective-permute-start(bf16[4,2,256,512]{3,2,1,0:T(8,128)(2,1)} %get-tuple-element.57), channel_id=1, source_target_pairs={{0,64},{16,80},{32,96},{48,112},{64,0},{80,16},{96,32},{112,48},{1... | collective-permute-start | bytes 6291464 | tf_op jit(solution)/shard_map/ppermute | solution.py:261
  199.1 19.6 %copy-start.7 = (bf16[2,2,256,512]{3,2,1,0:T(8,128)(2,1)}, bf16[2,2,256,512]{3,2,1,0:T(8,128)(2,1)S(1)}, u32[]{:S(2)}) copy-start(bf16[2,2,256,512]{3,2,1,0:T(8,128)(2,1)S(1)} %collective-permute-done.7) | copy-start | bytes 3145732
  215.1 3.6 %copy-start.8 = (bf16[2,2,256,512]{3,2,1,0:T(8,128)(2,1)}, bf16[2,2,256,512]{3,2,1,0:T(8,128)(2,1)S(1)}, u32[]{:S(2)}) copy-start(bf16[2,2,256,512]{3,2,1,0:T(8,128)(2,1)S(1)} %collective-permute-done.8) | copy-start | bytes 3145732
  215.1 26.6 %collective-permute-start.15 = (bf16[2,2,512,256]{3,2,1,0:T(8,128)(2,1)}, bf16[2,2,512,256]{3,2,1,0:T(8,128)(2,1)S(1)}, u32[]{:S(2)}, u32[]{:S(2)}) collective-permute-start(bf16[2,2,512,256]{3,2,1,0:T(8,128)(2,1)} %get-tuple-element.63), channel_id=1, source_target_pairs={{0,16},{16,32},{32,48},{48,0},{64,80},{80,96},{96,112},{112,64},{1... | collective-permute-start | bytes 3145736 | tf_op jit(solution)/shard_map/ppermute | solution.py:254
  215.1 49.4 %collective-permute-start.16 = (bf16[2,2,512,256]{3,2,1,0:T(8,128)(2,1)}, bf16[2,2,512,256]{3,2,1,0:T(8,128)(2,1)S(1)}, u32[]{:S(2)}, u32[]{:S(2)}) collective-permute-start(bf16[2,2,512,256]{3,2,1,0:T(8,128)(2,1)} %get-tuple-element.64), channel_id=1, source_target_pairs={{0,32},{16,48},{32,0},{48,16},{64,96},{80,112},{96,64},{112,80},{1... | collective-permute-start | bytes 3145736 | tf_op jit(solution)/shard_map/ppermute | solution.py:254
  218.7 45.7 %collective-permute-start.17 = (bf16[2,2,512,256]{3,2,1,0:T(8,128)(2,1)}, bf16[2,2,512,256]{3,2,1,0:T(8,128)(2,1)S(1)}, u32[]{:S(2)}, u32[]{:S(2)}) collective-permute-start(bf16[2,2,512,256]{3,2,1,0:T(8,128)(2,1)} %get-tuple-element.65), channel_id=1, source_target_pairs={{0,48},{16,0},{32,16},{48,32},{64,112},{80,64},{96,80},{112,96},{1... | collective-permute-start | bytes 3145736 | tf_op jit(solution)/shard_map/ppermute | solution.py:254
  218.7 45.7 %copy-start.9 = (bf16[2,2,512,256]{3,2,1,0:T(8,128)(2,1)S(1)}, bf16[2,2,512,256]{3,2,1,0:T(8,128)(2,1)}, u32[]{:S(2)}) copy-start(bf16[2,2,512,256]{3,2,1,0:T(8,128)(2,1)} %get-tuple-element.62) | copy-start | bytes 3145732
  221.3 72.2 %collective-permute-start.10 = (bf16[2,256,512]{2,1,0:T(8,128)(2,1)S(1)}, bf16[2,256,512]{2,1,0:T(8,128)(2,1)}, u32[]{:S(2)}, u32[]{:S(2)}) collective-permute-start(bf16[2,256,512]{2,1,0:T(8,128)(2,1)S(1)} %fusion.4), channel_id=1, source_target_pairs={{0,64},{16,80},{32,96},{48,112},{64,0},{80,16},{96,32},{112,48},{1... | collective-permute-start | bytes 1572872 | tf_op jit(solution)/shard_map/ppermute | solution.py:261
  264.9 1.3 copy-start.2
  266.3 29.3 %collective-permute-start.18 = (bf16[2,512,256]{2,1,0:T(8,128)(2,1)S(1)}, bf16[2,512,256]{2,1,0:T(8,128)(2,1)}, u32[]{:S(2)}, u32[]{:S(2)}) collective-permute-start(bf16[2,512,256]{2,1,0:T(8,128)(2,1)S(1)} %fusion.5), channel_id=1, source_target_pairs={{0,64},{16,80},{32,96},{48,112},{64,0},{80,16},{96,32},{112,48},{1... | collective-permute-start | bytes 1572872 | tf_op jit(solution)/shard_map/ppermute | solution.py:261
  288.1 7.5 %copy-start.3 = (f32[2,2,512,256]{3,2,1,0:T(8,128)S(1)}, f32[2,2,512,256]{3,2,1,0:T(8,128)}, u32[]{:S(2)}) copy-start(f32[2,2,512,256]{3,2,1,0:T(8,128)} %copy-done.2) | copy-start | bytes 6291460
  288.1 14.2 %collective-permute-start.12 = (bf16[2,256,512]{2,1,0:T(8,128)(2,1)}, bf16[2,256,512]{2,1,0:T(8,128)(2,1)S(1)}, u32[]{:S(2)}, u32[]{:S(2)}) collective-permute-start(bf16[2,256,512]{2,1,0:T(8,128)(2,1)} %get-tuple-element.59), channel_id=1, source_target_pairs={{0,16},{16,32},{32,48},{48,0},{64,80},{80,96},{96,112},{112,64},{1... | collective-permute-start | bytes 1572872 | tf_op jit(solution)/shard_map/ppermute | solution.py:254
  289.3 25.4 %collective-permute-start.13 = (bf16[2,256,512]{2,1,0:T(8,128)(2,1)}, bf16[2,256,512]{2,1,0:T(8,128)(2,1)S(1)}, u32[]{:S(2)}, u32[]{:S(2)}) collective-permute-start(bf16[2,256,512]{2,1,0:T(8,128)(2,1)} %get-tuple-element.60), channel_id=1, source_target_pairs={{0,32},{16,48},{32,0},{48,16},{64,96},{80,112},{96,64},{112,80},{1... | collective-permute-start | bytes 1572872 | tf_op jit(solution)/shard_map/ppermute | solution.py:254
  291.7 23.0 %copy-start.5 = (f32[2,256,512]{2,1,0:T(8,128)S(1)}, f32[2,256,512]{2,1,0:T(8,128)}, u32[]{:S(2)}) copy-start(f32[2,256,512]{2,1,0:T(8,128)} %get-tuple-element.58) | copy-start | bytes 3145732
  291.7 23.0 %collective-permute-start.14 = (bf16[2,256,512]{2,1,0:T(8,128)(2,1)}, bf16[2,256,512]{2,1,0:T(8,128)(2,1)S(1)}, u32[]{:S(2)}, u32[]{:S(2)}) collective-permute-start(bf16[2,256,512]{2,1,0:T(8,128)(2,1)} %get-tuple-element.61), channel_id=1, source_target_pairs={{0,48},{16,0},{32,16},{48,32},{64,112},{80,64},{96,80},{112,96},{1... | collective-permute-start | bytes 1572872 | tf_op jit(solution)/shard_map/ppermute | solution.py:254

commit v2 on v1

--- a/solution.py
+++ b/solution.py
@@ -2,6 +2,7 @@
 
 import jax
 import jax.numpy as jnp
+import numpy as np
 from jax import lax
 from jax.experimental import pallas as pl
 from jax.experimental.pallas import tpu as pltpu
@@ -86,45 +87,59 @@
     )(q, kv)
 
 
-def attend(flags, q, kvs, base, out_type):
-    rows = q.shape[0]
-    count = len(kvs)
+def attend(table, offset, work, queries, kvs, bases, out_types):
+    rows = queries[0].shape[-2]
+    count = len(work)
+    counts = (len(queries), len(kvs), sum(b is not None for b in bases), len(out_types))
 
     def kernel(*refs):
-        flags_ref, q_ref = refs[0], refs[1]
-        kv_refs = refs[2 : 2 + count]
-        base_ref = refs[2 + count]
-        out, acc, turned, value = refs[-4:]
-        acc[...] = base_ref[...]
+        flags_ref, refs = refs[0], refs[1:]
+        groups = []
+        for size in counts:
+            groups.append(refs[:size])
+            refs = refs[size:]
+        q_refs, kv_refs, base_refs, outs = groups
+        acc, q_all, turned, value = refs
+        base_refs = list(base_refs)
+        for n, q in enumerate(q_refs):
+            q_all[n] = q[0] if len(q.shape) == 3 else q[...]
+            if bases[n] is None:
+                acc[n] = jnp.zeros(acc.shape[1:], F32)
+            else:
+                acc[n] = base_refs.pop(0)[...]
 
         def one(n, carry):
-            @pl.when(flags_ref[n] != 0)
+            @pl.when(flags_ref[offset + n] != 0)
             def _():
-                for m, kv in enumerate(kv_refs):
+                side = flags_ref[offset + n] - 1
+                for m, (_, source) in enumerate(work):
 
                     @pl.when(n == m)
-                    def _(kv=kv):
-                        turned[...] = kv[0].T
-                        value[...] = kv[1]
-
-                add_block(q_ref, turned, value, acc, rows)
+                    def _(source=source):
+                        turned[...] = kv_refs[source][0].T
+                        value[...] = kv_refs[source][1]
+
+                add_block(q_all.at[side], turned, value, acc.at[side], rows)
 
             return carry
 
         lax.fori_loop(0, count, one, 0)
-        out[...] = acc[...].astype(out_type)
-
+        for n, out in enumerate(outs):
+            out[...] = acc[n].astype(out.dtype)
+
+    used = [b for b in bases if b is not None]
     return pl.pallas_call(
         kernel,
-        out_shape=jax.ShapeDtypeStruct((rows, HEAD_DIM), out_type),
-        in_specs=[smem()] + [vmem()] * (2 + count),
-        out_specs=vmem(),
+        out_shape=tuple(jax.ShapeDtypeStruct((rows, HEAD_DIM), t) for t in out_types),
+        in_specs=[smem()] + [vmem()] * sum(counts[:3]),
+        out_specs=(vmem(),) * len(out_types),
         scratch_shapes=[
-            pltpu.VMEM((rows, HEAD_DIM), F32),
+            pltpu.VMEM((len(queries), rows, HEAD_DIM), F32),
+            pltpu.VMEM((len(queries), rows, HEAD_DIM), BF16),
             pltpu.VMEM((HEAD_DIM, rows), BF16),
             pltpu.VMEM((rows, HEAD_DIM), BF16),
         ],
-    )(flags, q, *kvs, base)
+    )(table, *queries, *kvs, *used)
 
 
 def route_kernel(ids_ref, gates_ref, grad_ref, pick0_ref, pick1_ref, send_ref):
@@ -187,7 +202,7 @@
     ug_ref[0] = (hidden_grad * silu).astype(BF16)
 
 
-def weight_grad(order, source, act, groups, turned):
+def weight_grad(table, offset, source, act, groups, turned):
     cols = source.shape[2] // 8
     hid = act.shape[2]
     piece = (hid, cols) if turned else (cols, hid)
@@ -198,7 +213,7 @@
             done = 0
             for out, count in zip(outs, groups):
                 for n in range(count):
-                    at = pl.ds(pl.multiple_of(order_ref[done] * cols, cols), cols)
+                    at = pl.ds(pl.multiple_of(order_ref[offset + done] * cols, cols), cols)
                     rows = src[:, e * CAP : (e + 1) * CAP, at].reshape(ROWS, cols)
                     grad = mm(side, rows, 1, 0) if turned else mm(rows, side, 0, 0)
                     out[n, e] = grad.astype(BF16)
@@ -209,7 +224,7 @@
         out_shape=tuple(jax.ShapeDtypeStruct((c, 2, *piece), BF16) for c in groups),
         in_specs=[smem(), vmem(), vmem()],
         out_specs=(vmem(),) * len(groups),
-    )(order, source, act)
+    )(table, source, act)
 
 
 def expert_back_kernel(hidden_ref, down_ref, gg_ref, ug_ref, gate_ref, up_ref, out_ref):
@@ -265,23 +280,37 @@
     return lax.all_to_all(value, "exp", split_axis=0, concat_axis=0, tiled=True)
 
 
+AT_NEAR, AT_FAR, AT_REST, AT_Y, AT_X = 0, 4, 6, 8, 16
+
+
+def shard_table():
+    lines = []
+    for shard in range(8):
+        hi, y = divmod(shard, 4)
+        low, high = int(hi == 0), hi
+        line = [2 * low, int(y >= 1), high, int(y >= 3), 2 * low, high, int(y >= 2), 0]
+        for n in (1, 2, 3, 0):
+            line += [hi * 4 + (y + n) % 4, (1 - hi) * 4 + (y + n) % 4]
+        line += [(1 - hi) * 4 + (y + n) % 4 for n in range(4)]
+        line += [hi * 4 + (y + n) % 4 for n in range(4)]
+        lines.append(line)
+    return np.asarray(lines, np.int32)
+
+
 def step(queries, keys, values, gate_input, route_ids, route_gates, w_gate, w_up, w_down, out_grad):
     width = gate_input.shape[1]
     hid = w_gate.shape[2]
     ctx = lax.axis_index("ctx")
-    hi, y = ctx // 4, ctx % 4
     full = jax.ShapeDtypeStruct
     down_x = [(n, 4 + n) for n in range(4)]
-    in_high = lambda hi, y: hi == 1
+    table = lax.dynamic_index_in_dim(jnp.asarray(shard_table()), ctx, 0, keepdims=False)
 
     kv = jnp.stack([keys, values])
-    from_y1 = move_y(kv, 1, lambda hi, y: y < 3)
-    from_x = lax.ppermute(kv, "ctx", down_x)
-    from_y2 = move_y(kv, 2, lambda hi, y: hi == 0 or y < 2)
+    from_y1 = move_y(kv, 1, lambda hi, y: hi == 0 or y < 3)
+    from_x = move_x(jnp.where(ctx >= 4, queries[None], kv))
     from_y3 = move_y(kv, 3, lambda hi, y: y == 0)
-    from_xy1 = move_y(from_x, 1, in_high)
-    from_xy3 = move_y(from_x, 3, in_high)
-    from_xx = lax.ppermute(from_y2, "ctx", down_x)
+    from_y2 = move_y(from_y1, 1, lambda hi, y: hi == 0 or y in (1, 2))
+    from_xy3 = move_y(from_x, 3, lambda hi, y: hi == 1)
 
     pick0, pick1, send_grads = pl.pallas_call(
         route_kernel,
@@ -296,18 +325,28 @@
     )(route_ids.T, route_gates, out_grad)
     recv_grads = exchange(send_grads)
 
-    flag = lambda *conds: jnp.stack([c.astype(jnp.int32) for c in conds])
-    high = hi == 1
     acc = attend_own(queries, kv)
-    stages = (
-        (flag(y >= 1, high), [from_y1, from_x], F32),
-        (flag(y >= 2, y >= 3), [from_y2, from_y3], F32),
-        (flag(high, high), [from_xy1, from_xy3], F32),
-        (flag(high), [from_xx], BF16),
-    )
-    for flags, blocks, kind in stages:
-        acc = attend(flags, queries, blocks, acc, kind)
-    attended = acc
+    acc, lent = attend(
+        table,
+        AT_NEAR,
+        ((1, 0), (0, 0), (0, 1), (0, 2)),
+        [queries, from_x],
+        [from_y1, from_x, from_y3],
+        [acc, None],
+        (F32, F32),
+    )
+    acc, lent = attend(
+        table,
+        AT_FAR,
+        ((1, 0), (0, 1)),
+        [queries, from_x],
+        [from_y2, from_xy3],
+        [acc, lent],
+        (F32, BF16),
+    )
+    returned = lax.ppermute(lent, "ctx", down_x)
+    (acc,) = attend(table, AT_REST, ((0, 0),), [queries], [from_y2], [acc], (F32,))
+    attended = (acc + returned.astype(F32)).astype(BF16)
 
     expert_block = pl.BlockSpec((N_EXP, CAP, width), lambda e: (0, e, 0))
     in_weight = pl.BlockSpec((1, width, hid), lambda e: (e, 0, 0))
@@ -342,19 +381,13 @@
         name="expert_in",
     )(recv_inputs, hidden_grad, w_gate, w_up)
 
-    turn = jnp.arange(4, dtype=jnp.int32)
-    x_order = jnp.concatenate([(1 - hi) * 4 + (y + turn) % 4, hi * 4 + (y + turn) % 4])
-    far = (turn + 1) % 4
-    y_order = jnp.stack(
-        [hi * 4 + (y + far) % 4, (1 - hi) * 4 + (y + far) % 4], axis=1
-    ).reshape(8)
-    ga = weight_grad(y_order, recv_inputs, gate_grad, (2, 2, 2, 2), False)
+    ga = weight_grad(table, AT_Y, recv_inputs, gate_grad, (2, 2, 2, 2), False)
     got_g = []
     for n in range(3):
         got_g.append(move_y(ga[n], n + 1))
-    up_send, up_keep = weight_grad(x_order, recv_inputs, up_grad, (4, 4), False)
+    up_send, up_keep = weight_grad(table, AT_X, recv_inputs, up_grad, (4, 4), False)
     up_got = move_x(up_send)
-    do = weight_grad(y_order, recv_grads, hidden, (2, 2, 2, 2), True)
+    do = weight_grad(table, AT_Y, recv_grads, hidden, (2, 2, 2, 2), True)
     held = lax.optimization_barrier((*do[:3], *got_g))
     got_g = held[3:]
     got_d = []
@@ -396,7 +429,6 @@
 
     gate_part, gate_send = over_row(ga[3], got_g)
     gate_got = move_x(gate_send)
-    gate_sum = (gate_part + wide(gate_got)).astype(BF16)
     quarter = up_keep.shape[1:]
     up_part, *up_rest = pl.pallas_call(
         pair_sum_kernel,
@@ -408,6 +440,10 @@
     got_u = []
     for n in (1, 2, 3):
         got_u.append(move_y(up_rest[n - 1], n))
+    mixed, normed_grad, gate_got, *got_u = lax.optimization_barrier(
+        (mixed, normed_grad, gate_got, *got_u)
+    )
+    gate_sum = (gate_part + wide(gate_got)).astype(BF16)
     up_sum = (up_part + wide(got_u[0]) + wide(got_u[1]) + wide(got_u[2])).astype(BF16)
     down_part, down_send = over_row(do[3], got_d)
     down_got = move_x(down_send)

time: 324 us -> 327 us (level)
  starting transfers between devices: 121 us -> 66.4 us
  waiting for transfers between devices: 97.6 us -> 142 us
  Pallas kernels: 71.9 us -> 81.9 us
    ppermute x3 -> x4, starting transfers between devices: 58.3 us -> 13 us  [move_x(): return lax.ppermute(value, 'ctx', pairs)]
    ppermute x14 -> x13, waiting for transfers between devices: 65.3 us -> 107 us  [move_y(): return lax.ppermute(value, 'ctx', pairs)]
    pallas_call x4 -> x3, Pallas kernels: 12.4 us -> 22.6 us  [attend(): pl.pallas_call(kernel, out_shape=tuple((jax.ShapeDtypeStruct((rows, HEAD_...]
    ppermute x2 -> x1, starting transfers between devices: 13.1 us -> 5.75 us  [step(): returned = lax.ppermute(lent, 'ctx', down_x)]
    ppermute x14 -> x13, starting transfers between devices: 35.7 us -> 33.1 us  [move_y(): return lax.ppermute(value, 'ctx', pairs)]
    ppermute x2 -> x1, waiting for transfers between devices: 8.82 us -> 9.14 us  [step(): returned = lax.ppermute(lent, 'ctx', down_x)]
  transfers between devices with their start and end apart: 22 -> 21, of which waited for: 10 -> 10; matrix products, arithmetic and copies ran while one was open for 4% -> 4% of each run, Pallas kernels for 14% -> 19%
where the time goes in v2:
time: 327 us; the launch traced here: 325 us
  waiting for transfers between devices  142 us (43%)
  Pallas kernels  81.9 us (25%)
  starting transfers between devices  66.4 us (20%)
  blocking collectives  15.6 us (5%)
  other arithmetic  13.9 us (4%)
  local copies, waits for them, and re-layouts  5.1 us (2%)
    ppermute x13, waiting for transfers between devices, move_y(): return lax.ppermute(value, 'ctx', pairs)  107 us
    ppermute x13, starting transfers between devices, move_y(): return lax.ppermute(value, 'ctx', pairs)  33.1 us
    all_to_all x3, waiting for transfers between devices, exchange(): return lax.all_to_all(value, 'exp', split_axis=0, concat_axis=0, tiled=True)  23.3 us
    pallas_call x3, Pallas kernels, attend(): pl.pallas_call(kernel, out_shape=tuple((jax.ShapeDtypeStruct((rows, HEAD_...  22.6 us
    all_to_all x1, blocking collectives, exchange(): return lax.all_to_all(value, 'exp', split_axis=0, concat_axis=0, tiled=True)  15.6 us
    all_to_all x3, starting transfers between devices, exchange(): return lax.all_to_all(value, 'exp', split_axis=0, concat_axis=0, tiled=True)  14.6 us
    pallas_call x3, Pallas kernels, weight_grad(): pl.pallas_call(kernel, out_shape=tuple((jax.ShapeDtypeStruct((c, 2, *piec...  13.9 us
    ppermute x4, starting transfers between devices, move_x(): return lax.ppermute(value, 'ctx', pairs)  13 us
  transfers between devices with their start and end apart: 21, of which 10 were waited for; matrix products, arithmetic and copies ran while one was open for 4% of the time, Pallas kernels for 19%

profile of v2, /device:TPU:0, one launch (start us, length us, event | category | flops | bytes accessed | tf_op | source)
XLA Modules:
  0.0 325.4 jit_solution(2929181943056047687)
XLA Ops:
  0.6 2.6 broadcast_select_fusion
  3.2 3.6 %collective-permute-start = (bf16[2,2048,128]{2,1,0:T(8,128)(2,1)}, bf16[2,2048,128]{2,1,0:T(8,128)(2,1)}, u32[]{:S(2)}, u32[]{:S(2)}) collective-permute-start(bf16[2,2048,128]{2,1,0:T(8,128)(2,1)} %get-tuple-element.87.kv), channel_id=1, source_target_pairs={{0,16},{16,32},{32,48},{48,0},{64,80},{80,96},{96,112},{1,17},{17,... | collective-permute-start | bytes 3145736 | tf_op jit(solution)/shard_map/ppermute | solution.py:269
  6.8 4.0 %collective-permute-start.2 = (bf16[2,2048,128]{2,1,0:T(8,128)(2,1)S(1)}, bf16[2,2048,128]{2,1,0:T(8,128)(2,1)S(1)}, u32[]{:S(2)}, u32[]{:S(2)}) collective-permute-start(bf16[2,2048,128]{2,1,0:T(8,128)(2,1)S(1)} %get-tuple-element.86), channel_id=1, source_target_pairs={{0,64},{16,80},{32,96},{48,112},{64,0},{80,16},{96,32},{112,48},{1... | collective-permute-start | bytes 3145736 | tf_op jit(solution)/shard_map/ppermute | solution.py:276
  10.8 2.8 collective-permute-start.4
  13.6 18.1 %collective-permute-done.refs_3_ = bf16[2,2048,128]{2,1,0:T(8,128)(2,1)} collective-permute-done((bf16[2,2048,128]{2,1,0:T(8,128)(2,1)}, bf16[2,2048,128]{2,1,0:T(8,128)(2,1)}, u32[]{:S(2)}, u32[]{:S(2)}) %collective-permute-start) | collective-permute-done | bytes 1048608 | tf_op jit(solution)/shard_map/ppermute | solution.py:269
  31.7 2.2 collective-permute-start.1
  33.9 0.0 collective-permute-done.2.refs_2_.refs_4_
  33.9 1.7 collective-permute-start.3
  35.6 0.7 copy.17.gates_ref
  36.3 3.9 %route.1 = (bf16[512,128]{1,0:T(8,128)(2,1)}, bf16[512,128]{1,0:T(8,128)(2,1)}, bf16[16,32,2048]{2,1,0:T(8,128)(2,1)}) custom-call(s32[2,128]{1,0:T(2,128)} %bitcast.25, f32[128,2]{1,0:T(8,128)} %copy.17.gates_ref, bf16[128,2048]{1,0:T(8,128)(2,1)} %grad_ref.1), custom_call_target="tpu_custom_call" | custom-call | tf_op jit(solution)/shard_map/route/pallas_call | solution.py:315
  40.2 6.3 %all-to-all-start = ((bf16[16,32,2048]{2,1,0:T(8,128)(2,1)}), bf16[16,32,2048]{2,1,0:T(8,128)(2,1)S(1)}, u32[]{:S(2)}, u32[]{:S(2)}) async-start(bf16[16,32,2048]{2,1,0:T(8,128)(2,1)} %get-tuple-element.50), calls=%async_computation | async-start | bytes 4194304 | tf_op jit(solution)/shard_map/all_to_all | solution.py:280
  46.6 5.6 %attend_own.1.refs_6_ = f32[2048,128]{1,0:T(8,128)} custom-call(bf16[2048,128]{1,0:T(8,128)(2,1)} %refs_1_.5, bf16[2,2048,128]{2,1,0:T(8,128)(2,1)} %get-tuple-element.87.kv), custom_call_target="tpu_custom_call" | custom-call | tf_op jit(solution)/shard_map/attend_own/pallas_call | solution.py:80
  52.2 1.2 dynamic-slice_bitcast_fusion.refs_0_.order_ref
  53.4 0.0 collective-permute-done.4.refs_5_
  53.4 10.0 %shard_map.154 = (f32[2048,128]{1,0:T(8,128)}, f32[2048,128]{1,0:T(8,128)}) custom-call(s32[24]{0:T(128)} %dynamic-slice_bitcast_fusion.refs_0_.order_ref, bf16[2048,128]{1,0:T(8,128)(2,1)} %refs_1_.5, bf16[2,2048,128]{2,1,0:T(8,128)(2,1)} %copy-done.2, bf16[2,2048,128]{2,1,0:T(8,128)(2,1)} %collective-permute-done.refs_3_, bf16[2,2048,128]{2,1,0:T(8,128)(2,1)} %copy-done.2, ...), custom_call_target="tpu_custom_call" | custom-call | tf_op jit(solution)/shard_map/pallas_call | solution.py:131
  63.4 0.0 collective-permute-done.1.refs_3_.refs_2_
  63.4 9.7 %shard_map.155 = (f32[2048,128]{1,0:T(8,128)}, bf16[2048,128]{1,0:T(8,128)(2,1)}) custom-call(s32[24]{0:T(128)} %dynamic-slice_bitcast_fusion.refs_0_.order_ref, bf16[2048,128]{1,0:T(8,128)(2,1)} %refs_1_.5, bf16[2,2048,128]{2,1,0:T(8,128)(2,1)} %copy-done.2, bf16[2,2048,128]{2,1,0:T(8,128)(2,1)} %collective-permute-done.1.refs_3_.refs_2_, ...), custom_call_target="tpu_custom_call" | custom-call | tf_op jit(solution)/shard_map/pallas_call | solution.py:131
  73.1 5.7 %collective-permute-start.5 = (bf16[2048,128]{1,0:T(8,128)(2,1)}, bf16[2048,128]{1,0:T(8,128)(2,1)S(1)}, u32[]{:S(2)}, u32[]{:S(2)}) collective-permute-start(bf16[2048,128]{1,0:T(8,128)(2,1)} %get-tuple-element.49), channel_id=1, source_target_pairs={{0,64},{16,80},{32,96},{48,112},{1,65},{17,81},{33,97},{49,113},{2... | collective-permute-start | bytes 1572872 | tf_op jit(solution)/shard_map/ppermute | solution.py:347
  78.8 2.9 shard_map.156
  81.7 9.1 %collective-permute-done.5 = bf16[2048,128]{1,0:T(8,128)(2,1)S(1)} collective-permute-done((bf16[2048,128]{1,0:T(8,128)(2,1)}, bf16[2048,128]{1,0:T(8,128)(2,1)S(1)}, u32[]{:S(2)}, u32[]{:S(2)}) %collective-permute-start.5) | collective-permute-done | bytes 524320 | tf_op jit(solution)/shard_map/ppermute | solution.py:347
  90.9 1.3 add_convert_fusion.1
  92.2 15.6 %all_to_all.20.tok_ref = bf16[16,128,128]{2,1,0:T(8,128)(2,1)} all-to-all(bf16[16,128,128]{2,1,0:T(8,128)(2,1)S(1)} %bitcast.22), channel_id=1, replica_groups=mesh['ctx'=8,'exp'=16] {'exp'}, dimensions={0} | all-to-all | bytes 1048576 | tf_op jit(solution)/shard_map/all_to_all | solution.py:280
  107.8 3.7 %norm.1 = (bf16[128,2048]{1,0:T(8,128)(2,1)}, bf16[16,32,2048]{2,1,0:T(8,128)(2,1)}) custom-call(bf16[16,128,128]{2,1,0:T(8,128)(2,1)} %all_to_all.20.tok_ref, bf16[128,2048]{1,0:T(8,128)(2,1)} %gate_ref.3, bf16[512,128]{1,0:T(8,128)(2,1)} %get-tuple-element.52.pick0_ref, bf16[512,128]{1,0:T(8,128)(2,1)} %get-tuple-element.53.pick1_ref), custom_call_target="tpu_custom_call" | custom-call | tf_op jit(solution)/shard_map/norm/pallas_call | solution.py:365
  111.5 3.7 %all-to-all-start.2 = ((bf16[16,32,2048]{2,1,0:T(8,128)(2,1)}), bf16[16,32,2048]{2,1,0:T(8,128)(2,1)S(1)}, u32[]{:S(2)}, u32[]{:S(2)}) async-start(bf16[16,32,2048]{2,1,0:T(8,128)(2,1)} %get-tuple-element.55), calls=%async_computation.2 | async-start | bytes 4194304 | tf_op jit(solution)/shard_map/all_to_all | solution.py:280
  115.2 4.5 %hidden_grad.1.hg_ref = f32[2,256,512]{2,1,0:T(8,128)} custom-call(bf16[16,32,2048]{2,1,0:T(8,128)(2,1)} %copy-done.1, bf16[2,512,2048]{2,1,0:T(8,128)(2,1)} %down_ref.3), custom_call_target="tpu_custom_call" | custom-call | tf_op jit(solution)/shard_map/hidden_grad/pallas_call | solution.py:357
  119.6 23.3 %all-to-all-done.2.in_ref.src = bf16[16,32,2048]{2,1,0:T(8,128)(2,1)S(1)} async-done(((bf16[16,32,2048]{2,1,0:T(8,128)(2,1)}), bf16[16,32,2048]{2,1,0:T(8,128)(2,1)S(1)}, u32[]{:S(2)}, u32[]{:S(2)}) %all-to-all-start.2) | async-done | bytes 2097184 | tf_op jit(solution)/shard_map/all_to_all | solution.py:280
  143.0 1.4 copy-done
  144.3 6.6 %expert_in.1 = (bf16[2,256,512]{2,1,0:T(8,128)(2,1)}, bf16[2,256,512]{2,1,0:T(8,128)(2,1)}, bf16[2,256,512]{2,1,0:T(8,128)(2,1)}) custom-call(bf16[16,32,2048]{2,1,0:T(8,128)(2,1)} %copy-done, f32[2,256,512]{2,1,0:T(8,128)} %hidden_grad.1.hg_ref, bf16[2,2048,512]{2,1,0:T(8,128)(2,1)} %gate_ref.5, bf16[2,2048,512]{2,1,0:T(8,128)(2,1)} %up_ref.3), custom_call_target="tpu_custom_call" | custom-call | tf_op jit(solution)/shard_map/expert_in/pallas_call | solution.py:375
  150.9 10.0 %expert_back.1 = bf16[16,4,16,2048]{3,2,1,0:T(8,128)(2,1)} custom-call(bf16[2,256,512]{2,1,0:T(8,128)(2,1)} %get-tuple-element.57.hidden_ref.act_ref, bf16[2,512,2048]{2,1,0:T(8,128)(2,1)} %down_ref.3, bf16[2,256,512]{2,1,0:T(8,128)(2,1)} %get-tuple-element.58.gg_ref.act_ref, bf16[2,256,512]{2,1,0:T(8,128)(2,1)} %get-tuple-element.59.ug_ref.act_ref, ...), custom_call_target="tpu_custom_call" | custom-call | tf_op jit(solution)/shard_map/expert_back/pallas_call | solution.py:399
  160.9 4.5 %all-to-all-start.3 = ((bf16[16,4,16,2048]{3,2,1,0:T(8,128)(2,1)}), bf16[16,4,16,2048]{3,2,1,0:T(8,128)(2,1)}, u32[]{:S(2)}, u32[]{:S(2)}) async-start(bf16[16,4,16,2048]{3,2,1,0:T(8,128)(2,1)} %expert_back.1), calls=%async_computation.3 | async-start | bytes 8388608 | tf_op jit(solution)/shard_map/all_to_all | solution.py:280
  165.4 4.6 %shard_map.157 = (bf16[2,2,256,512]{3,2,1,0:T(8,128)(2,1)}, bf16[2,2,256,512]{3,2,1,0:T(8,128)(2,1)}, bf16[2,2,256,512]{3,2,1,0:T(8,128)(2,1)}, bf16[2,2,256,512]{3,2,1,0:T(8,128)(2,1)}) custom-call(s32[24]{0:T(128)} %dynamic-slice_bitcast_fusion.refs_0_.order_ref, bf16[16,32,2048]{2,1,0:T(8,128)(2,1)} %copy-done, ...), custom_call_target="tpu_custom_call" | custom-call | tf_op jit(solution)/shard_map/pallas_call | solution.py:222
  170.0 7.3 %collective-permute-start.6 = (bf16[2,2,256,512]{3,2,1,0:T(8,128)(2,1)}, bf16[2,2,256,512]{3,2,1,0:T(8,128)(2,1)S(1)}, u32[]{:S(2)}, u32[]{:S(2)}) collective-permute-start(bf16[2,2,256,512]{3,2,1,0:T(8,128)(2,1)} %get-tuple-element.64), channel_id=1, source_target_pairs={{0,16},{16,32},{32,48},{48,0},{64,80},{80,96},{96,112},{112,64},{1... | collective-permute-start | bytes 3145736 | tf_op jit(solution)/shard_map/ppermute | solution.py:269
  177.3 8.0 %collective-permute-start.7 = (bf16[2,2,256,512]{3,2,1,0:T(8,128)(2,1)}, bf16[2,2,256,512]{3,2,1,0:T(8,128)(2,1)S(1)}, u32[]{:S(2)}, u32[]{:S(2)}) collective-permute-start(bf16[2,2,256,512]{3,2,1,0:T(8,128)(2,1)} %get-tuple-element.65), channel_id=1, source_target_pairs={{0,32},{16,48},{32,0},{48,16},{64,96},{80,112},{96,64},{112,80},{1... | collective-permute-start | bytes 3145736 | tf_op jit(solution)/shard_map/ppermute | solution.py:269
  185.3 0.0 collective-permute-start.8
  185.3 4.6 %shard_map.158 = (bf16[2,2,512,256]{3,2,1,0:T(8,128)(2,1)}, bf16[2,2,512,256]{3,2,1,0:T(8,128)(2,1)}, bf16[2,2,512,256]{3,2,1,0:T(8,128)(2,1)}, bf16[2,2,512,256]{3,2,1,0:T(8,128)(2,1)}) custom-call(s32[24]{0:T(128)} %dynamic-slice_bitcast_fusion.refs_0_.order_ref, bf16[16,32,2048]{2,1,0:T(8,128)(2,1)} %copy-done.1, ...), custom_call_target="tpu_custom_call" | custom-call | tf_op jit(solution)/shard_map/pallas_call | solution.py:222
  189.9 17.7 %collective-permute-done.6 = bf16[2,2,256,512]{3,2,1,0:T(8,128)(2,1)S(1)} collective-permute-done((bf16[2,2,256,512]{3,2,1,0:T(8,128)(2,1)}, bf16[2,2,256,512]{3,2,1,0:T(8,128)(2,1)S(1)}, u32[]{:S(2)}, u32[]{:S(2)}) %collective-permute-start.6) | collective-permute-done | bytes 1048608 | tf_op jit(solution)/shard_map/ppermute | solution.py:269
  207.6 23.6 %collective-permute-done.7 = bf16[2,2,256,512]{3,2,1,0:T(8,128)(2,1)S(1)} collective-permute-done((bf16[2,2,256,512]{3,2,1,0:T(8,128)(2,1)}, bf16[2,2,256,512]{3,2,1,0:T(8,128)(2,1)S(1)}, u32[]{:S(2)}, u32[]{:S(2)}) %collective-permute-start.7) | collective-permute-done | bytes 1048608 | tf_op jit(solution)/shard_map/ppermute | solution.py:269
  231.2 0.0 collective-permute-done.8
  231.2 0.1 collective-permute-start.14
  231.3 3.4 %collective-permute-start.15 = (bf16[2,2,512,256]{3,2,1,0:T(8,128)(2,1)}, bf16[2,2,512,256]{3,2,1,0:T(8,128)(2,1)}, u32[]{:S(2)}, u32[]{:S(2)}) collective-permute-start(bf16[2,2,512,256]{3,2,1,0:T(8,128)(2,1)} %get-tuple-element.84), channel_id=1, source_target_pairs={{0,32},{16,48},{32,0},{48,16},{64,96},{80,112},{96,64},{112,80},{1... | collective-permute-start | bytes 3145736 | tf_op jit(solution)/shard_map/ppermute | solution.py:269
  234.8 4.8 %shard_map.159 = (bf16[4,2,256,512]{3,2,1,0:T(8,128)(2,1)}, bf16[4,2,256,512]{3,2,1,0:T(8,128)(2,1)}) custom-call(s32[24]{0:T(128)} %dynamic-slice_bitcast_fusion.refs_0_.order_ref, bf16[16,32,2048]{2,1,0:T(8,128)(2,1)} %copy-done, bf16[2,256,512]{2,1,0:T(8,128)(2,1)} %get-tuple-element.59.ug_ref.act_ref), custom_call_target="tpu_custom_call" | custom-call | tf_op jit(solution)/shard_map/pallas_call | solution.py:222
  239.5 4.5 %collective-permute-start.10 = (bf16[4,2,256,512]{3,2,1,0:T(8,128)(2,1)}, bf16[4,2,256,512]{3,2,1,0:T(8,128)(2,1)}, u32[]{:S(2)}, u32[]{:S(2)}) collective-permute-start(bf16[4,2,256,512]{3,2,1,0:T(8,128)(2,1)} %get-tuple-element.71), channel_id=1, source_target_pairs={{0,64},{16,80},{32,96},{48,112},{64,0},{80,16},{96,32},{112,48},{1... | collective-permute-start | bytes 6291464 | tf_op jit(solution)/shard_map/ppermute | solution.py:276
  244.0 13.3 %collective-permute-done.14 = bf16[2,2,512,256]{3,2,1,0:T(8,128)(2,1)} collective-permute-done((bf16[2,2,512,256]{3,2,1,0:T(8,128)(2,1)}, bf16[2,2,512,256]{3,2,1,0:T(8,128)(2,1)}, u32[]{:S(2)}, u32[]{:S(2)}) %collective-permute-start.14) | collective-permute-done | bytes 1048608 | tf_op jit(solution)/shard_map/ppermute | solution.py:269
  257.3 23.3 %collective-permute-done.15 = bf16[2,2,512,256]{3,2,1,0:T(8,128)(2,1)} collective-permute-done((bf16[2,2,512,256]{3,2,1,0:T(8,128)(2,1)}, bf16[2,2,512,256]{3,2,1,0:T(8,128)(2,1)}, u32[]{:S(2)}, u32[]{:S(2)}) %collective-permute-start.15) | collective-permute-done | bytes 1048608 | tf_op jit(solution)/shard_map/ppermute | solution.py:269
  280.6 0.0 collective-permute-done.16
  280.6 2.7 convert_add_fusion
  283.4 0.9 fusion.5
  284.3 4.5 %collective-permute-start.17 = (bf16[2,512,256]{2,1,0:T(8,128)(2,1)}, bf16[2,512,256]{2,1,0:T(8,128)(2,1)}, u32[]{:S(2)}, u32[]{:S(2)}) collective-permute-start(bf16[2,512,256]{2,1,0:T(8,128)(2,1)} %fusion.5), channel_id=1, source_target_pairs={{0,64},{16,80},{32,96},{48,112},{64,0},{80,16},{96,32},{112,48},{1... | collective-permute-start | bytes 1572872 | tf_op jit(solution)/shard_map/ppermute | solution.py:276
  288.8 2.1 convert_add_fusion.1
  290.9 0.9 fusion.4
  291.7 0.0 collective-permute-start.9
  291.8 3.8 %pair_sum.1 = (f32[2,256,512]{2,1,0:T(8,128)}, bf16[2,256,512]{2,1,0:T(8,128)(2,1)}, bf16[2,256,512]{2,1,0:T(8,128)(2,1)}, bf16[2,256,512]{2,1,0:T(8,128)(2,1)}) custom-call(bf16[4,2,256,512]{3,2,1,0:T(8,128)(2,1)} %get-tuple-element.70.keep_ref, bf16[4,2,256,512]{3,2,1,0:T(8,128)(2,1)} %collective-permute-done.10.got_ref), custom_call_target="tpu_custom_call" | custom-call | tf_op jit(solution)/shard_map/pair_sum/pallas_call | solution.py:433
  295.6 0.9 collective-permute-start.11
  296.5 2.9 collective-permute-start.12
  299.4 0.2 collective-permute-start.13
  299.6 2.3 collective-permute-done.17
  301.9 2.3 fusion.1
  304.2 0.0 all-to-all-done.3.back_ref
  304.2 3.5 %ngrad.1 = bf16[128,2048]{1,0:T(8,128)(2,1)} custom-call(bf16[16,4,16,2048]{3,2,1,0:T(8,128)(2,1)} %all-to-all-done.3.back_ref, bf16[512,128]{1,0:T(8,128)(2,1)} %get-tuple-element.52.pick0_ref, bf16[512,128]{1,0:T(8,128)(2,1)} %get-tuple-element.53.pick1_ref), custom_call_target="tpu_custom_call" | custom-call | tf_op jit(solution)/shard_map/ngrad/pallas_call | solution.py:420
  307.7 3.9 %mixed.1 = bf16[128,2048]{1,0:T(8,128)(2,1)} custom-call(bf16[16,4,16,2048]{3,2,1,0:T(8,128)(2,1)} %all-to-all-done.3.back_ref, bf16[512,128]{1,0:T(8,128)(2,1)} %get-tuple-element.52.pick0_ref, bf16[512,128]{1,0:T(8,128)(2,1)} %get-tuple-element.53.pick1_ref, f32[128,2]{1,0:T(8,128)} %copy.17.gates_ref), custom_call_target="tpu_custom_call" | custom-call | tf_op jit(solution)/shard_map/mixed/pallas_call | solution.py:417
  311.6 0.5 collective-permute-done.9
  312.1 0.0 collective-permute-done.11
  312.1 10.4 %collective-permute-done.12 = bf16[2,256,512]{2,1,0:T(8,128)(2,1)} collective-permute-done((bf16[2,256,512]{2,1,0:T(8,128)(2,1)}, bf16[2,256,512]{2,1,0:T(8,128)(2,1)}, u32[]{:S(2)}, u32[]{:S(2)}) %collective-permute-start.12) | collective-permute-done | bytes 524320 | tf_op jit(solution)/shard_map/ppermute | solution.py:269
  322.5 2.9 fusion.3
  (22 shorter events, 0.0 us)
Async XLA Ops:
  0.6 35.0 %copy-start.8 = (f32[128,2]{0,1:T(2,128)S(1)}, f32[128,2]{0,1:T(2,128)}, u32[]{:S(2)}) copy-start(f32[128,2]{0,1:T(2,128)} %param.16) | copy-start | bytes 3076
  3.2 28.5 %collective-permute-start = (bf16[2,2048,128]{2,1,0:T(8,128)(2,1)}, bf16[2,2048,128]{2,1,0:T(8,128)(2,1)}, u32[]{:S(2)}, u32[]{:S(2)}) collective-permute-start(bf16[2,2048,128]{2,1,0:T(8,128)(2,1)} %get-tuple-element.87.kv), channel_id=1, source_target_pairs={{0,16},{16,32},{32,48},{48,0},{64,80},{80,96},{96,112},{1,17},{17,... | collective-permute-start | bytes 3145736 | tf_op jit(solution)/shard_map/ppermute | solution.py:269
  6.8 27.1 %collective-permute-start.2 = (bf16[2,2048,128]{2,1,0:T(8,128)(2,1)S(1)}, bf16[2,2048,128]{2,1,0:T(8,128)(2,1)S(1)}, u32[]{:S(2)}, u32[]{:S(2)}) collective-permute-start(bf16[2,2048,128]{2,1,0:T(8,128)(2,1)S(1)} %get-tuple-element.86), channel_id=1, source_target_pairs={{0,64},{16,80},{32,96},{48,112},{64,0},{80,16},{96,32},{112,48},{1... | collective-permute-start | bytes 3145736 | tf_op jit(solution)/shard_map/ppermute | solution.py:276
  10.8 42.6 %collective-permute-start.4 = (bf16[2,2048,128]{2,1,0:T(8,128)(2,1)}, bf16[2,2048,128]{2,1,0:T(8,128)(2,1)}, u32[]{:S(2)}, u32[]{:S(2)}) collective-permute-start(bf16[2,2048,128]{2,1,0:T(8,128)(2,1)} %get-tuple-element.87.kv), channel_id=1, source_target_pairs={{0,48},{64,112},{1,49},{65,113},{2,50},{66,114},{3,51},{67,115},{4... | collective-permute-start | bytes 3145736 | tf_op jit(solution)/shard_map/ppermute | solution.py:269
  31.7 31.6 %collective-permute-start.1 = (bf16[2,2048,128]{2,1,0:T(8,128)(2,1)}, bf16[2,2048,128]{2,1,0:T(8,128)(2,1)}, u32[]{:S(2)}, u32[]{:S(2)}) collective-permute-start(bf16[2,2048,128]{2,1,0:T(8,128)(2,1)} %collective-permute-done.refs_3_), channel_id=1, source_target_pairs={{0,16},{16,32},{32,48},{48,0},{80,96},{96,112},{1,17},{17,33},{33,... | collective-permute-start | bytes 3145736 | tf_op jit(solution)/shard_map/ppermute | solution.py:269
  33.9 6.3 %copy-start.2 = (bf16[2,2048,128]{2,1,0:T(8,128)(2,1)}, bf16[2,2048,128]{2,1,0:T(8,128)(2,1)S(1)}, u32[]{:S(2)}) copy-start(bf16[2,2048,128]{2,1,0:T(8,128)(2,1)S(1)} %collective-permute-done.2.refs_2_.refs_4_) | copy-start | bytes 3145732
  33.9 29.4 %collective-permute-start.3 = (bf16[2,2048,128]{2,1,0:T(8,128)(2,1)S(1)}, bf16[2,2048,128]{2,1,0:T(8,128)(2,1)}, u32[]{:S(2)}, u32[]{:S(2)}) collective-permute-start(bf16[2,2048,128]{2,1,0:T(8,128)(2,1)S(1)} %collective-permute-done.2.refs_2_.refs_4_), channel_id=1, source_target_pairs={{64,112},{80,64},{96,80},{112,96},{65,113},{81,65},{97,81},{113,97... | collective-permute-start | bytes 3145736 | tf_op jit(solution)/shard_map/ppermute | solution.py:269
  40.2 52.0 %all-to-all-start = ((bf16[16,32,2048]{2,1,0:T(8,128)(2,1)}), bf16[16,32,2048]{2,1,0:T(8,128)(2,1)S(1)}, u32[]{:S(2)}, u32[]{:S(2)}) async-start(bf16[16,32,2048]{2,1,0:T(8,128)(2,1)} %get-tuple-element.50), calls=%async_computation | async-start | bytes 4194304 | tf_op jit(solution)/shard_map/all_to_all | solution.py:280
  73.1 17.8 %collective-permute-start.5 = (bf16[2048,128]{1,0:T(8,128)(2,1)}, bf16[2048,128]{1,0:T(8,128)(2,1)S(1)}, u32[]{:S(2)}, u32[]{:S(2)}) collective-permute-start(bf16[2048,128]{1,0:T(8,128)(2,1)} %get-tuple-element.49), channel_id=1, source_target_pairs={{0,64},{16,80},{32,96},{48,112},{1,65},{17,81},{33,97},{49,113},{2... | collective-permute-start | bytes 1572872 | tf_op jit(solution)/shard_map/ppermute | solution.py:347
  92.2 19.2 %copy-start.1 = (bf16[16,32,2048]{2,1,0:T(8,128)(2,1)}, bf16[16,32,2048]{2,1,0:T(8,128)(2,1)S(1)}, u32[]{:S(2)}) copy-start(bf16[16,32,2048]{2,1,0:T(8,128)(2,1)S(1)} %all-to-all-done.grad_ref.src) | copy-start | bytes 6291460
  111.5 31.5 %all-to-all-start.2 = ((bf16[16,32,2048]{2,1,0:T(8,128)(2,1)}), bf16[16,32,2048]{2,1,0:T(8,128)(2,1)S(1)}, u32[]{:S(2)}, u32[]{:S(2)}) async-start(bf16[16,32,2048]{2,1,0:T(8,128)(2,1)} %get-tuple-element.55), calls=%async_computation.2 | async-start | bytes 4194304 | tf_op jit(solution)/shard_map/all_to_all | solution.py:280
  143.0 1.4 copy-start
  160.9 143.3 %all-to-all-start.3 = ((bf16[16,4,16,2048]{3,2,1,0:T(8,128)(2,1)}), bf16[16,4,16,2048]{3,2,1,0:T(8,128)(2,1)}, u32[]{:S(2)}, u32[]{:S(2)}) async-start(bf16[16,4,16,2048]{3,2,1,0:T(8,128)(2,1)} %expert_back.1), calls=%async_computation.3 | async-start | bytes 8388608 | tf_op jit(solution)/shard_map/all_to_all | solution.py:280
  170.0 37.6 %collective-permute-start.6 = (bf16[2,2,256,512]{3,2,1,0:T(8,128)(2,1)}, bf16[2,2,256,512]{3,2,1,0:T(8,128)(2,1)S(1)}, u32[]{:S(2)}, u32[]{:S(2)}) collective-permute-start(bf16[2,2,256,512]{3,2,1,0:T(8,128)(2,1)} %get-tuple-element.64), channel_id=1, source_target_pairs={{0,16},{16,32},{32,48},{48,0},{64,80},{80,96},{96,112},{112,64},{1... | collective-permute-start | bytes 3145736 | tf_op jit(solution)/shard_map/ppermute | solution.py:269
  177.3 53.9 %collective-permute-start.7 = (bf16[2,2,256,512]{3,2,1,0:T(8,128)(2,1)}, bf16[2,2,256,512]{3,2,1,0:T(8,128)(2,1)S(1)}, u32[]{:S(2)}, u32[]{:S(2)}) collective-permute-start(bf16[2,2,256,512]{3,2,1,0:T(8,128)(2,1)} %get-tuple-element.65), channel_id=1, source_target_pairs={{0,32},{16,48},{32,0},{48,16},{64,96},{80,112},{96,64},{112,80},{1... | collective-permute-start | bytes 3145736 | tf_op jit(solution)/shard_map/ppermute | solution.py:269
  185.3 45.9 %collective-permute-start.8 = (bf16[2,2,256,512]{3,2,1,0:T(8,128)(2,1)}, bf16[2,2,256,512]{3,2,1,0:T(8,128)(2,1)S(1)}, u32[]{:S(2)}, u32[]{:S(2)}) collective-permute-start(bf16[2,2,256,512]{3,2,1,0:T(8,128)(2,1)} %get-tuple-element.66), channel_id=1, source_target_pairs={{0,48},{16,0},{32,16},{48,32},{64,112},{80,64},{96,80},{112,96},{1... | collective-permute-start | bytes 3145736 | tf_op jit(solution)/shard_map/ppermute | solution.py:269
  231.2 52.1 %copy-start.6 = (bf16[2,2,256,512]{3,2,1,0:T(8,128)(2,1)}, bf16[2,2,256,512]{3,2,1,0:T(8,128)(2,1)S(1)}, u32[]{:S(2)}) copy-start(bf16[2,2,256,512]{3,2,1,0:T(8,128)(2,1)S(1)} %collective-permute-done.7) | copy-start | bytes 3145732
  231.2 52.1 %copy-start.7 = (bf16[2,2,256,512]{3,2,1,0:T(8,128)(2,1)}, bf16[2,2,256,512]{3,2,1,0:T(8,128)(2,1)S(1)}, u32[]{:S(2)}) copy-start(bf16[2,2,256,512]{3,2,1,0:T(8,128)(2,1)S(1)} %collective-permute-done.8) | copy-start | bytes 3145732
  231.2 26.1 %collective-permute-start.14 = (bf16[2,2,512,256]{3,2,1,0:T(8,128)(2,1)}, bf16[2,2,512,256]{3,2,1,0:T(8,128)(2,1)}, u32[]{:S(2)}, u32[]{:S(2)}) collective-permute-start(bf16[2,2,512,256]{3,2,1,0:T(8,128)(2,1)} %get-tuple-element.83), channel_id=1, source_target_pairs={{0,16},{16,32},{32,48},{48,0},{64,80},{80,96},{96,112},{112,64},{1... | collective-permute-start | bytes 3145736 | tf_op jit(solution)/shard_map/ppermute | solution.py:269
  231.3 49.3 %collective-permute-start.15 = (bf16[2,2,512,256]{3,2,1,0:T(8,128)(2,1)}, bf16[2,2,512,256]{3,2,1,0:T(8,128)(2,1)}, u32[]{:S(2)}, u32[]{:S(2)}) collective-permute-start(bf16[2,2,512,256]{3,2,1,0:T(8,128)(2,1)} %get-tuple-element.84), channel_id=1, source_target_pairs={{0,32},{16,48},{32,0},{48,16},{64,96},{80,112},{96,64},{112,80},{1... | collective-permute-start | bytes 3145736 | tf_op jit(solution)/shard_map/ppermute | solution.py:269
  234.8 45.8 %collective-permute-start.16 = (bf16[2,2,512,256]{3,2,1,0:T(8,128)(2,1)}, bf16[2,2,512,256]{3,2,1,0:T(8,128)(2,1)}, u32[]{:S(2)}, u32[]{:S(2)}) collective-permute-start(bf16[2,2,512,256]{3,2,1,0:T(8,128)(2,1)} %get-tuple-element.85), channel_id=1, source_target_pairs={{0,48},{16,0},{32,16},{48,32},{64,112},{80,64},{96,80},{112,96},{1... | collective-permute-start | bytes 3145736 | tf_op jit(solution)/shard_map/ppermute | solution.py:269
  239.5 52.2 %collective-permute-start.10 = (bf16[4,2,256,512]{3,2,1,0:T(8,128)(2,1)}, bf16[4,2,256,512]{3,2,1,0:T(8,128)(2,1)}, u32[]{:S(2)}, u32[]{:S(2)}) collective-permute-start(bf16[4,2,256,512]{3,2,1,0:T(8,128)(2,1)} %get-tuple-element.71), channel_id=1, source_target_pairs={{0,64},{16,80},{32,96},{48,112},{64,0},{80,16},{96,32},{112,48},{1... | collective-permute-start | bytes 6291464 | tf_op jit(solution)/shard_map/ppermute | solution.py:276
  280.6 8.2 %copy-start.5 = (bf16[2,2,256,512]{3,2,1,0:T(8,128)(2,1)S(1)}, bf16[2,2,256,512]{3,2,1,0:T(8,128)(2,1)}, u32[]{:S(2)}) copy-start(bf16[2,2,256,512]{3,2,1,0:T(8,128)(2,1)} %get-tuple-element.60) | copy-start | bytes 3145732
  283.4 7.5 %copy-start.3 = (f32[2,2,512,256]{3,2,1,0:T(8,128)}, f32[2,2,512,256]{3,2,1,0:T(8,128)S(1)}, u32[]{:S(2)}) copy-start(f32[2,2,512,256]{3,2,1,0:T(8,128)S(1)} %convert_add_fusion) | copy-start | bytes 6291460
  284.3 17.6 %collective-permute-start.17 = (bf16[2,512,256]{2,1,0:T(8,128)(2,1)}, bf16[2,512,256]{2,1,0:T(8,128)(2,1)}, u32[]{:S(2)}, u32[]{:S(2)}) collective-permute-start(bf16[2,512,256]{2,1,0:T(8,128)(2,1)} %fusion.5), channel_id=1, source_target_pairs={{0,64},{16,80},{32,96},{48,112},{64,0},{80,16},{96,32},{112,48},{1... | collective-permute-start | bytes 1572872 | tf_op jit(solution)/shard_map/ppermute | solution.py:276
  291.7 20.3 %collective-permute-start.9 = (bf16[2,256,512]{2,1,0:T(8,128)(2,1)}, bf16[2,256,512]{2,1,0:T(8,128)(2,1)}, u32[]{:S(2)}, u32[]{:S(2)}) collective-permute-start(bf16[2,256,512]{2,1,0:T(8,128)(2,1)} %fusion.4), channel_id=1, source_target_pairs={{0,64},{16,80},{32,96},{48,112},{64,0},{80,16},{96,32},{112,48},{1... | collective-permute-start | bytes 1572872 | tf_op jit(solution)/shard_map/ppermute | solution.py:276
  295.6 16.5 %collective-permute-start.11 = (bf16[2,256,512]{2,1,0:T(8,128)(2,1)}, bf16[2,256,512]{2,1,0:T(8,128)(2,1)}, u32[]{:S(2)}, u32[]{:S(2)}) collective-permute-start(bf16[2,256,512]{2,1,0:T(8,128)(2,1)} %get-tuple-element.72), channel_id=1, source_target_pairs={{0,16},{16,32},{32,48},{48,0},{64,80},{80,96},{96,112},{112,64},{1... | collective-permute-start | bytes 1572872 | tf_op jit(solution)/shard_map/ppermute | solution.py:269
  296.5 26.0 %collective-permute-start.12 = (bf16[2,256,512]{2,1,0:T(8,128)(2,1)}, bf16[2,256,512]{2,1,0:T(8,128)(2,1)}, u32[]{:S(2)}, u32[]{:S(2)}) collective-permute-start(bf16[2,256,512]{2,1,0:T(8,128)(2,1)} %get-tuple-element.73), channel_id=1, source_target_pairs={{0,32},{16,48},{32,0},{48,16},{64,96},{80,112},{96,64},{112,80},{1... | collective-permute-start | bytes 1572872 | tf_op jit(solution)/shard_map/ppermute | solution.py:269
  299.4 23.1 %collective-permute-start.13 = (bf16[2,256,512]{2,1,0:T(8,128)(2,1)}, bf16[2,256,512]{2,1,0:T(8,128)(2,1)}, u32[]{:S(2)}, u32[]{:S(2)}) collective-permute-start(bf16[2,256,512]{2,1,0:T(8,128)(2,1)} %get-tuple-element.74), channel_id=1, source_target_pairs={{0,48},{16,0},{32,16},{48,32},{64,112},{80,64},{96,80},{112,96},{1... | collective-permute-start | bytes 1572872 | tf_op jit(solution)/shard_map/ppermute | solution.py:269
  307.7 14.8 %copy-start.4 = (f32[2,256,512]{2,1,0:T(8,128)S(1)}, f32[2,256,512]{2,1,0:T(8,128)}, u32[]{:S(2)}) copy-start(f32[2,256,512]{2,1,0:T(8,128)} %get-tuple-element.78) | copy-start | bytes 3145732

commit v3 on v2

--- a/solution.py
+++ b/solution.py
@@ -208,23 +208,35 @@
     piece = (hid, cols) if turned else (cols, hid)
 
     def kernel(order_ref, src, act_ref, *outs):
-        for e in range(2):
-            side = act_ref[e].T if turned else act_ref[e]
-            done = 0
-            for out, count in zip(outs, groups):
-                for n in range(count):
-                    at = pl.ds(pl.multiple_of(order_ref[offset + done] * cols, cols), cols)
+        sides = [act_ref[e].T if turned else act_ref[e] for e in range(2)]
+        for out, (first, count, experts) in zip(outs, groups):
+            for n in range(count):
+                owner = order_ref[offset + first + n]
+                at = pl.ds(pl.multiple_of(owner * cols, cols), cols)
+                for m, e in enumerate(experts):
                     rows = src[:, e * CAP : (e + 1) * CAP, at].reshape(ROWS, cols)
+                    side = sides[e]
                     grad = mm(side, rows, 1, 0) if turned else mm(rows, side, 0, 0)
-                    out[n, e] = grad.astype(BF16)
-                    done += 1
+                    out[n, m] = grad.astype(BF16)
 
     return pl.pallas_call(
         kernel,
-        out_shape=tuple(jax.ShapeDtypeStruct((c, 2, *piece), BF16) for c in groups),
+        out_shape=tuple(jax.ShapeDtypeStruct((c, len(x), *piece), BF16) for _, c, x in groups),
         in_specs=[smem(), vmem(), vmem()],
         out_specs=(vmem(),) * len(groups),
     )(table, source, act)
+
+
+def relay_kernel(near1_ref, far1_ref, near3_ref, far3_ref, out1_ref, out3_ref):
+    out1_ref[...] = (near1_ref[...].astype(F32) + far1_ref[...].astype(F32)).astype(BF16)
+    out3_ref[...] = (near3_ref[...].astype(F32) + far3_ref[...].astype(F32)).astype(BF16)
+
+
+def row_sum_kernel(own_ref, a1_ref, a3_ref, b1_ref, b3_ref, keep_ref, send_ref):
+    for e, (one, three) in enumerate(((a1_ref, a3_ref), (b1_ref, b3_ref))):
+        for n, out in enumerate((keep_ref, send_ref)):
+            total = own_ref[n, e].astype(F32) + one[n, 0].astype(F32) + three[n, 0].astype(F32)
+            out[e] = total.astype(out.dtype)
 
 
 def expert_back_kernel(hidden_ref, down_ref, gg_ref, ug_ref, gate_ref, up_ref, out_ref):
@@ -276,10 +288,32 @@
     return lax.ppermute(value, "ctx", pairs)
 
 
+def along_row(pieces):
+    one_a, one_b, two_a, two_b, three_a, three_b, _ = pieces
+    far1 = move_y(two_a, 1)
+    far3 = move_y(two_b, 3)
+    b1 = move_y(one_b, 1)
+    a3 = move_y(three_a, 3)
+    both1, both3 = pl.pallas_call(
+        relay_kernel,
+        out_shape=(
+            jax.ShapeDtypeStruct(one_a.shape, BF16),
+            jax.ShapeDtypeStruct(one_a.shape, BF16),
+        ),
+        in_specs=[vmem()] * 4,
+        out_specs=(vmem(),) * 2,
+        name="relay",
+    )(one_a, far1, three_b, far3)
+    a1 = move_y(both1, 1)
+    b3 = move_y(both3, 3)
+    return a1, a3, b1, b3
+
+
 def exchange(value):
     return lax.all_to_all(value, "exp", split_axis=0, concat_axis=0, tiled=True)
 
 
+ROW_GROUPS = tuple((n, 2, (e,)) for n in (0, 2, 4) for e in (0, 1)) + ((6, 2, (0, 1)),)
 AT_NEAR, AT_FAR, AT_REST, AT_Y, AT_X = 0, 4, 6, 8, 16
 
 
@@ -381,19 +415,22 @@
         name="expert_in",
     )(recv_inputs, hidden_grad, w_gate, w_up)
 
-    ga = weight_grad(table, AT_Y, recv_inputs, gate_grad, (2, 2, 2, 2), False)
-    got_g = []
+    ga = weight_grad(table, AT_Y, recv_inputs, gate_grad, ROW_GROUPS, False)
+    got_g = along_row(ga)
+    up_send, up_keep, *ua = weight_grad(
+        table,
+        0,
+        recv_inputs,
+        up_grad,
+        ((AT_X, 4, (0,)), (AT_X + 4, 4, (0,))) + tuple((AT_Y + n, 2, (1,)) for n in (0, 2, 4, 6)),
+        False,
+    )
+    up_got = move_x(up_send)
+    do = weight_grad(table, AT_Y, recv_grads, hidden, ROW_GROUPS, True)
+    got_d = along_row(do)
+    got_a = []
     for n in range(3):
-        got_g.append(move_y(ga[n], n + 1))
-    up_send, up_keep = weight_grad(table, AT_X, recv_inputs, up_grad, (4, 4), False)
-    up_got = move_x(up_send)
-    do = weight_grad(table, AT_Y, recv_grads, hidden, (2, 2, 2, 2), True)
-    held = lax.optimization_barrier((*do[:3], *got_g))
-    got_g = held[3:]
-    got_d = []
-    for n in range(3):
-        got_d.append(move_y(held[n], n + 1))
-
+        got_a.append(move_y(ua[n], n + 1))
     early = lambda shape: pl.BlockSpec((1, *shape), lambda n: (jnp.minimum(n, 1), 0, 0))
     late = lambda shape: pl.BlockSpec((1, *shape), lambda n: (jnp.maximum(n - 2, 0), 0, 0))
     expert_back = pl.pallas_call(
@@ -424,11 +461,19 @@
     wide = lambda v: v.astype(F32)
 
     def over_row(own, got):
-        sums = wide(own) + wide(got[0]) + wide(got[1]) + wide(got[2])
-        return sums[0], sums[1].astype(BF16)
-
-    gate_part, gate_send = over_row(ga[3], got_g)
+        shape = own.shape[1:]
+        return pl.pallas_call(
+            row_sum_kernel,
+            out_shape=(full(shape, F32), full(shape, BF16)),
+            in_specs=[vmem()] * 5,
+            out_specs=(vmem(),) * 2,
+            name="row_sum",
+        )(own, *got)
+
+    gate_part, gate_send = over_row(ga[6], got_g)
     gate_got = move_x(gate_send)
+    sums = wide(ua[3]) + wide(got_a[0]) + wide(got_a[1]) + wide(got_a[2])
+    got_ax = move_x(sums[1].astype(BF16))
     quarter = up_keep.shape[1:]
     up_part, *up_rest = pl.pallas_call(
         pair_sum_kernel,
@@ -444,8 +489,10 @@
         (mixed, normed_grad, gate_got, *got_u)
     )
     gate_sum = (gate_part + wide(gate_got)).astype(BF16)
-    up_sum = (up_part + wide(got_u[0]) + wide(got_u[1]) + wide(got_u[2])).astype(BF16)
-    down_part, down_send = over_row(do[3], got_d)
+    up_first = (up_part + wide(got_u[0]) + wide(got_u[1]) + wide(got_u[2])).astype(BF16)
+    up_last = (sums[0] + wide(got_ax)).astype(BF16)
+    up_sum = jnp.concatenate([up_first, up_last])
+    down_part, down_send = over_row(do[6], got_d)
     down_got = move_x(down_send)
     down_sum = (down_part + wide(down_got)).astype(BF16)
     return (normed, mixed, normed_grad, gate_sum, up_sum, down_sum)

time: 327 us -> 310 us (0.948)
  waiting for transfers between devices: 142 us -> 104 us
  starting transfers between devices: 66.4 us -> 79.4 us
  Pallas kernels: 81.9 us -> 91.6 us
    ppermute x13 -> x22, waiting for transfers between devices: 107 us -> 49.8 us  [move_y(): return lax.ppermute(value, 'ctx', pairs)]
    ppermute x4 -> x5, waiting for transfers between devices: 2.76 us -> 21.2 us  [move_x(): return lax.ppermute(value, 'ctx', pairs)]
    pallas_call x3 -> x7, Pallas kernels: 13.9 us -> 24.6 us  [the longest x3 12.8 us: weight_grad(): pl.pallas_call(kernel, out_shape=tuple((jax.ShapeDtypeStruct((c, len(x),...]
    ppermute x13 -> x22, starting transfers between devices: 33.1 us -> 43.4 us  [move_y(): return lax.ppermute(value, 'ctx', pairs)]
    ppermute x4 -> x5, starting transfers between devices: 13 us -> 17.1 us  [move_x(): return lax.ppermute(value, 'ctx', pairs)]
  transfers between devices with their start and end apart: 21 -> 31, of which waited for: 10 -> 13; matrix products, arithmetic and copies ran while one was open for 4% -> 3% of each run, Pallas kernels for 19% -> 23%
where the time goes in v3:
time: 310 us; the launch traced here: 308 us
  waiting for transfers between devices  104 us (34%)
  Pallas kernels  91.6 us (30%)
  starting transfers between devices  79.4 us (26%)
  blocking collectives  15.6 us (5%)
  other arithmetic  11.6 us (4%)
  local copies, waits for them, and re-layouts  5.85 us (2%)
    ppermute x22, waiting for transfers between devices, move_y(): return lax.ppermute(value, 'ctx', pairs)  49.8 us
    ppermute x22, starting transfers between devices, move_y(): return lax.ppermute(value, 'ctx', pairs)  43.4 us
    all_to_all x3, waiting for transfers between devices, exchange(): return lax.all_to_all(value, 'exp', split_axis=0, concat_axis=0, tiled=True)  23.3 us
    pallas_call x3, Pallas kernels, attend(): pl.pallas_call(kernel, out_shape=tuple((jax.ShapeDtypeStruct((rows, HEAD_...  22.6 us
    ppermute x5, waiting for transfers between devices, move_x(): return lax.ppermute(value, 'ctx', pairs)  21.2 us
    ppermute x5, starting transfers between devices, move_x(): return lax.ppermute(value, 'ctx', pairs)  17.1 us
    all_to_all x1, blocking collectives, exchange(): return lax.all_to_all(value, 'exp', split_axis=0, concat_axis=0, tiled=True)  15.6 us
    all_to_all x3, starting transfers between devices, exchange(): return lax.all_to_all(value, 'exp', split_axis=0, concat_axis=0, tiled=True)  13.7 us
  transfers between devices with their start and end apart: 31, of which 13 were waited for; matrix products, arithmetic and copies ran while one was open for 3% of the time, Pallas kernels for 23%

profile of v3, /device:TPU:0, one launch (start us, length us, event | category | flops | bytes accessed | tf_op | source)
XLA Modules:
  0.0 308.4 jit_solution(16244319877167145106)
XLA Ops:
  0.6 2.6 broadcast_select_fusion
  3.2 3.1 %collective-permute-start.2 = (bf16[2,2048,128]{2,1,0:T(8,128)(2,1)S(1)}, bf16[2,2048,128]{2,1,0:T(8,128)(2,1)S(1)}, u32[]{:S(2)}, u32[]{:S(2)}) collective-permute-start(bf16[2,2048,128]{2,1,0:T(8,128)(2,1)S(1)} %get-tuple-element.110), channel_id=1, source_target_pairs={{0,64},{16,80},{32,96},{48,112},{64,0},{80,16},{96,32},{112,48},{1... | collective-permute-start | bytes 3145736 | tf_op jit(solution)/shard_map/ppermute | solution.py:288
  6.4 3.5 %collective-permute-start = (bf16[2,2048,128]{2,1,0:T(8,128)(2,1)}, bf16[2,2048,128]{2,1,0:T(8,128)(2,1)}, u32[]{:S(2)}, u32[]{:S(2)}) collective-permute-start(bf16[2,2048,128]{2,1,0:T(8,128)(2,1)} %get-tuple-element.111.kv), channel_id=1, source_target_pairs={{0,16},{16,32},{32,48},{48,0},{64,80},{80,96},{96,112},{1,17},{17,... | collective-permute-start | bytes 3145736 | tf_op jit(solution)/shard_map/ppermute | solution.py:281
  9.8 4.5 %collective-permute-start.4 = (bf16[2,2048,128]{2,1,0:T(8,128)(2,1)}, bf16[2,2048,128]{2,1,0:T(8,128)(2,1)}, u32[]{:S(2)}, u32[]{:S(2)}) collective-permute-start(bf16[2,2048,128]{2,1,0:T(8,128)(2,1)} %get-tuple-element.111.kv), channel_id=1, source_target_pairs={{0,48},{64,112},{1,49},{65,113},{2,50},{66,114},{3,51},{67,115},{4... | collective-permute-start | bytes 3145736 | tf_op jit(solution)/shard_map/ppermute | solution.py:281
  14.4 15.1 %collective-permute-done.2.refs_2_.refs_4_ = bf16[2,2048,128]{2,1,0:T(8,128)(2,1)S(1)} collective-permute-done((bf16[2,2048,128]{2,1,0:T(8,128)(2,1)S(1)}, bf16[2,2048,128]{2,1,0:T(8,128)(2,1)S(1)}, u32[]{:S(2)}, u32[]{:S(2)}) %collective-permute-start.2) | collective-permute-done | bytes 1048608 | tf_op jit(solution)/shard_map/ppermute | solution.py:288
  29.5 1.6 collective-permute-start.3
  31.2 3.3 %collective-permute-done.refs_3_ = bf16[2,2048,128]{2,1,0:T(8,128)(2,1)} collective-permute-done((bf16[2,2048,128]{2,1,0:T(8,128)(2,1)}, bf16[2,2048,128]{2,1,0:T(8,128)(2,1)}, u32[]{:S(2)}, u32[]{:S(2)}) %collective-permute-start) | collective-permute-done | bytes 1048608 | tf_op jit(solution)/shard_map/ppermute | solution.py:281
  34.5 2.2 collective-permute-start.1
  36.7 1.4 copy.17.gates_ref
  38.1 3.9 %route.1 = (bf16[512,128]{1,0:T(8,128)(2,1)}, bf16[512,128]{1,0:T(8,128)(2,1)}, bf16[16,32,2048]{2,1,0:T(8,128)(2,1)}) custom-call(s32[2,128]{1,0:T(2,128)} %bitcast.17, f32[128,2]{1,0:T(8,128)} %copy.17.gates_ref, bf16[128,2048]{1,0:T(8,128)(2,1)} %grad_ref.1), custom_call_target="tpu_custom_call" | custom-call | tf_op jit(solution)/shard_map/route/pallas_call | solution.py:349
  41.9 5.5 %all-to-all-start = ((bf16[16,32,2048]{2,1,0:T(8,128)(2,1)}), bf16[16,32,2048]{2,1,0:T(8,128)(2,1)S(1)}, u32[]{:S(2)}, u32[]{:S(2)}) async-start(bf16[16,32,2048]{2,1,0:T(8,128)(2,1)} %get-tuple-element.62), calls=%async_computation | async-start | bytes 4194304 | tf_op jit(solution)/shard_map/all_to_all | solution.py:313
  47.4 5.6 %attend_own.1.refs_6_ = f32[2048,128]{1,0:T(8,128)} custom-call(bf16[2048,128]{1,0:T(8,128)(2,1)} %refs_1_.5, bf16[2,2048,128]{2,1,0:T(8,128)(2,1)} %get-tuple-element.111.kv), custom_call_target="tpu_custom_call" | custom-call | tf_op jit(solution)/shard_map/attend_own/pallas_call | solution.py:80
  53.0 1.2 dynamic-slice_bitcast_fusion.refs_0_.order_ref
  54.3 10.0 %shard_map.154 = (f32[2048,128]{1,0:T(8,128)}, f32[2048,128]{1,0:T(8,128)}) custom-call(s32[24]{0:T(128)} %dynamic-slice_bitcast_fusion.refs_0_.order_ref, bf16[2048,128]{1,0:T(8,128)(2,1)} %refs_1_.5, bf16[2,2048,128]{2,1,0:T(8,128)(2,1)} %copy-done.2, bf16[2,2048,128]{2,1,0:T(8,128)(2,1)} %collective-permute-done.refs_3_, bf16[2,2048,128]{2,1,0:T(8,128)(2,1)} %copy-done.2, ...), custom_call_target="tpu_custom_call" | custom-call | tf_op jit(solution)/shard_map/pallas_call | solution.py:131
  64.2 9.7 %shard_map.155 = (f32[2048,128]{1,0:T(8,128)}, bf16[2048,128]{1,0:T(8,128)(2,1)}) custom-call(s32[24]{0:T(128)} %dynamic-slice_bitcast_fusion.refs_0_.order_ref, bf16[2048,128]{1,0:T(8,128)(2,1)} %refs_1_.5, bf16[2,2048,128]{2,1,0:T(8,128)(2,1)} %copy-done.2, bf16[2,2048,128]{2,1,0:T(8,128)(2,1)} %collective-permute-done.1.refs_3_.refs_2_, ...), custom_call_target="tpu_custom_call" | custom-call | tf_op jit(solution)/shard_map/pallas_call | solution.py:131
  74.0 5.2 %collective-permute-start.5 = (bf16[2048,128]{1,0:T(8,128)(2,1)}, bf16[2048,128]{1,0:T(8,128)(2,1)S(1)}, u32[]{:S(2)}, u32[]{:S(2)}) collective-permute-start(bf16[2048,128]{1,0:T(8,128)(2,1)} %get-tuple-element.61), channel_id=1, source_target_pairs={{0,64},{16,80},{32,96},{48,112},{1,65},{17,81},{33,97},{49,113},{2... | collective-permute-start | bytes 1572872 | tf_op jit(solution)/shard_map/ppermute | solution.py:381
  79.2 2.9 shard_map.156
  82.0 9.1 %collective-permute-done.5 = bf16[2048,128]{1,0:T(8,128)(2,1)S(1)} collective-permute-done((bf16[2048,128]{1,0:T(8,128)(2,1)}, bf16[2048,128]{1,0:T(8,128)(2,1)S(1)}, u32[]{:S(2)}, u32[]{:S(2)}) %collective-permute-start.5) | collective-permute-done | bytes 524320 | tf_op jit(solution)/shard_map/ppermute | solution.py:381
  91.2 1.3 add_convert_fusion.2
  92.5 15.6 %all_to_all.20.tok_ref = bf16[16,128,128]{2,1,0:T(8,128)(2,1)} all-to-all(bf16[16,128,128]{2,1,0:T(8,128)(2,1)S(1)} %bitcast.14), channel_id=1, replica_groups=mesh['ctx'=8,'exp'=16] {'exp'}, dimensions={0} | all-to-all | bytes 1048576 | tf_op jit(solution)/shard_map/all_to_all | solution.py:313
  108.1 3.7 %norm.1 = (bf16[128,2048]{1,0:T(8,128)(2,1)}, bf16[16,32,2048]{2,1,0:T(8,128)(2,1)}) custom-call(bf16[16,128,128]{2,1,0:T(8,128)(2,1)} %all_to_all.20.tok_ref, bf16[128,2048]{1,0:T(8,128)(2,1)} %gate_ref.3, bf16[512,128]{1,0:T(8,128)(2,1)} %get-tuple-element.64.pick0_ref, bf16[512,128]{1,0:T(8,128)(2,1)} %get-tuple-element.65.pick1_ref), custom_call_target="tpu_custom_call" | custom-call | tf_op jit(solution)/shard_map/norm/pallas_call | solution.py:399
  111.8 3.7 %all-to-all-start.2 = ((bf16[16,32,2048]{2,1,0:T(8,128)(2,1)}), bf16[16,32,2048]{2,1,0:T(8,128)(2,1)S(1)}, u32[]{:S(2)}, u32[]{:S(2)}) async-start(bf16[16,32,2048]{2,1,0:T(8,128)(2,1)} %get-tuple-element.67), calls=%async_computation.2 | async-start | bytes 4194304 | tf_op jit(solution)/shard_map/all_to_all | solution.py:313
  115.5 4.5 %hidden_grad.1.hg_ref = f32[2,256,512]{2,1,0:T(8,128)} custom-call(bf16[16,32,2048]{2,1,0:T(8,128)(2,1)} %copy-done.1, bf16[2,512,2048]{2,1,0:T(8,128)(2,1)} %down_ref.3), custom_call_target="tpu_custom_call" | custom-call | tf_op jit(solution)/shard_map/hidden_grad/pallas_call | solution.py:391
  119.9 23.3 %all-to-all-done.2.in_ref.src = bf16[16,32,2048]{2,1,0:T(8,128)(2,1)S(1)} async-done(((bf16[16,32,2048]{2,1,0:T(8,128)(2,1)}), bf16[16,32,2048]{2,1,0:T(8,128)(2,1)S(1)}, u32[]{:S(2)}, u32[]{:S(2)}) %all-to-all-start.2) | async-done | bytes 2097184 | tf_op jit(solution)/shard_map/all_to_all | solution.py:313
  143.3 1.3 copy-done
  144.6 6.6 %expert_in.1 = (bf16[2,256,512]{2,1,0:T(8,128)(2,1)}, bf16[2,256,512]{2,1,0:T(8,128)(2,1)}, bf16[2,256,512]{2,1,0:T(8,128)(2,1)}) custom-call(bf16[16,32,2048]{2,1,0:T(8,128)(2,1)} %copy-done, f32[2,256,512]{2,1,0:T(8,128)} %hidden_grad.1.hg_ref, bf16[2,2048,512]{2,1,0:T(8,128)(2,1)} %gate_ref.5, bf16[2,2048,512]{2,1,0:T(8,128)(2,1)} %up_ref.3), custom_call_target="tpu_custom_call" | custom-call | tf_op jit(solution)/shard_map/expert_in/pallas_call | solution.py:409
  151.1 10.1 %expert_back.1 = bf16[16,4,16,2048]{3,2,1,0:T(8,128)(2,1)} custom-call(bf16[2,256,512]{2,1,0:T(8,128)(2,1)} %get-tuple-element.69.hidden_ref.act_ref, bf16[2,512,2048]{2,1,0:T(8,128)(2,1)} %down_ref.3, bf16[2,256,512]{2,1,0:T(8,128)(2,1)} %get-tuple-element.70.gg_ref.act_ref, bf16[2,256,512]{2,1,0:T(8,128)(2,1)} %get-tuple-element.71.ug_ref.act_ref, ...), custom_call_target="tpu_custom_call" | custom-call | tf_op jit(solution)/shard_map/expert_back/pallas_call | solution.py:436
  161.2 4.6 %all-to-all-start.3 = ((bf16[16,4,16,2048]{3,2,1,0:T(8,128)(2,1)}), bf16[16,4,16,2048]{3,2,1,0:T(8,128)(2,1)}, u32[]{:S(2)}, u32[]{:S(2)}) async-start(bf16[16,4,16,2048]{3,2,1,0:T(8,128)(2,1)} %expert_back.1), calls=%async_computation.3 | async-start | bytes 8388608 | tf_op jit(solution)/shard_map/all_to_all | solution.py:313
  165.8 4.2 %shard_map.159 = (bf16[2,1,512,256]{3,2,1,0:T(8,128)(2,1)}, bf16[2,1,512,256]{3,2,1,0:T(8,128)(2,1)}, bf16[2,1,512,256]{3,2,1,0:T(8,128)(2,1)}, bf16[2,1,512,256...) custom-call(s32[24]{0:T(128)} %dynamic-slice_bitcast_fusion.refs_0_., ...), custom_call_target="tpu_custom_call" | custom-call | tf_op jit(solution)/shard_map/pallas_call | solution.py:222
  170.0 7.4 %collective-permute-start.21 = (bf16[2,1,512,256]{3,2,1,0:T(8,128)(2,1)}, bf16[2,1,512,256]{3,2,1,0:T(8,128)(2,1)S(1)}, u32[]{:S(2)}, u32[]{:S(2)}) collective-permute-start(bf16[2,1,512,256]{3,2,1,0:T(8,128)(2,1)} %get-tuple-element.101), channel_id=1, source_target_pairs={{0,16},{16,32},{32,48},{48,0},{64,80},{80,96},{96,112},{112,64},{1... | collective-permute-start | bytes 1572872 | tf_op jit(solution)/shard_map/ppermute | solution.py:281
  177.4 4.2 %collective-permute-start.22 = (bf16[2,1,512,256]{3,2,1,0:T(8,128)(2,1)}, bf16[2,1,512,256]{3,2,1,0:T(8,128)(2,1)S(1)}, u32[]{:S(2)}, u32[]{:S(2)}) collective-permute-start(bf16[2,1,512,256]{3,2,1,0:T(8,128)(2,1)} %get-tuple-element.103), channel_id=1, source_target_pairs={{0,48},{16,0},{32,16},{48,32},{64,112},{80,64},{96,80},{112,96},{1... | collective-permute-start | bytes 1572872 | tf_op jit(solution)/shard_map/ppermute | solution.py:281
  181.6 2.0 collective-permute-start.24
  183.6 4.3 %shard_map.157 = (bf16[2,1,256,512]{3,2,1,0:T(8,128)(2,1)}, bf16[2,1,256,512]{3,2,1,0:T(8,128)(2,1)}, bf16[2,1,256,512]{3,2,1,0:T(8,128)(2,1)}, bf16[2,1,256,512...) custom-call(s32[24]{0:T(128)} %dynamic-slice_bitcast_fusion.refs_0_., ...), custom_call_target="tpu_custom_call" | custom-call | tf_op jit(solution)/shard_map/pallas_call | solution.py:222
  187.9 6.6 %collective-permute-done.21.far1_ref = bf16[2,1,512,256]{3,2,1,0:T(8,128)(2,1)S(1)} collective-permute-done((bf16[2,1,512,256]{3,2,1,0:T(8,128)(2,1)}, bf16[2,1,512,256]{3,2,1,0:T(8,128)(2,1)S(1)}, u32[]{:S(2)}, u32[]{:S(2)}) %collective-permute-start.21) | collective-permute-done | bytes 524320 | tf_op jit(solution)/shard_map/ppermute | solution.py:281
  194.6 2.0 collective-permute-start.7
  196.6 4.3 %shard_map.158 = (bf16[4,1,256,512]{3,2,1,0:T(8,128)(2,1)}, bf16[4,1,256,512]{3,2,1,0:T(8,128)(2,1)}, bf16[2,1,256,512]{3,2,1,0:T(8,128)(2,1)}, bf16[2,1,256,512...) custom-call(s32[24]{0:T(128)} %dynamic-slice_bitcast_fusion.refs_0_.order_ref, ...), custom_call_target="tpu_custom_call" | custom-call | tf_op jit(solution)/shard_map/pallas_call | solution.py:222
  201.7 2.6 relay.3
  204.3 1.2 collective-permute-done.24.a3_ref
  205.5 3.8 %collective-permute-start.18 = (bf16[2,1,256,512]{3,2,1,0:T(8,128)(2,1)}, bf16[2,1,256,512]{3,2,1,0:T(8,128)(2,1)S(1)}, u32[]{:S(2)}, u32[]{:S(2)}) collective-permute-start(bf16[2,1,256,512]{3,2,1,0:T(8,128)(2,1)} %get-tuple-element.97), channel_id=1, source_target_pairs={{0,32},{16,48},{32,0},{48,16},{64,96},{80,112},{96,64},{112,80},{1... | collective-permute-start | bytes 1572872 | tf_op jit(solution)/shard_map/ppermute | solution.py:281
  209.9 7.1 %collective-permute-done.6.far1_ref = bf16[2,1,256,512]{3,2,1,0:T(8,128)(2,1)S(1)} collective-permute-done((bf16[2,1,256,512]{3,2,1,0:T(8,128)(2,1)}, bf16[2,1,256,512]{3,2,1,0:T(8,128)(2,1)S(1)}, u32[]{:S(2)}, u32[]{:S(2)}) %collective-permute-start.6) | collective-permute-done | bytes 524320 | tf_op jit(solution)/shard_map/ppermute | solution.py:281
  217.1 10.9 %collective-permute-done.7.far3_ref = bf16[2,1,256,512]{3,2,1,0:T(8,128)(2,1)S(1)} collective-permute-done((bf16[2,1,256,512]{3,2,1,0:T(8,128)(2,1)}, bf16[2,1,256,512]{3,2,1,0:T(8,128)(2,1)S(1)}, u32[]{:S(2)}, u32[]{:S(2)}) %collective-permute-start.7) | collective-permute-done | bytes 524320 | tf_op jit(solution)/shard_map/ppermute | solution.py:281
  227.9 3.6 %collective-permute-start.26 = (bf16[2,1,512,256]{3,2,1,0:T(8,128)(2,1)}, bf16[2,1,512,256]{3,2,1,0:T(8,128)(2,1)}, u32[]{:S(2)}, u32[]{:S(2)}) collective-permute-start(bf16[2,1,512,256]{3,2,1,0:T(8,128)(2,1)} %get-tuple-element.107), channel_id=1, source_target_pairs={{0,48},{16,0},{32,16},{48,32},{64,112},{80,64},{96,80},{112,96},{1... | collective-permute-start | bytes 1572872 | tf_op jit(solution)/shard_map/ppermute | solution.py:281
  231.6 2.7 relay.2
  234.4 6.7 %collective-permute-done.18 = bf16[2,1,256,512]{3,2,1,0:T(8,128)(2,1)S(1)} collective-permute-done((bf16[2,1,256,512]{3,2,1,0:T(8,128)(2,1)}, bf16[2,1,256,512]{3,2,1,0:T(8,128)(2,1)S(1)}, u32[]{:S(2)}, u32[]{:S(2)}) %collective-permute-start.18) | collective-permute-done | bytes 524320 | tf_op jit(solution)/shard_map/ppermute | solution.py:281
  241.1 4.6 %collective-permute-start.13 = (bf16[4,1,256,512]{3,2,1,0:T(8,128)(2,1)}, bf16[4,1,256,512]{3,2,1,0:T(8,128)(2,1)S(1)}, u32[]{:S(2)}, u32[]{:S(2)}) collective-permute-start(bf16[4,1,256,512]{3,2,1,0:T(8,128)(2,1)} %get-tuple-element.83), channel_id=1, source_target_pairs={{0,64},{16,80},{32,96},{48,112},{64,0},{80,16},{96,32},{112,48},{1... | collective-permute-start | bytes 3145736 | tf_op jit(solution)/shard_map/ppermute | solution.py:288
  245.6 5.2 %collective-permute-done.23.a1_ref = bf16[2,1,512,256]{3,2,1,0:T(8,128)(2,1)} collective-permute-done((bf16[2,1,512,256]{3,2,1,0:T(8,128)(2,1)}, bf16[2,1,512,256]{3,2,1,0:T(8,128)(2,1)}, u32[]{:S(2)}, u32[]{:S(2)}) %collective-permute-start.23) | collective-permute-done | bytes 524320 | tf_op jit(solution)/shard_map/ppermute | solution.py:281
  250.9 3.2 %collective-permute-start.11 = (bf16[2,1,256,512]{3,2,1,0:T(8,128)(2,1)}, bf16[2,1,256,512]{3,2,1,0:T(8,128)(2,1)}, u32[]{:S(2)}, u32[]{:S(2)}) collective-permute-start(bf16[2,1,256,512]{3,2,1,0:T(8,128)(2,1)} %get-tuple-element.80), channel_id=1, source_target_pairs={{0,48},{16,0},{32,16},{48,32},{64,112},{80,64},{96,80},{112,96},{1... | collective-permute-start | bytes 1572872 | tf_op jit(solution)/shard_map/ppermute | solution.py:281
  254.1 1.8 convert_add_fusion
  255.9 3.2 %row_sum.3 = (f32[2,512,256]{2,1,0:T(8,128)}, bf16[2,512,256]{2,1,0:T(8,128)(2,1)}) custom-call(bf16[2,2,512,256]{3,2,1,0:T(8,128)(2,1)} %get-tuple-element.99.own_ref, bf16[2,1,512,256]{3,2,1,0:T(8,128)(2,1)} %collective-permute-done.23.a1_ref, bf16[2,1,512,256]{3,2,1,0:T(8,128)(2,1)} %copy-done.7, bf16[2,1,512,256]{3,2,1,0:T(8,128)(2,1)} %copy-done.8, ...), custom_call_target="tpu_custom_call" | custom-call | tf_op jit(solution)/shard_map/row_sum/pallas_call | solution.py:465
  259.2 2.5 collective-permute-done.9.a3_ref
  261.6 4.5 %collective-permute-start.27 = (bf16[2,512,256]{2,1,0:T(8,128)(2,1)}, bf16[2,512,256]{2,1,0:T(8,128)(2,1)}, u32[]{:S(2)}, u32[]{:S(2)}) collective-permute-start(bf16[2,512,256]{2,1,0:T(8,128)(2,1)} %get-tuple-element.109), channel_id=1, source_target_pairs={{0,64},{16,80},{32,96},{48,112},{64,0},{80,16},{96,32},{112,48},{1... | collective-permute-start | bytes 1572872 | tf_op jit(solution)/shard_map/ppermute | solution.py:288
  266.6 6.3 %collective-permute-done.8.a1_ref = bf16[2,1,256,512]{3,2,1,0:T(8,128)(2,1)} collective-permute-done((bf16[2,1,256,512]{3,2,1,0:T(8,128)(2,1)}, bf16[2,1,256,512]{3,2,1,0:T(8,128)(2,1)}, u32[]{:S(2)}, u32[]{:S(2)}) %collective-permute-start.8) | collective-permute-done | bytes 524320 | tf_op jit(solution)/shard_map/ppermute | solution.py:281
  272.9 3.2 %row_sum.2 = (f32[2,256,512]{2,1,0:T(8,128)}, bf16[2,256,512]{2,1,0:T(8,128)(2,1)}) custom-call(bf16[2,2,256,512]{3,2,1,0:T(8,128)(2,1)} %get-tuple-element.72.own_ref, bf16[2,1,256,512]{3,2,1,0:T(8,128)(2,1)} %collective-permute-done.8.a1_ref, bf16[2,1,256,512]{3,2,1,0:T(8,128)(2,1)} %collective-permute-done.9.a3_ref, ...), custom_call_target="tpu_custom_call" | custom-call | tf_op jit(solution)/shard_map/row_sum/pallas_call | solution.py:465
  276.1 4.5 %collective-permute-start.12 = (bf16[2,256,512]{2,1,0:T(8,128)(2,1)}, bf16[2,256,512]{2,1,0:T(8,128)(2,1)}, u32[]{:S(2)}, u32[]{:S(2)}) collective-permute-start(bf16[2,256,512]{2,1,0:T(8,128)(2,1)} %get-tuple-element.81), channel_id=1, source_target_pairs={{0,64},{16,80},{32,96},{48,112},{64,0},{80,16},{96,32},{112,48},{1... | collective-permute-start | bytes 1572872 | tf_op jit(solution)/shard_map/ppermute | solution.py:288
  280.6 6.1 %collective-permute-done.20 = bf16[1,256,512]{2,1,0:T(8,128)(2,1)} collective-permute-done((bf16[1,256,512]{2,1,0:T(8,128)(2,1)S(1)}, bf16[1,256,512]{2,1,0:T(8,128)(2,1)}, u32[]{:S(2)}, u32[]{:S(2)}) %collective-permute-start.20) | collective-permute-done | bytes 262176 | tf_op jit(solution)/shard_map/ppermute | solution.py:288
  286.7 1.0 fusion.1
  287.7 1.0 copy-done.3
  288.8 2.7 pair_sum.1
  291.5 3.5 %collective-permute-start.15 = (bf16[1,256,512]{2,1,0:T(8,128)(2,1)}, bf16[1,256,512]{2,1,0:T(8,128)(2,1)S(1)}, u32[]{:S(2)}, u32[]{:S(2)}) collective-permute-start(bf16[1,256,512]{2,1,0:T(8,128)(2,1)} %get-tuple-element.85), channel_id=1, source_target_pairs={{0,32},{16,48},{32,0},{48,16},{64,96},{80,112},{96,64},{112,80},{1... | collective-permute-start | bytes 786440 | tf_op jit(solution)/shard_map/ppermute | solution.py:281
  294.9 1.0 collective-permute-start.16
  296.0 1.9 add_convert_fusion
  297.9 3.9 %mixed.1 = bf16[128,2048]{1,0:T(8,128)(2,1)} custom-call(bf16[16,4,16,2048]{3,2,1,0:T(8,128)(2,1)} %all-to-all-done.3.back_ref, bf16[512,128]{1,0:T(8,128)(2,1)} %get-tuple-element.64.pick0_ref, bf16[512,128]{1,0:T(8,128)(2,1)} %get-tuple-element.65.pick1_ref, f32[128,2]{1,0:T(8,128)} %copy.17.gates_ref), custom_call_target="tpu_custom_call" | custom-call | tf_op jit(solution)/shard_map/mixed/pallas_call | solution.py:454
  301.8 3.6 %ngrad.1 = bf16[128,2048]{1,0:T(8,128)(2,1)} custom-call(bf16[16,4,16,2048]{3,2,1,0:T(8,128)(2,1)} %all-to-all-done.3.back_ref, bf16[512,128]{1,0:T(8,128)(2,1)} %get-tuple-element.64.pick0_ref, bf16[512,128]{1,0:T(8,128)(2,1)} %get-tuple-element.65.pick1_ref), custom_call_target="tpu_custom_call" | custom-call | tf_op jit(solution)/shard_map/ngrad/pallas_call | solution.py:457
  306.4 2.0 add_convert_fusion.1
  (59 shorter events, 3.0 us)
Async XLA Ops:
  3.2 26.3 %collective-permute-start.2 = (bf16[2,2048,128]{2,1,0:T(8,128)(2,1)S(1)}, bf16[2,2048,128]{2,1,0:T(8,128)(2,1)S(1)}, u32[]{:S(2)}, u32[]{:S(2)}) collective-permute-start(bf16[2,2048,128]{2,1,0:T(8,128)(2,1)S(1)} %get-tuple-element.110), channel_id=1, source_target_pairs={{0,64},{16,80},{32,96},{48,112},{64,0},{80,16},{96,32},{112,48},{1... | collective-permute-start | bytes 3145736 | tf_op jit(solution)/shard_map/ppermute | solution.py:288
  6.4 28.1 %collective-permute-start = (bf16[2,2048,128]{2,1,0:T(8,128)(2,1)}, bf16[2,2048,128]{2,1,0:T(8,128)(2,1)}, u32[]{:S(2)}, u32[]{:S(2)}) collective-permute-start(bf16[2,2048,128]{2,1,0:T(8,128)(2,1)} %get-tuple-element.111.kv), channel_id=1, source_target_pairs={{0,16},{16,32},{32,48},{48,0},{64,80},{80,96},{96,112},{1,17},{17,... | collective-permute-start | bytes 3145736 | tf_op jit(solution)/shard_map/ppermute | solution.py:281
  9.8 44.4 %collective-permute-start.4 = (bf16[2,2048,128]{2,1,0:T(8,128)(2,1)}, bf16[2,2048,128]{2,1,0:T(8,128)(2,1)}, u32[]{:S(2)}, u32[]{:S(2)}) collective-permute-start(bf16[2,2048,128]{2,1,0:T(8,128)(2,1)} %get-tuple-element.111.kv), channel_id=1, source_target_pairs={{0,48},{64,112},{1,49},{65,113},{2,50},{66,114},{3,51},{67,115},{4... | collective-permute-start | bytes 3145736 | tf_op jit(solution)/shard_map/ppermute | solution.py:281
  29.5 24.7 %copy-start.2 = (bf16[2,2048,128]{2,1,0:T(8,128)(2,1)}, bf16[2,2048,128]{2,1,0:T(8,128)(2,1)S(1)}, u32[]{:S(2)}) copy-start(bf16[2,2048,128]{2,1,0:T(8,128)(2,1)S(1)} %collective-permute-done.2.refs_2_.refs_4_) | copy-start | bytes 3145732
  29.5 34.7 %collective-permute-start.3 = (bf16[2,2048,128]{2,1,0:T(8,128)(2,1)S(1)}, bf16[2,2048,128]{2,1,0:T(8,128)(2,1)}, u32[]{:S(2)}, u32[]{:S(2)}) collective-permute-start(bf16[2,2048,128]{2,1,0:T(8,128)(2,1)S(1)} %collective-permute-done.2.refs_2_.refs_4_), channel_id=1, source_target_pairs={{64,112},{80,64},{96,80},{112,96},{65,113},{81,65},{97,81},{113,97... | collective-permute-start | bytes 3145736 | tf_op jit(solution)/shard_map/ppermute | solution.py:281
  34.5 29.8 %collective-permute-start.1 = (bf16[2,2048,128]{2,1,0:T(8,128)(2,1)}, bf16[2,2048,128]{2,1,0:T(8,128)(2,1)}, u32[]{:S(2)}, u32[]{:S(2)}) collective-permute-start(bf16[2,2048,128]{2,1,0:T(8,128)(2,1)} %collective-permute-done.refs_3_), channel_id=1, source_target_pairs={{0,16},{16,32},{32,48},{48,0},{80,96},{96,112},{1,17},{17,33},{33,... | collective-permute-start | bytes 3145736 | tf_op jit(solution)/shard_map/ppermute | solution.py:281
  41.9 50.6 %all-to-all-start = ((bf16[16,32,2048]{2,1,0:T(8,128)(2,1)}), bf16[16,32,2048]{2,1,0:T(8,128)(2,1)S(1)}, u32[]{:S(2)}, u32[]{:S(2)}) async-start(bf16[16,32,2048]{2,1,0:T(8,128)(2,1)} %get-tuple-element.62), calls=%async_computation | async-start | bytes 4194304 | tf_op jit(solution)/shard_map/all_to_all | solution.py:313
  74.0 17.2 %collective-permute-start.5 = (bf16[2048,128]{1,0:T(8,128)(2,1)}, bf16[2048,128]{1,0:T(8,128)(2,1)S(1)}, u32[]{:S(2)}, u32[]{:S(2)}) collective-permute-start(bf16[2048,128]{1,0:T(8,128)(2,1)} %get-tuple-element.61), channel_id=1, source_target_pairs={{0,64},{16,80},{32,96},{48,112},{1,65},{17,81},{33,97},{49,113},{2... | collective-permute-start | bytes 1572872 | tf_op jit(solution)/shard_map/ppermute | solution.py:381
  92.5 19.2 %copy-start.1 = (bf16[16,32,2048]{2,1,0:T(8,128)(2,1)}, bf16[16,32,2048]{2,1,0:T(8,128)(2,1)S(1)}, u32[]{:S(2)}) copy-start(bf16[16,32,2048]{2,1,0:T(8,128)(2,1)S(1)} %all-to-all-done.grad_ref.src) | copy-start | bytes 6291460
  111.8 31.5 %all-to-all-start.2 = ((bf16[16,32,2048]{2,1,0:T(8,128)(2,1)}), bf16[16,32,2048]{2,1,0:T(8,128)(2,1)S(1)}, u32[]{:S(2)}, u32[]{:S(2)}) async-start(bf16[16,32,2048]{2,1,0:T(8,128)(2,1)} %get-tuple-element.67), calls=%async_computation.2 | async-start | bytes 4194304 | tf_op jit(solution)/shard_map/all_to_all | solution.py:313
  143.3 1.3 copy-start
  161.2 136.7 %all-to-all-start.3 = ((bf16[16,4,16,2048]{3,2,1,0:T(8,128)(2,1)}), bf16[16,4,16,2048]{3,2,1,0:T(8,128)(2,1)}, u32[]{:S(2)}, u32[]{:S(2)}) async-start(bf16[16,4,16,2048]{3,2,1,0:T(8,128)(2,1)} %expert_back.1), calls=%async_computation.3 | async-start | bytes 8388608 | tf_op jit(solution)/shard_map/all_to_all | solution.py:313
  170.0 24.6 %collective-permute-start.21 = (bf16[2,1,512,256]{3,2,1,0:T(8,128)(2,1)}, bf16[2,1,512,256]{3,2,1,0:T(8,128)(2,1)S(1)}, u32[]{:S(2)}, u32[]{:S(2)}) collective-permute-start(bf16[2,1,512,256]{3,2,1,0:T(8,128)(2,1)} %get-tuple-element.101), channel_id=1, source_target_pairs={{0,16},{16,32},{32,48},{48,0},{64,80},{80,96},{96,112},{112,64},{1... | collective-permute-start | bytes 1572872 | tf_op jit(solution)/shard_map/ppermute | solution.py:281
  177.4 23.5 %collective-permute-start.22 = (bf16[2,1,512,256]{3,2,1,0:T(8,128)(2,1)}, bf16[2,1,512,256]{3,2,1,0:T(8,128)(2,1)S(1)}, u32[]{:S(2)}, u32[]{:S(2)}) collective-permute-start(bf16[2,1,512,256]{3,2,1,0:T(8,128)(2,1)} %get-tuple-element.103), channel_id=1, source_target_pairs={{0,48},{16,0},{32,16},{48,32},{64,112},{80,64},{96,80},{112,96},{1... | collective-permute-start | bytes 1572872 | tf_op jit(solution)/shard_map/ppermute | solution.py:281
  181.6 23.9 %collective-permute-start.24 = (bf16[2,1,512,256]{3,2,1,0:T(8,128)(2,1)}, bf16[2,1,512,256]{3,2,1,0:T(8,128)(2,1)S(1)}, u32[]{:S(2)}, u32[]{:S(2)}) collective-permute-start(bf16[2,1,512,256]{3,2,1,0:T(8,128)(2,1)} %get-tuple-element.105), channel_id=1, source_target_pairs={{0,48},{16,0},{32,16},{48,32},{64,112},{80,64},{96,80},{112,96},{1... | collective-permute-start | bytes 1572872 | tf_op jit(solution)/shard_map/ppermute | solution.py:281
  183.6 25.7 %collective-permute-start.25 = (bf16[2,1,512,256]{3,2,1,0:T(8,128)(2,1)}, bf16[2,1,512,256]{3,2,1,0:T(8,128)(2,1)S(1)}, u32[]{:S(2)}, u32[]{:S(2)}) collective-permute-start(bf16[2,1,512,256]{3,2,1,0:T(8,128)(2,1)} %get-tuple-element.106), channel_id=1, source_target_pairs={{0,16},{16,32},{32,48},{48,0},{64,80},{80,96},{96,112},{112,64},{1... | collective-permute-start | bytes 1572872 | tf_op jit(solution)/shard_map/ppermute | solution.py:281
  187.9 29.1 %collective-permute-start.6 = (bf16[2,1,256,512]{3,2,1,0:T(8,128)(2,1)}, bf16[2,1,256,512]{3,2,1,0:T(8,128)(2,1)S(1)}, u32[]{:S(2)}, u32[]{:S(2)}) collective-permute-start(bf16[2,1,256,512]{3,2,1,0:T(8,128)(2,1)} %get-tuple-element.74), channel_id=1, source_target_pairs={{0,16},{16,32},{32,48},{48,0},{64,80},{80,96},{96,112},{112,64},{1... | collective-permute-start | bytes 1572872 | tf_op jit(solution)/shard_map/ppermute | solution.py:281
  194.6 7.1 %copy-start.13 = (bf16[2,1,512,256]{3,2,1,0:T(8,128)(2,1)}, bf16[2,1,512,256]{3,2,1,0:T(8,128)(2,1)S(1)}, u32[]{:S(2)}) copy-start(bf16[2,1,512,256]{3,2,1,0:T(8,128)(2,1)S(1)} %collective-permute-done.21.far1_ref) | copy-start | bytes 1572868
  194.6 33.4 %collective-permute-start.7 = (bf16[2,1,256,512]{3,2,1,0:T(8,128)(2,1)}, bf16[2,1,256,512]{3,2,1,0:T(8,128)(2,1)S(1)}, u32[]{:S(2)}, u32[]{:S(2)}) collective-permute-start(bf16[2,1,256,512]{3,2,1,0:T(8,128)(2,1)} %get-tuple-element.76), channel_id=1, source_target_pairs={{0,48},{16,0},{32,16},{48,32},{64,112},{80,64},{96,80},{112,96},{1... | collective-permute-start | bytes 1572872 | tf_op jit(solution)/shard_map/ppermute | solution.py:281
  200.9 0.8 copy-start.14
  201.7 29.9 %collective-permute-start.17 = (bf16[2,1,256,512]{3,2,1,0:T(8,128)(2,1)}, bf16[2,1,256,512]{3,2,1,0:T(8,128)(2,1)S(1)}, u32[]{:S(2)}, u32[]{:S(2)}) collective-permute-start(bf16[2,1,256,512]{3,2,1,0:T(8,128)(2,1)} %get-tuple-element.96), channel_id=1, source_target_pairs={{0,16},{16,32},{32,48},{48,0},{64,80},{80,96},{96,112},{112,64},{1... | collective-permute-start | bytes 1572872 | tf_op jit(solution)/shard_map/ppermute | solution.py:281
  205.5 50.4 %copy-start.7 = (bf16[2,1,512,256]{3,2,1,0:T(8,128)(2,1)}, bf16[2,1,512,256]{3,2,1,0:T(8,128)(2,1)S(1)}, u32[]{:S(2)}) copy-start(bf16[2,1,512,256]{3,2,1,0:T(8,128)(2,1)S(1)} %collective-permute-done.24.a3_ref) | copy-start | bytes 1572868
  205.5 35.6 %collective-permute-start.18 = (bf16[2,1,256,512]{3,2,1,0:T(8,128)(2,1)}, bf16[2,1,256,512]{3,2,1,0:T(8,128)(2,1)S(1)}, u32[]{:S(2)}, u32[]{:S(2)}) collective-permute-start(bf16[2,1,256,512]{3,2,1,0:T(8,128)(2,1)} %get-tuple-element.97), channel_id=1, source_target_pairs={{0,32},{16,48},{32,0},{48,16},{64,96},{80,112},{96,64},{112,80},{1... | collective-permute-start | bytes 1572872 | tf_op jit(solution)/shard_map/ppermute | solution.py:281
  209.3 46.6 %copy-start.8 = (bf16[2,1,512,256]{3,2,1,0:T(8,128)(2,1)}, bf16[2,1,512,256]{3,2,1,0:T(8,128)(2,1)S(1)}, u32[]{:S(2)}) copy-start(bf16[2,1,512,256]{3,2,1,0:T(8,128)(2,1)S(1)} %collective-permute-done.25.b1_ref) | copy-start | bytes 1572868
  209.3 31.7 %collective-permute-start.19 = (bf16[2,1,256,512]{3,2,1,0:T(8,128)(2,1)}, bf16[2,1,256,512]{3,2,1,0:T(8,128)(2,1)}, u32[]{:S(2)}, u32[]{:S(2)}) collective-permute-start(bf16[2,1,256,512]{3,2,1,0:T(8,128)(2,1)} %get-tuple-element.98), channel_id=1, source_target_pairs={{0,48},{16,0},{32,16},{48,32},{64,112},{80,64},{96,80},{112,96},{1... | collective-permute-start | bytes 1572872 | tf_op jit(solution)/shard_map/ppermute | solution.py:281
  217.1 14.6 %copy-start.10 = (bf16[2,1,256,512]{3,2,1,0:T(8,128)(2,1)}, bf16[2,1,256,512]{3,2,1,0:T(8,128)(2,1)S(1)}, u32[]{:S(2)}) copy-start(bf16[2,1,256,512]{3,2,1,0:T(8,128)(2,1)S(1)} %collective-permute-done.6.far1_ref) | copy-start | bytes 1572868
  217.1 33.8 %collective-permute-start.23 = (bf16[2,1,512,256]{3,2,1,0:T(8,128)(2,1)}, bf16[2,1,512,256]{3,2,1,0:T(8,128)(2,1)}, u32[]{:S(2)}, u32[]{:S(2)}) collective-permute-start(bf16[2,1,512,256]{3,2,1,0:T(8,128)(2,1)} %get-tuple-element.104), channel_id=1, source_target_pairs={{0,16},{16,32},{32,48},{48,0},{64,80},{80,96},{96,112},{112,64},{1... | collective-permute-start | bytes 1572872 | tf_op jit(solution)/shard_map/ppermute | solution.py:281
  227.9 3.7 %copy-start.12 = (bf16[2,1,256,512]{3,2,1,0:T(8,128)(2,1)}, bf16[2,1,256,512]{3,2,1,0:T(8,128)(2,1)S(1)}, u32[]{:S(2)}) copy-start(bf16[2,1,256,512]{3,2,1,0:T(8,128)(2,1)S(1)} %collective-permute-done.7.far3_ref) | copy-start | bytes 1572868
  227.9 22.9 %collective-permute-start.26 = (bf16[2,1,512,256]{3,2,1,0:T(8,128)(2,1)}, bf16[2,1,512,256]{3,2,1,0:T(8,128)(2,1)}, u32[]{:S(2)}, u32[]{:S(2)}) collective-permute-start(bf16[2,1,512,256]{3,2,1,0:T(8,128)(2,1)} %get-tuple-element.107), channel_id=1, source_target_pairs={{0,48},{16,0},{32,16},{48,32},{64,112},{80,64},{96,80},{112,96},{1... | collective-permute-start | bytes 1572872 | tf_op jit(solution)/shard_map/ppermute | solution.py:281
  231.5 9.5 %copy-start.9 = (bf16[2,1,256,512]{3,2,1,0:T(8,128)(2,1)}, bf16[2,1,256,512]{3,2,1,0:T(8,128)(2,1)S(1)}, u32[]{:S(2)}) copy-start(bf16[2,1,256,512]{3,2,1,0:T(8,128)(2,1)S(1)} %collective-permute-done.17) | copy-start | bytes 1572868
  231.5 30.1 %collective-permute-start.9 = (bf16[2,1,256,512]{3,2,1,0:T(8,128)(2,1)}, bf16[2,1,256,512]{3,2,1,0:T(8,128)(2,1)}, u32[]{:S(2)}, u32[]{:S(2)}) collective-permute-start(bf16[2,1,256,512]{3,2,1,0:T(8,128)(2,1)} %get-tuple-element.78), channel_id=1, source_target_pairs={{0,48},{16,0},{32,16},{48,32},{64,112},{80,64},{96,80},{112,96},{1... | collective-permute-start | bytes 1572872 | tf_op jit(solution)/shard_map/ppermute | solution.py:281
  241.0 13.1 %copy-start.11 = (bf16[2,1,256,512]{3,2,1,0:T(8,128)(2,1)}, bf16[2,1,256,512]{3,2,1,0:T(8,128)(2,1)S(1)}, u32[]{:S(2)}) copy-start(bf16[2,1,256,512]{3,2,1,0:T(8,128)(2,1)S(1)} %collective-permute-done.18) | copy-start | bytes 1572868
  241.0 25.1 %collective-permute-start.10 = (bf16[2,1,256,512]{3,2,1,0:T(8,128)(2,1)}, bf16[2,1,256,512]{3,2,1,0:T(8,128)(2,1)}, u32[]{:S(2)}, u32[]{:S(2)}) collective-permute-start(bf16[2,1,256,512]{3,2,1,0:T(8,128)(2,1)} %get-tuple-element.79), channel_id=1, source_target_pairs={{0,16},{16,32},{32,48},{48,0},{64,80},{80,96},{96,112},{112,64},{1... | collective-permute-start | bytes 1572872 | tf_op jit(solution)/shard_map/ppermute | solution.py:281
  241.1 46.7 %collective-permute-start.13 = (bf16[4,1,256,512]{3,2,1,0:T(8,128)(2,1)}, bf16[4,1,256,512]{3,2,1,0:T(8,128)(2,1)S(1)}, u32[]{:S(2)}, u32[]{:S(2)}) collective-permute-start(bf16[4,1,256,512]{3,2,1,0:T(8,128)(2,1)} %get-tuple-element.83), channel_id=1, source_target_pairs={{0,64},{16,80},{32,96},{48,112},{64,0},{80,16},{96,32},{112,48},{1... | collective-permute-start | bytes 3145736 | tf_op jit(solution)/shard_map/ppermute | solution.py:288
  250.9 22.0 %collective-permute-start.8 = (bf16[2,1,256,512]{3,2,1,0:T(8,128)(2,1)}, bf16[2,1,256,512]{3,2,1,0:T(8,128)(2,1)}, u32[]{:S(2)}, u32[]{:S(2)}) collective-permute-start(bf16[2,1,256,512]{3,2,1,0:T(8,128)(2,1)} %get-tuple-element.77), channel_id=1, source_target_pairs={{0,16},{16,32},{32,48},{48,0},{64,80},{80,96},{96,112},{112,64},{1... | collective-permute-start | bytes 1572872 | tf_op jit(solution)/shard_map/ppermute | solution.py:281
  250.9 22.0 %collective-permute-start.11 = (bf16[2,1,256,512]{3,2,1,0:T(8,128)(2,1)}, bf16[2,1,256,512]{3,2,1,0:T(8,128)(2,1)}, u32[]{:S(2)}, u32[]{:S(2)}) collective-permute-start(bf16[2,1,256,512]{3,2,1,0:T(8,128)(2,1)} %get-tuple-element.80), channel_id=1, source_target_pairs={{0,48},{16,0},{32,16},{48,32},{64,112},{80,64},{96,80},{112,96},{1... | collective-permute-start | bytes 1572872 | tf_op jit(solution)/shard_map/ppermute | solution.py:281
  259.2 36.8 %copy-start.5 = (f32[2,512,256]{2,1,0:T(8,128)S(1)}, f32[2,512,256]{2,1,0:T(8,128)}, u32[]{:S(2)}) copy-start(f32[2,512,256]{2,1,0:T(8,128)} %get-tuple-element.108) | copy-start | bytes 3145732
  261.6 34.3 %collective-permute-start.27 = (bf16[2,512,256]{2,1,0:T(8,128)(2,1)}, bf16[2,512,256]{2,1,0:T(8,128)(2,1)}, u32[]{:S(2)}, u32[]{:S(2)}) collective-permute-start(bf16[2,512,256]{2,1,0:T(8,128)(2,1)} %get-tuple-element.109), channel_id=1, source_target_pairs={{0,64},{16,80},{32,96},{48,112},{64,0},{80,16},{96,32},{112,48},{1... | collective-permute-start | bytes 1572872 | tf_op jit(solution)/shard_map/ppermute | solution.py:288
  266.2 20.5 %collective-permute-start.20 = (bf16[1,256,512]{2,1,0:T(8,128)(2,1)S(1)}, bf16[1,256,512]{2,1,0:T(8,128)(2,1)}, u32[]{:S(2)}, u32[]{:S(2)}) collective-permute-start(bf16[1,256,512]{2,1,0:T(8,128)(2,1)S(1)} %fusion.2), channel_id=1, source_target_pairs={{0,64},{16,80},{32,96},{48,112},{64,0},{80,16},{96,32},{112,48},{1... | collective-permute-start | bytes 786440 | tf_op jit(solution)/shard_map/ppermute | solution.py:288
  276.1 29.3 %collective-permute-start.12 = (bf16[2,256,512]{2,1,0:T(8,128)(2,1)}, bf16[2,256,512]{2,1,0:T(8,128)(2,1)}, u32[]{:S(2)}, u32[]{:S(2)}) collective-permute-start(bf16[2,256,512]{2,1,0:T(8,128)(2,1)} %get-tuple-element.81), channel_id=1, source_target_pairs={{0,64},{16,80},{32,96},{48,112},{64,0},{80,16},{96,32},{112,48},{1... | collective-permute-start | bytes 1572872 | tf_op jit(solution)/shard_map/ppermute | solution.py:288
  287.7 1.1 copy-start.3
  291.4 14.0 %collective-permute-start.14 = (bf16[1,256,512]{2,1,0:T(8,128)(2,1)}, bf16[1,256,512]{2,1,0:T(8,128)(2,1)S(1)}, u32[]{:S(2)}, u32[]{:S(2)}) collective-permute-start(bf16[1,256,512]{2,1,0:T(8,128)(2,1)} %get-tuple-element.84), channel_id=1, source_target_pairs={{0,16},{16,32},{32,48},{48,0},{64,80},{80,96},{96,112},{112,64},{1... | collective-permute-start | bytes 786440 | tf_op jit(solution)/shard_map/ppermute | solution.py:281
  291.5 14.0 %collective-permute-start.15 = (bf16[1,256,512]{2,1,0:T(8,128)(2,1)}, bf16[1,256,512]{2,1,0:T(8,128)(2,1)S(1)}, u32[]{:S(2)}, u32[]{:S(2)}) collective-permute-start(bf16[1,256,512]{2,1,0:T(8,128)(2,1)} %get-tuple-element.85), channel_id=1, source_target_pairs={{0,32},{16,48},{32,0},{48,16},{64,96},{80,112},{96,64},{112,80},{1... | collective-permute-start | bytes 786440 | tf_op jit(solution)/shard_map/ppermute | solution.py:281
  294.9 10.5 %collective-permute-start.16 = (bf16[1,256,512]{2,1,0:T(8,128)(2,1)}, bf16[1,256,512]{2,1,0:T(8,128)(2,1)S(1)}, u32[]{:S(2)}, u32[]{:S(2)}) collective-permute-start(bf16[1,256,512]{2,1,0:T(8,128)(2,1)} %get-tuple-element.86), channel_id=1, source_target_pairs={{0,48},{16,0},{32,16},{48,32},{64,112},{80,64},{96,80},{112,96},{1... | collective-permute-start | bytes 786440 | tf_op jit(solution)/shard_map/ppermute | solution.py:281
  297.9 7.5 %copy-start.6 = (f32[1,256,512]{2,1,0:T(8,128)S(1)}, f32[1,256,512]{2,1,0:T(8,128)}, u32[]{:S(2)}) copy-start(f32[1,256,512]{2,1,0:T(8,128)} %get-tuple-element.91) | copy-start | bytes 1572868
  301.8 4.6 %copy-start.4 = (f32[2,256,512]{2,1,0:T(8,128)S(1)}, f32[2,256,512]{2,1,0:T(8,128)}, u32[]{:S(2)}) copy-start(f32[2,256,512]{2,1,0:T(8,128)} %get-tuple-element.89) | copy-start | bytes 3145732

commit v4 on v3

--- a/solution.py
+++ b/solution.py
@@ -394,7 +394,7 @@
         out_shape=full((2, ROWS, hid), F32),
         in_specs=[expert_block, out_weight],
         out_specs=act_block,
-        name="hidden_grad",
+        name="hg",
     )(recv_grads, w_down)
     normed, send_inputs = pl.pallas_call(
         norm_kernel,
@@ -473,7 +473,8 @@
     gate_part, gate_send = over_row(ga[6], got_g)
     gate_got = move_x(gate_send)
     sums = wide(ua[3]) + wide(got_a[0]) + wide(got_a[1]) + wide(got_a[2])
-    got_ax = move_x(sums[1].astype(BF16))
+    up_sent = sums[1].astype(BF16)
+    got_ax = move_x(up_sent)
     quarter = up_keep.shape[1:]
     up_part, *up_rest = pl.pallas_call(
         pair_sum_kernel,
@@ -485,9 +486,7 @@
     got_u = []
     for n in (1, 2, 3):
         got_u.append(move_y(up_rest[n - 1], n))
-    mixed, normed_grad, gate_got, *got_u = lax.optimization_barrier(
-        (mixed, normed_grad, gate_got, *got_u)
-    )
+    _, gate_got, *got_u = lax.optimization_barrier((up_sent, gate_got, *got_u))
     gate_sum = (gate_part + wide(gate_got)).astype(BF16)
     up_first = (up_part + wide(got_u[0]) + wide(got_u[1]) + wide(got_u[2])).astype(BF16)
     up_last = (sums[0] + wide(got_ax)).astype(BF16)

time: 310 us -> 319 us (1.029)
  waiting for transfers between devices: 104 us -> 110 us
    ppermute x22, waiting for transfers between devices: 49.8 us -> 75.5 us  [move_y(): return lax.ppermute(value, 'ctx', pairs)]
    ppermute x5, waiting for transfers between devices: 21.2 us -> 2.45 us  [move_x(): return lax.ppermute(value, 'ctx', pairs)]
    ppermute x22, starting transfers between devices: 43.4 us -> 47.9 us  [move_y(): return lax.ppermute(value, 'ctx', pairs)]
  transfers between devices with their start and end apart: 31 -> 31, of which waited for: 13 -> 14; matrix products, arithmetic and copies ran while one was open for 3% -> 4% of each run, Pallas kernels for 23% -> 20%
where the time goes in v4:
time: 319 us; the launch traced here: 318 us
  waiting for transfers between devices  110 us (34%)
  Pallas kernels  91.5 us (29%)
  starting transfers between devices  82.5 us (26%)
  blocking collectives  15.5 us (5%)
  other arithmetic  11.3 us (4%)
  local copies, waits for them, and re-layouts  5.5 us (2%)
    ppermute x22, waiting for transfers between devices, move_y(): return lax.ppermute(value, 'ctx', pairs)  75.5 us
    ppermute x22, starting transfers between devices, move_y(): return lax.ppermute(value, 'ctx', pairs)  47.9 us
    all_to_all x3, waiting for transfers between devices, exchange(): return lax.all_to_all(value, 'exp', split_axis=0, concat_axis=0, tiled=True)  23.3 us
    pallas_call x3, Pallas kernels, attend(): pl.pallas_call(kernel, out_shape=tuple((jax.ShapeDtypeStruct((rows, HEAD_...  22.6 us
    all_to_all x1, blocking collectives, exchange(): return lax.all_to_all(value, 'exp', split_axis=0, concat_axis=0, tiled=True)  15.5 us
    all_to_all x3, starting transfers between devices, exchange(): return lax.all_to_all(value, 'exp', split_axis=0, concat_axis=0, tiled=True)  14.6 us
    ppermute x5, starting transfers between devices, move_x(): return lax.ppermute(value, 'ctx', pairs)  14.2 us
    pallas_call x3, Pallas kernels, weight_grad(): pl.pallas_call(kernel, out_shape=tuple((jax.ShapeDtypeStruct((c, len(x),...  12.9 us
  transfers between devices with their start and end apart: 31, of which 14 were waited for; matrix products, arithmetic and copies ran while one was open for 4% of the time, Pallas kernels for 20%

profile of v4, /device:TPU:0, one launch (start us, length us, event | category | flops | bytes accessed | tf_op | source)
XLA Modules:
  0.0 317.6 jit_solution(2985182516436713448)
XLA Ops:
  0.6 2.6 broadcast_select_fusion
  3.2 3.6 %collective-permute-start = (bf16[2,2048,128]{2,1,0:T(8,128)(2,1)}, bf16[2,2048,128]{2,1,0:T(8,128)(2,1)}, u32[]{:S(2)}, u32[]{:S(2)}) collective-permute-start(bf16[2,2048,128]{2,1,0:T(8,128)(2,1)} %get-tuple-element.107.kv), channel_id=1, source_target_pairs={{0,16},{16,32},{32,48},{48,0},{64,80},{80,96},{96,112},{1,17},{17,... | collective-permute-start | bytes 3145736 | tf_op jit(solution)/shard_map/ppermute | solution.py:281
  6.8 4.0 %collective-permute-start.2 = (bf16[2,2048,128]{2,1,0:T(8,128)(2,1)S(1)}, bf16[2,2048,128]{2,1,0:T(8,128)(2,1)S(1)}, u32[]{:S(2)}, u32[]{:S(2)}) collective-permute-start(bf16[2,2048,128]{2,1,0:T(8,128)(2,1)S(1)} %get-tuple-element.106), channel_id=1, source_target_pairs={{0,64},{16,80},{32,96},{48,112},{64,0},{80,16},{96,32},{112,48},{1... | collective-permute-start | bytes 3145736 | tf_op jit(solution)/shard_map/ppermute | solution.py:288
  10.8 2.8 collective-permute-start.4
  13.6 18.1 %collective-permute-done.refs_3_ = bf16[2,2048,128]{2,1,0:T(8,128)(2,1)} collective-permute-done((bf16[2,2048,128]{2,1,0:T(8,128)(2,1)}, bf16[2,2048,128]{2,1,0:T(8,128)(2,1)}, u32[]{:S(2)}, u32[]{:S(2)}) %collective-permute-start) | collective-permute-done | bytes 1048608 | tf_op jit(solution)/shard_map/ppermute | solution.py:281
  31.7 2.2 collective-permute-start.1
  33.9 1.7 collective-permute-start.3
  35.6 1.4 copy.17.gates_ref
  37.0 3.9 %route.1 = (bf16[512,128]{1,0:T(8,128)(2,1)}, bf16[512,128]{1,0:T(8,128)(2,1)}, bf16[16,32,2048]{2,1,0:T(8,128)(2,1)}) custom-call(s32[2,128]{1,0:T(2,128)} %bitcast.17, f32[128,2]{1,0:T(8,128)} %copy.17.gates_ref, bf16[128,2048]{1,0:T(8,128)(2,1)} %grad_ref.1), custom_call_target="tpu_custom_call" | custom-call | tf_op jit(solution)/shard_map/route/pallas_call | solution.py:349
  40.9 6.3 %all-to-all-start = ((bf16[16,32,2048]{2,1,0:T(8,128)(2,1)}), bf16[16,32,2048]{2,1,0:T(8,128)(2,1)S(1)}, u32[]{:S(2)}, u32[]{:S(2)}) async-start(bf16[16,32,2048]{2,1,0:T(8,128)(2,1)} %get-tuple-element.60), calls=%async_computation | async-start | bytes 4194304 | tf_op jit(solution)/shard_map/all_to_all | solution.py:313
  47.2 5.6 %attend_own.1.refs_6_ = f32[2048,128]{1,0:T(8,128)} custom-call(bf16[2048,128]{1,0:T(8,128)(2,1)} %refs_1_.5, bf16[2,2048,128]{2,1,0:T(8,128)(2,1)} %get-tuple-element.107.kv), custom_call_target="tpu_custom_call" | custom-call | tf_op jit(solution)/shard_map/attend_own/pallas_call | solution.py:80
  52.8 1.2 dynamic-slice_bitcast_fusion.refs_0_.order_ref
  54.1 10.0 %shard_map.154 = (f32[2048,128]{1,0:T(8,128)}, f32[2048,128]{1,0:T(8,128)}) custom-call(s32[24]{0:T(128)} %dynamic-slice_bitcast_fusion.refs_0_.order_ref, bf16[2048,128]{1,0:T(8,128)(2,1)} %refs_1_.5, bf16[2,2048,128]{2,1,0:T(8,128)(2,1)} %copy-done.2, bf16[2,2048,128]{2,1,0:T(8,128)(2,1)} %collective-permute-done.refs_3_, bf16[2,2048,128]{2,1,0:T(8,128)(2,1)} %copy-done.2, ...), custom_call_target="tpu_custom_call" | custom-call | tf_op jit(solution)/shard_map/pallas_call | solution.py:131
  64.1 9.7 %shard_map.155 = (f32[2048,128]{1,0:T(8,128)}, bf16[2048,128]{1,0:T(8,128)(2,1)}) custom-call(s32[24]{0:T(128)} %dynamic-slice_bitcast_fusion.refs_0_.order_ref, bf16[2048,128]{1,0:T(8,128)(2,1)} %refs_1_.5, bf16[2,2048,128]{2,1,0:T(8,128)(2,1)} %copy-done.2, bf16[2,2048,128]{2,1,0:T(8,128)(2,1)} %collective-permute-done.1.refs_3_.refs_2_, ...), custom_call_target="tpu_custom_call" | custom-call | tf_op jit(solution)/shard_map/pallas_call | solution.py:131
  73.8 5.7 %collective-permute-start.5 = (bf16[2048,128]{1,0:T(8,128)(2,1)}, bf16[2048,128]{1,0:T(8,128)(2,1)S(1)}, u32[]{:S(2)}, u32[]{:S(2)}) collective-permute-start(bf16[2048,128]{1,0:T(8,128)(2,1)} %get-tuple-element.59), channel_id=1, source_target_pairs={{0,64},{16,80},{32,96},{48,112},{1,65},{17,81},{33,97},{49,113},{2... | collective-permute-start | bytes 1572872 | tf_op jit(solution)/shard_map/ppermute | solution.py:381
  79.5 2.9 shard_map.156
  82.4 9.1 %collective-permute-done.5 = bf16[2048,128]{1,0:T(8,128)(2,1)S(1)} collective-permute-done((bf16[2048,128]{1,0:T(8,128)(2,1)}, bf16[2048,128]{1,0:T(8,128)(2,1)S(1)}, u32[]{:S(2)}, u32[]{:S(2)}) %collective-permute-start.5) | collective-permute-done | bytes 524320 | tf_op jit(solution)/shard_map/ppermute | solution.py:381
  91.5 1.3 add_convert_fusion.2
  92.9 15.5 %all_to_all.20.tok_ref = bf16[16,128,128]{2,1,0:T(8,128)(2,1)} all-to-all(bf16[16,128,128]{2,1,0:T(8,128)(2,1)S(1)} %bitcast.14), channel_id=1, replica_groups=mesh['ctx'=8,'exp'=16] {'exp'}, dimensions={0} | all-to-all | bytes 1048576 | tf_op jit(solution)/shard_map/all_to_all | solution.py:313
  108.4 3.7 %norm.1 = (bf16[128,2048]{1,0:T(8,128)(2,1)}, bf16[16,32,2048]{2,1,0:T(8,128)(2,1)}) custom-call(bf16[16,128,128]{2,1,0:T(8,128)(2,1)} %all_to_all.20.tok_ref, bf16[128,2048]{1,0:T(8,128)(2,1)} %gate_ref.3, bf16[512,128]{1,0:T(8,128)(2,1)} %get-tuple-element.62.pick0_ref, bf16[512,128]{1,0:T(8,128)(2,1)} %get-tuple-element.63.pick1_ref), custom_call_target="tpu_custom_call" | custom-call | tf_op jit(solution)/shard_map/norm/pallas_call | solution.py:399
  112.1 3.7 %all-to-all-start.2 = ((bf16[16,32,2048]{2,1,0:T(8,128)(2,1)}), bf16[16,32,2048]{2,1,0:T(8,128)(2,1)S(1)}, u32[]{:S(2)}, u32[]{:S(2)}) async-start(bf16[16,32,2048]{2,1,0:T(8,128)(2,1)} %get-tuple-element.65), calls=%async_computation.2 | async-start | bytes 4194304 | tf_op jit(solution)/shard_map/all_to_all | solution.py:313
  115.8 4.5 %hg.1.hg_ref = f32[2,256,512]{2,1,0:T(8,128)} custom-call(bf16[16,32,2048]{2,1,0:T(8,128)(2,1)} %copy-done.1, bf16[2,512,2048]{2,1,0:T(8,128)(2,1)} %down_ref.3), custom_call_target="tpu_custom_call" | custom-call | tf_op jit(solution)/shard_map/hg/pallas_call | solution.py:391
  120.3 23.3 %all-to-all-done.2.in_ref.src = bf16[16,32,2048]{2,1,0:T(8,128)(2,1)S(1)} async-done(((bf16[16,32,2048]{2,1,0:T(8,128)(2,1)}), bf16[16,32,2048]{2,1,0:T(8,128)(2,1)S(1)}, u32[]{:S(2)}, u32[]{:S(2)}) %all-to-all-start.2) | async-done | bytes 2097184 | tf_op jit(solution)/shard_map/all_to_all | solution.py:313
  143.6 1.3 copy-done
  144.9 6.5 %expert_in.1 = (bf16[2,256,512]{2,1,0:T(8,128)(2,1)}, bf16[2,256,512]{2,1,0:T(8,128)(2,1)}, bf16[2,256,512]{2,1,0:T(8,128)(2,1)}) custom-call(bf16[16,32,2048]{2,1,0:T(8,128)(2,1)} %copy-done, f32[2,256,512]{2,1,0:T(8,128)} %hg.1.hg_ref, bf16[2,2048,512]{2,1,0:T(8,128)(2,1)} %gate_ref.5, bf16[2,2048,512]{2,1,0:T(8,128)(2,1)} %up_ref.3), custom_call_target="tpu_custom_call" | custom-call | tf_op jit(solution)/shard_map/expert_in/pallas_call | solution.py:409
  151.5 10.1 %expert_back.1 = bf16[16,4,16,2048]{3,2,1,0:T(8,128)(2,1)} custom-call(bf16[2,256,512]{2,1,0:T(8,128)(2,1)} %get-tuple-element.67.hidden_ref.act_ref, bf16[2,512,2048]{2,1,0:T(8,128)(2,1)} %down_ref.3, bf16[2,256,512]{2,1,0:T(8,128)(2,1)} %get-tuple-element.68.gg_ref.act_ref, bf16[2,256,512]{2,1,0:T(8,128)(2,1)} %get-tuple-element.69.ug_ref.act_ref, ...), custom_call_target="tpu_custom_call" | custom-call | tf_op jit(solution)/shard_map/expert_back/pallas_call | solution.py:436
  161.6 4.6 %all-to-all-start.3 = ((bf16[16,4,16,2048]{3,2,1,0:T(8,128)(2,1)}), bf16[16,4,16,2048]{3,2,1,0:T(8,128)(2,1)}, u32[]{:S(2)}, u32[]{:S(2)}) async-start(bf16[16,4,16,2048]{3,2,1,0:T(8,128)(2,1)} %expert_back.1), calls=%async_computation.3 | async-start | bytes 8388608 | tf_op jit(solution)/shard_map/all_to_all | solution.py:313
  166.2 4.2 %shard_map.159 = (bf16[2,1,512,256]{3,2,1,0:T(8,128)(2,1)}, bf16[2,1,512,256]{3,2,1,0:T(8,128)(2,1)}, bf16[2,1,512,256]{3,2,1,0:T(8,128)(2,1)}, bf16[2,1,512,256...) custom-call(s32[24]{0:T(128)} %dynamic-slice_bitcast_fusion.refs_0_., ...), custom_call_target="tpu_custom_call" | custom-call | tf_op jit(solution)/shard_map/pallas_call | solution.py:222
  170.3 7.3 %collective-permute-start.21 = (bf16[2,1,512,256]{3,2,1,0:T(8,128)(2,1)}, bf16[2,1,512,256]{3,2,1,0:T(8,128)(2,1)S(1)}, u32[]{:S(2)}, u32[]{:S(2)}) collective-permute-start(bf16[2,1,512,256]{3,2,1,0:T(8,128)(2,1)} %get-tuple-element.97), channel_id=1, source_target_pairs={{0,16},{16,32},{32,48},{48,0},{64,80},{80,96},{96,112},{112,64},{1... | collective-permute-start | bytes 1572872 | tf_op jit(solution)/shard_map/ppermute | solution.py:281
  177.6 6.6 %collective-permute-start.22 = (bf16[2,1,512,256]{3,2,1,0:T(8,128)(2,1)}, bf16[2,1,512,256]{3,2,1,0:T(8,128)(2,1)S(1)}, u32[]{:S(2)}, u32[]{:S(2)}) collective-permute-start(bf16[2,1,512,256]{3,2,1,0:T(8,128)(2,1)} %get-tuple-element.99), channel_id=1, source_target_pairs={{0,48},{16,0},{32,16},{48,32},{64,112},{80,64},{96,80},{112,96},{1... | collective-permute-start | bytes 1572872 | tf_op jit(solution)/shard_map/ppermute | solution.py:281
  184.2 2.0 collective-permute-start.24
  186.2 4.3 %shard_map.158 = (bf16[4,1,256,512]{3,2,1,0:T(8,128)(2,1)}, bf16[4,1,256,512]{3,2,1,0:T(8,128)(2,1)}, bf16[2,1,256,512]{3,2,1,0:T(8,128)(2,1)}, bf16[2,1,256,512...) custom-call(s32[24]{0:T(128)} %dynamic-slice_bitcast_fusion.refs_0_.order_ref, ...), custom_call_target="tpu_custom_call" | custom-call | tf_op jit(solution)/shard_map/pallas_call | solution.py:222
  190.6 4.4 %shard_map.157 = (bf16[2,1,256,512]{3,2,1,0:T(8,128)(2,1)}, bf16[2,1,256,512]{3,2,1,0:T(8,128)(2,1)}, bf16[2,1,256,512]{3,2,1,0:T(8,128)(2,1)}, bf16[2,1,256,512...) custom-call(s32[24]{0:T(128)} %dynamic-slice_bitcast_fusion.refs_0_., ...), custom_call_target="tpu_custom_call" | custom-call | tf_op jit(solution)/shard_map/pallas_call | solution.py:222
  194.9 2.2 collective-permute-done.21.far1_ref
  197.2 2.0 collective-permute-start.7
  199.2 1.5 collective-permute-start.13
  200.7 7.4 %collective-permute-done.24.a3_ref = bf16[2,1,512,256]{3,2,1,0:T(8,128)(2,1)S(1)} collective-permute-done((bf16[2,1,512,256]{3,2,1,0:T(8,128)(2,1)}, bf16[2,1,512,256]{3,2,1,0:T(8,128)(2,1)S(1)}, u32[]{:S(2)}, u32[]{:S(2)}) %collective-permute-start.24) | collective-permute-done | bytes 524320 | tf_op jit(solution)/shard_map/ppermute | solution.py:281
  208.1 3.6 %collective-permute-start.14 = (bf16[2,1,256,512]{3,2,1,0:T(8,128)(2,1)}, bf16[2,1,256,512]{3,2,1,0:T(8,128)(2,1)}, u32[]{:S(2)}, u32[]{:S(2)}) collective-permute-start(bf16[2,1,256,512]{3,2,1,0:T(8,128)(2,1)} %get-tuple-element.83), channel_id=1, source_target_pairs={{0,48},{16,0},{32,16},{48,32},{64,112},{80,64},{96,80},{112,96},{1... | collective-permute-start | bytes 1572872 | tf_op jit(solution)/shard_map/ppermute | solution.py:281
  211.7 8.0 %collective-permute-done.6.far1_ref = bf16[2,1,256,512]{3,2,1,0:T(8,128)(2,1)S(1)} collective-permute-done((bf16[2,1,256,512]{3,2,1,0:T(8,128)(2,1)}, bf16[2,1,256,512]{3,2,1,0:T(8,128)(2,1)S(1)}, u32[]{:S(2)}, u32[]{:S(2)}) %collective-permute-start.6) | collective-permute-done | bytes 524320 | tf_op jit(solution)/shard_map/ppermute | solution.py:281
  219.7 2.0 collective-permute-start.9
  221.7 8.9 %collective-permute-done.7.far3_ref = bf16[2,1,256,512]{3,2,1,0:T(8,128)(2,1)S(1)} collective-permute-done((bf16[2,1,256,512]{3,2,1,0:T(8,128)(2,1)}, bf16[2,1,256,512]{3,2,1,0:T(8,128)(2,1)S(1)}, u32[]{:S(2)}, u32[]{:S(2)}) %collective-permute-start.7) | collective-permute-done | bytes 524320 | tf_op jit(solution)/shard_map/ppermute | solution.py:281
  231.3 4.5 %collective-permute-start.16 = (bf16[4,1,256,512]{3,2,1,0:T(8,128)(2,1)}, bf16[4,1,256,512]{3,2,1,0:T(8,128)(2,1)S(1)}, u32[]{:S(2)}, u32[]{:S(2)}) collective-permute-start(bf16[4,1,256,512]{3,2,1,0:T(8,128)(2,1)} %get-tuple-element.86), channel_id=1, source_target_pairs={{0,64},{16,80},{32,96},{48,112},{64,0},{80,16},{96,32},{112,48},{1... | collective-permute-start | bytes 3145736 | tf_op jit(solution)/shard_map/ppermute | solution.py:288
  235.8 2.6 relay.3
  238.4 2.6 relay.2
  241.8 1.9 collective-permute-start.23
  243.6 1.9 collective-permute-start.11
  245.5 7.5 %collective-permute-done.9.a3_ref = bf16[2,1,256,512]{3,2,1,0:T(8,128)(2,1)} collective-permute-done((bf16[2,1,256,512]{3,2,1,0:T(8,128)(2,1)}, bf16[2,1,256,512]{3,2,1,0:T(8,128)(2,1)}, u32[]{:S(2)}, u32[]{:S(2)}) %collective-permute-start.9) | collective-permute-done | bytes 524320 | tf_op jit(solution)/shard_map/ppermute | solution.py:281
  253.0 1.9 collective-permute-start.8
  254.9 1.5 convert_add_fusion
  256.4 7.1 %collective-permute-done.11.b3_ref = bf16[2,1,256,512]{3,2,1,0:T(8,128)(2,1)} collective-permute-done((bf16[2,1,256,512]{3,2,1,0:T(8,128)(2,1)}, bf16[2,1,256,512]{3,2,1,0:T(8,128)(2,1)}, u32[]{:S(2)}, u32[]{:S(2)}) %collective-permute-start.11) | collective-permute-done | bytes 524320 | tf_op jit(solution)/shard_map/ppermute | solution.py:281
  263.5 3.7 %collective-permute-start.26 = (bf16[2,1,512,256]{3,2,1,0:T(8,128)(2,1)}, bf16[2,1,512,256]{3,2,1,0:T(8,128)(2,1)}, u32[]{:S(2)}, u32[]{:S(2)}) collective-permute-start(bf16[2,1,512,256]{3,2,1,0:T(8,128)(2,1)} %get-tuple-element.103), channel_id=1, source_target_pairs={{0,48},{16,0},{32,16},{48,32},{64,112},{80,64},{96,80},{112,96},{1... | collective-permute-start | bytes 1572872 | tf_op jit(solution)/shard_map/ppermute | solution.py:281
  267.2 10.7 %collective-permute-done.8.a1_ref = bf16[2,1,256,512]{3,2,1,0:T(8,128)(2,1)} collective-permute-done((bf16[2,1,256,512]{3,2,1,0:T(8,128)(2,1)}, bf16[2,1,256,512]{3,2,1,0:T(8,128)(2,1)}, u32[]{:S(2)}, u32[]{:S(2)}) %collective-permute-start.8) | collective-permute-done | bytes 524320 | tf_op jit(solution)/shard_map/ppermute | solution.py:281
  277.9 2.1 collective-permute-start.20
  279.9 3.2 %row_sum.2 = (f32[2,256,512]{2,1,0:T(8,128)}, bf16[2,256,512]{2,1,0:T(8,128)(2,1)}) custom-call(bf16[2,2,256,512]{3,2,1,0:T(8,128)(2,1)} %get-tuple-element.70.own_ref, bf16[2,1,256,512]{3,2,1,0:T(8,128)(2,1)} %collective-permute-done.8.a1_ref, bf16[2,1,256,512]{3,2,1,0:T(8,128)(2,1)} %collective-permute-done.9.a3_ref, bf16[2,1,256,512]{3,2,1,0:T(8,128)(2,1)} %copy-done.9, ...), custom_call_target="tpu_custom_call" | custom-call | tf_op jit(solution)/shard_map/row_sum/pallas_call | solution.py:465
  283.2 1.5 collective-permute-start.15
  284.7 2.8 pair_sum.1
  287.5 3.2 %collective-permute-start.18 = (bf16[1,256,512]{2,1,0:T(8,128)(2,1)}, bf16[1,256,512]{2,1,0:T(8,128)(2,1)S(1)}, u32[]{:S(2)}, u32[]{:S(2)}) collective-permute-start(bf16[1,256,512]{2,1,0:T(8,128)(2,1)} %get-tuple-element.88), channel_id=1, source_target_pairs={{0,32},{16,48},{32,0},{48,16},{64,96},{80,112},{96,64},{112,80},{1... | collective-permute-start | bytes 786440 | tf_op jit(solution)/shard_map/ppermute | solution.py:281
  291.9 3.2 %row_sum.3 = (f32[2,512,256]{2,1,0:T(8,128)}, bf16[2,512,256]{2,1,0:T(8,128)(2,1)}) custom-call(bf16[2,2,512,256]{3,2,1,0:T(8,128)(2,1)} %get-tuple-element.95.own_ref, bf16[2,1,512,256]{3,2,1,0:T(8,128)(2,1)} %collective-permute-done.23.a1_ref, bf16[2,1,512,256]{3,2,1,0:T(8,128)(2,1)} %copy-done.7, bf16[2,1,512,256]{3,2,1,0:T(8,128)(2,1)} %collective-permute-done.25.b1_ref, ...), custom_call_target="tpu_custom_call" | custom-call | tf_op jit(solution)/shard_map/row_sum/pallas_call | solution.py:465
  295.1 2.1 collective-permute-start.27
  297.2 4.5 %collective-permute-done.17 = bf16[1,256,512]{2,1,0:T(8,128)(2,1)} collective-permute-done((bf16[1,256,512]{2,1,0:T(8,128)(2,1)}, bf16[1,256,512]{2,1,0:T(8,128)(2,1)}, u32[]{:S(2)}, u32[]{:S(2)}) %collective-permute-start.17) | collective-permute-done | bytes 262176 | tf_op jit(solution)/shard_map/ppermute | solution.py:281
  304.9 2.0 add_convert_fusion.1
  306.9 2.4 collective-permute-done.27
  310.3 3.5 %ngrad.1 = bf16[128,2048]{1,0:T(8,128)(2,1)} custom-call(bf16[16,4,16,2048]{3,2,1,0:T(8,128)(2,1)} %all-to-all-done.3.back_ref, bf16[512,128]{1,0:T(8,128)(2,1)} %get-tuple-element.62.pick0_ref, bf16[512,128]{1,0:T(8,128)(2,1)} %get-tuple-element.63.pick1_ref), custom_call_target="tpu_custom_call" | custom-call | tf_op jit(solution)/shard_map/ngrad/pallas_call | solution.py:457
  313.8 3.8 %mixed.1 = bf16[128,2048]{1,0:T(8,128)(2,1)} custom-call(bf16[16,4,16,2048]{3,2,1,0:T(8,128)(2,1)} %all-to-all-done.3.back_ref, bf16[512,128]{1,0:T(8,128)(2,1)} %get-tuple-element.62.pick0_ref, bf16[512,128]{1,0:T(8,128)(2,1)} %get-tuple-element.63.pick1_ref, f32[128,2]{1,0:T(8,128)} %copy.17.gates_ref), custom_call_target="tpu_custom_call" | custom-call | tf_op jit(solution)/shard_map/mixed/pallas_call | solution.py:454
  (59 shorter events, 7.0 us)
Async XLA Ops:
  3.2 28.5 %collective-permute-start = (bf16[2,2048,128]{2,1,0:T(8,128)(2,1)}, bf16[2,2048,128]{2,1,0:T(8,128)(2,1)}, u32[]{:S(2)}, u32[]{:S(2)}) collective-permute-start(bf16[2,2048,128]{2,1,0:T(8,128)(2,1)} %get-tuple-element.107.kv), channel_id=1, source_target_pairs={{0,16},{16,32},{32,48},{48,0},{64,80},{80,96},{96,112},{1,17},{17,... | collective-permute-start | bytes 3145736 | tf_op jit(solution)/shard_map/ppermute | solution.py:281
  6.8 27.1 %collective-permute-start.2 = (bf16[2,2048,128]{2,1,0:T(8,128)(2,1)S(1)}, bf16[2,2048,128]{2,1,0:T(8,128)(2,1)S(1)}, u32[]{:S(2)}, u32[]{:S(2)}) collective-permute-start(bf16[2,2048,128]{2,1,0:T(8,128)(2,1)S(1)} %get-tuple-element.106), channel_id=1, source_target_pairs={{0,64},{16,80},{32,96},{48,112},{64,0},{80,16},{96,32},{112,48},{1... | collective-permute-start | bytes 3145736 | tf_op jit(solution)/shard_map/ppermute | solution.py:288
  10.8 43.2 %collective-permute-start.4 = (bf16[2,2048,128]{2,1,0:T(8,128)(2,1)}, bf16[2,2048,128]{2,1,0:T(8,128)(2,1)}, u32[]{:S(2)}, u32[]{:S(2)}) collective-permute-start(bf16[2,2048,128]{2,1,0:T(8,128)(2,1)} %get-tuple-element.107.kv), channel_id=1, source_target_pairs={{0,48},{64,112},{1,49},{65,113},{2,50},{66,114},{3,51},{67,115},{4... | collective-permute-start | bytes 3145736 | tf_op jit(solution)/shard_map/ppermute | solution.py:281
  31.7 32.3 %collective-permute-start.1 = (bf16[2,2048,128]{2,1,0:T(8,128)(2,1)}, bf16[2,2048,128]{2,1,0:T(8,128)(2,1)}, u32[]{:S(2)}, u32[]{:S(2)}) collective-permute-start(bf16[2,2048,128]{2,1,0:T(8,128)(2,1)} %collective-permute-done.refs_3_), channel_id=1, source_target_pairs={{0,16},{16,32},{32,48},{48,0},{80,96},{96,112},{1,17},{17,33},{33,... | collective-permute-start | bytes 3145736 | tf_op jit(solution)/shard_map/ppermute | solution.py:281
  33.9 20.1 %copy-start.2 = (bf16[2,2048,128]{2,1,0:T(8,128)(2,1)}, bf16[2,2048,128]{2,1,0:T(8,128)(2,1)S(1)}, u32[]{:S(2)}) copy-start(bf16[2,2048,128]{2,1,0:T(8,128)(2,1)S(1)} %collective-permute-done.2.refs_2_.refs_4_) | copy-start | bytes 3145732
  33.9 30.1 %collective-permute-start.3 = (bf16[2,2048,128]{2,1,0:T(8,128)(2,1)S(1)}, bf16[2,2048,128]{2,1,0:T(8,128)(2,1)}, u32[]{:S(2)}, u32[]{:S(2)}) collective-permute-start(bf16[2,2048,128]{2,1,0:T(8,128)(2,1)S(1)} %collective-permute-done.2.refs_2_.refs_4_), channel_id=1, source_target_pairs={{64,112},{80,64},{96,80},{112,96},{65,113},{81,65},{97,81},{113,97... | collective-permute-start | bytes 3145736 | tf_op jit(solution)/shard_map/ppermute | solution.py:281
  40.9 52.0 %all-to-all-start = ((bf16[16,32,2048]{2,1,0:T(8,128)(2,1)}), bf16[16,32,2048]{2,1,0:T(8,128)(2,1)S(1)}, u32[]{:S(2)}, u32[]{:S(2)}) async-start(bf16[16,32,2048]{2,1,0:T(8,128)(2,1)} %get-tuple-element.60), calls=%async_computation | async-start | bytes 4194304 | tf_op jit(solution)/shard_map/all_to_all | solution.py:313
  73.8 17.8 %collective-permute-start.5 = (bf16[2048,128]{1,0:T(8,128)(2,1)}, bf16[2048,128]{1,0:T(8,128)(2,1)S(1)}, u32[]{:S(2)}, u32[]{:S(2)}) collective-permute-start(bf16[2048,128]{1,0:T(8,128)(2,1)} %get-tuple-element.59), channel_id=1, source_target_pairs={{0,64},{16,80},{32,96},{48,112},{1,65},{17,81},{33,97},{49,113},{2... | collective-permute-start | bytes 1572872 | tf_op jit(solution)/shard_map/ppermute | solution.py:381
  92.9 19.2 %copy-start.1 = (bf16[16,32,2048]{2,1,0:T(8,128)(2,1)}, bf16[16,32,2048]{2,1,0:T(8,128)(2,1)S(1)}, u32[]{:S(2)}) copy-start(bf16[16,32,2048]{2,1,0:T(8,128)(2,1)S(1)} %all-to-all-done.grad_ref.src) | copy-start | bytes 6291460
  112.1 31.5 %all-to-all-start.2 = ((bf16[16,32,2048]{2,1,0:T(8,128)(2,1)}), bf16[16,32,2048]{2,1,0:T(8,128)(2,1)S(1)}, u32[]{:S(2)}, u32[]{:S(2)}) async-start(bf16[16,32,2048]{2,1,0:T(8,128)(2,1)} %get-tuple-element.65), calls=%async_computation.2 | async-start | bytes 4194304 | tf_op jit(solution)/shard_map/all_to_all | solution.py:313
  143.6 1.3 copy-start
  161.6 148.7 %all-to-all-start.3 = ((bf16[16,4,16,2048]{3,2,1,0:T(8,128)(2,1)}), bf16[16,4,16,2048]{3,2,1,0:T(8,128)(2,1)}, u32[]{:S(2)}, u32[]{:S(2)}) async-start(bf16[16,4,16,2048]{3,2,1,0:T(8,128)(2,1)} %expert_back.1), calls=%async_computation.3 | async-start | bytes 8388608 | tf_op jit(solution)/shard_map/all_to_all | solution.py:313
  170.3 26.9 %collective-permute-start.21 = (bf16[2,1,512,256]{3,2,1,0:T(8,128)(2,1)}, bf16[2,1,512,256]{3,2,1,0:T(8,128)(2,1)S(1)}, u32[]{:S(2)}, u32[]{:S(2)}) collective-permute-start(bf16[2,1,512,256]{3,2,1,0:T(8,128)(2,1)} %get-tuple-element.97), channel_id=1, source_target_pairs={{0,16},{16,32},{32,48},{48,0},{64,80},{80,96},{96,112},{112,64},{1... | collective-permute-start | bytes 1572872 | tf_op jit(solution)/shard_map/ppermute | solution.py:281
  177.6 21.6 %collective-permute-start.22 = (bf16[2,1,512,256]{3,2,1,0:T(8,128)(2,1)}, bf16[2,1,512,256]{3,2,1,0:T(8,128)(2,1)S(1)}, u32[]{:S(2)}, u32[]{:S(2)}) collective-permute-start(bf16[2,1,512,256]{3,2,1,0:T(8,128)(2,1)} %get-tuple-element.99), channel_id=1, source_target_pairs={{0,48},{16,0},{32,16},{48,32},{64,112},{80,64},{96,80},{112,96},{1... | collective-permute-start | bytes 1572872 | tf_op jit(solution)/shard_map/ppermute | solution.py:281
  184.2 23.9 %collective-permute-start.24 = (bf16[2,1,512,256]{3,2,1,0:T(8,128)(2,1)}, bf16[2,1,512,256]{3,2,1,0:T(8,128)(2,1)S(1)}, u32[]{:S(2)}, u32[]{:S(2)}) collective-permute-start(bf16[2,1,512,256]{3,2,1,0:T(8,128)(2,1)} %get-tuple-element.101), channel_id=1, source_target_pairs={{0,48},{16,0},{32,16},{48,32},{64,112},{80,64},{96,80},{112,96},{1... | collective-permute-start | bytes 1572872 | tf_op jit(solution)/shard_map/ppermute | solution.py:281
  190.6 64.3 %copy-start.8 = (bf16[2,1,256,512]{3,2,1,0:T(8,128)(2,1)S(1)}, bf16[2,1,256,512]{3,2,1,0:T(8,128)(2,1)}, u32[]{:S(2)}) copy-start(bf16[2,1,256,512]{3,2,1,0:T(8,128)(2,1)} %get-tuple-element.80) | copy-start | bytes 1572868
  190.6 21.1 %collective-permute-start.12 = (bf16[2,1,256,512]{3,2,1,0:T(8,128)(2,1)}, bf16[2,1,256,512]{3,2,1,0:T(8,128)(2,1)S(1)}, u32[]{:S(2)}, u32[]{:S(2)}) collective-permute-start(bf16[2,1,256,512]{3,2,1,0:T(8,128)(2,1)} %get-tuple-element.81), channel_id=1, source_target_pairs={{0,16},{16,32},{32,48},{48,0},{64,80},{80,96},{96,112},{112,64},{1... | collective-permute-start | bytes 1572872 | tf_op jit(solution)/shard_map/ppermute | solution.py:281
  194.9 24.7 %collective-permute-start.6 = (bf16[2,1,256,512]{3,2,1,0:T(8,128)(2,1)}, bf16[2,1,256,512]{3,2,1,0:T(8,128)(2,1)S(1)}, u32[]{:S(2)}, u32[]{:S(2)}) collective-permute-start(bf16[2,1,256,512]{3,2,1,0:T(8,128)(2,1)} %get-tuple-element.72), channel_id=1, source_target_pairs={{0,16},{16,32},{32,48},{48,0},{64,80},{80,96},{96,112},{112,64},{1... | collective-permute-start | bytes 1572872 | tf_op jit(solution)/shard_map/ppermute | solution.py:281
  197.2 14.5 %copy-start.10 = (bf16[2,1,512,256]{3,2,1,0:T(8,128)(2,1)}, bf16[2,1,512,256]{3,2,1,0:T(8,128)(2,1)S(1)}, u32[]{:S(2)}) copy-start(bf16[2,1,512,256]{3,2,1,0:T(8,128)(2,1)S(1)} %collective-permute-done.21.far1_ref) | copy-start | bytes 1572868
  197.2 33.4 %collective-permute-start.7 = (bf16[2,1,256,512]{3,2,1,0:T(8,128)(2,1)}, bf16[2,1,256,512]{3,2,1,0:T(8,128)(2,1)S(1)}, u32[]{:S(2)}, u32[]{:S(2)}) collective-permute-start(bf16[2,1,256,512]{3,2,1,0:T(8,128)(2,1)} %get-tuple-element.74), channel_id=1, source_target_pairs={{0,48},{16,0},{32,16},{48,32},{64,112},{80,64},{96,80},{112,96},{1... | collective-permute-start | bytes 1572872 | tf_op jit(solution)/shard_map/ppermute | solution.py:281
  199.2 31.3 %copy-start.11 = (bf16[2,1,512,256]{3,2,1,0:T(8,128)(2,1)}, bf16[2,1,512,256]{3,2,1,0:T(8,128)(2,1)S(1)}, u32[]{:S(2)}) copy-start(bf16[2,1,512,256]{3,2,1,0:T(8,128)(2,1)S(1)} %collective-permute-done.22.far3_ref) | copy-start | bytes 1572868
  199.2 41.8 %collective-permute-start.13 = (bf16[2,1,256,512]{3,2,1,0:T(8,128)(2,1)}, bf16[2,1,256,512]{3,2,1,0:T(8,128)(2,1)}, u32[]{:S(2)}, u32[]{:S(2)}) collective-permute-start(bf16[2,1,256,512]{3,2,1,0:T(8,128)(2,1)} %get-tuple-element.82), channel_id=1, source_target_pairs={{0,32},{16,48},{32,0},{48,16},{64,96},{80,112},{96,64},{112,80},{1... | collective-permute-start | bytes 1572872 | tf_op jit(solution)/shard_map/ppermute | solution.py:281
  208.1 46.8 %copy-start.7 = (bf16[2,1,512,256]{3,2,1,0:T(8,128)(2,1)}, bf16[2,1,512,256]{3,2,1,0:T(8,128)(2,1)S(1)}, u32[]{:S(2)}) copy-start(bf16[2,1,512,256]{3,2,1,0:T(8,128)(2,1)S(1)} %collective-permute-done.24.a3_ref) | copy-start | bytes 1572868
  208.1 33.7 %collective-permute-start.14 = (bf16[2,1,256,512]{3,2,1,0:T(8,128)(2,1)}, bf16[2,1,256,512]{3,2,1,0:T(8,128)(2,1)}, u32[]{:S(2)}, u32[]{:S(2)}) collective-permute-start(bf16[2,1,256,512]{3,2,1,0:T(8,128)(2,1)} %get-tuple-element.83), channel_id=1, source_target_pairs={{0,48},{16,0},{32,16},{48,32},{64,112},{80,64},{96,80},{112,96},{1... | collective-permute-start | bytes 1572872 | tf_op jit(solution)/shard_map/ppermute | solution.py:281
  211.7 32.0 %collective-permute-start.10 = (bf16[2,1,256,512]{3,2,1,0:T(8,128)(2,1)}, bf16[2,1,256,512]{3,2,1,0:T(8,128)(2,1)S(1)}, u32[]{:S(2)}, u32[]{:S(2)}) collective-permute-start(bf16[2,1,256,512]{3,2,1,0:T(8,128)(2,1)} %get-tuple-element.77), channel_id=1, source_target_pairs={{0,16},{16,32},{32,48},{48,0},{64,80},{80,96},{96,112},{112,64},{1... | collective-permute-start | bytes 1572872 | tf_op jit(solution)/shard_map/ppermute | solution.py:281
  219.7 10.9 %copy-start.12 = (bf16[2,1,256,512]{3,2,1,0:T(8,128)(2,1)}, bf16[2,1,256,512]{3,2,1,0:T(8,128)(2,1)S(1)}, u32[]{:S(2)}) copy-start(bf16[2,1,256,512]{3,2,1,0:T(8,128)(2,1)S(1)} %collective-permute-done.6.far1_ref) | copy-start | bytes 1572868
  219.7 33.3 %collective-permute-start.9 = (bf16[2,1,256,512]{3,2,1,0:T(8,128)(2,1)}, bf16[2,1,256,512]{3,2,1,0:T(8,128)(2,1)}, u32[]{:S(2)}, u32[]{:S(2)}) collective-permute-start(bf16[2,1,256,512]{3,2,1,0:T(8,128)(2,1)} %get-tuple-element.76), channel_id=1, source_target_pairs={{0,48},{16,0},{32,16},{48,32},{64,112},{80,64},{96,80},{112,96},{1... | collective-permute-start | bytes 1572872 | tf_op jit(solution)/shard_map/ppermute | solution.py:281
  230.5 0.8 copy-start.13
  231.3 51.9 %collective-permute-start.16 = (bf16[4,1,256,512]{3,2,1,0:T(8,128)(2,1)}, bf16[4,1,256,512]{3,2,1,0:T(8,128)(2,1)S(1)}, u32[]{:S(2)}, u32[]{:S(2)}) collective-permute-start(bf16[4,1,256,512]{3,2,1,0:T(8,128)(2,1)} %get-tuple-element.86), channel_id=1, source_target_pairs={{0,64},{16,80},{32,96},{48,112},{64,0},{80,16},{96,32},{112,48},{1... | collective-permute-start | bytes 3145736 | tf_op jit(solution)/shard_map/ppermute | solution.py:288
  241.0 46.4 %collective-permute-start.25 = (bf16[2,1,512,256]{3,2,1,0:T(8,128)(2,1)}, bf16[2,1,512,256]{3,2,1,0:T(8,128)(2,1)}, u32[]{:S(2)}, u32[]{:S(2)}) collective-permute-start(bf16[2,1,512,256]{3,2,1,0:T(8,128)(2,1)} %get-tuple-element.102), channel_id=1, source_target_pairs={{0,16},{16,32},{32,48},{48,0},{64,80},{80,96},{96,112},{112,64},{1... | collective-permute-start | bytes 1572872 | tf_op jit(solution)/shard_map/ppermute | solution.py:281
  241.8 48.9 %collective-permute-start.23 = (bf16[2,1,512,256]{3,2,1,0:T(8,128)(2,1)}, bf16[2,1,512,256]{3,2,1,0:T(8,128)(2,1)}, u32[]{:S(2)}, u32[]{:S(2)}) collective-permute-start(bf16[2,1,512,256]{3,2,1,0:T(8,128)(2,1)} %get-tuple-element.100), channel_id=1, source_target_pairs={{0,16},{16,32},{32,48},{48,0},{64,80},{80,96},{96,112},{112,64},{1... | collective-permute-start | bytes 1572872 | tf_op jit(solution)/shard_map/ppermute | solution.py:281
  243.6 11.2 %copy-start.9 = (bf16[2,1,256,512]{3,2,1,0:T(8,128)(2,1)}, bf16[2,1,256,512]{3,2,1,0:T(8,128)(2,1)S(1)}, u32[]{:S(2)}) copy-start(bf16[2,1,256,512]{3,2,1,0:T(8,128)(2,1)S(1)} %collective-permute-done.10.b1_ref) | copy-start | bytes 1572868
  243.6 19.8 %collective-permute-start.11 = (bf16[2,1,256,512]{3,2,1,0:T(8,128)(2,1)}, bf16[2,1,256,512]{3,2,1,0:T(8,128)(2,1)}, u32[]{:S(2)}, u32[]{:S(2)}) collective-permute-start(bf16[2,1,256,512]{3,2,1,0:T(8,128)(2,1)} %get-tuple-element.78), channel_id=1, source_target_pairs={{0,48},{16,0},{32,16},{48,32},{64,112},{80,64},{96,80},{112,96},{1... | collective-permute-start | bytes 1572872 | tf_op jit(solution)/shard_map/ppermute | solution.py:281
  253.0 24.9 %collective-permute-start.8 = (bf16[2,1,256,512]{3,2,1,0:T(8,128)(2,1)}, bf16[2,1,256,512]{3,2,1,0:T(8,128)(2,1)}, u32[]{:S(2)}, u32[]{:S(2)}) collective-permute-start(bf16[2,1,256,512]{3,2,1,0:T(8,128)(2,1)} %get-tuple-element.75), channel_id=1, source_target_pairs={{0,16},{16,32},{32,48},{48,0},{64,80},{80,96},{96,112},{112,64},{1... | collective-permute-start | bytes 1572872 | tf_op jit(solution)/shard_map/ppermute | solution.py:281
  263.5 28.4 %collective-permute-start.26 = (bf16[2,1,512,256]{3,2,1,0:T(8,128)(2,1)}, bf16[2,1,512,256]{3,2,1,0:T(8,128)(2,1)}, u32[]{:S(2)}, u32[]{:S(2)}) collective-permute-start(bf16[2,1,512,256]{3,2,1,0:T(8,128)(2,1)} %get-tuple-element.103), channel_id=1, source_target_pairs={{0,48},{16,0},{32,16},{48,32},{64,112},{80,64},{96,80},{112,96},{1... | collective-permute-start | bytes 1572872 | tf_op jit(solution)/shard_map/ppermute | solution.py:281
  277.9 9.6 %collective-permute-start.20 = (bf16[1,256,512]{2,1,0:T(8,128)(2,1)S(1)}, bf16[1,256,512]{2,1,0:T(8,128)(2,1)}, u32[]{:S(2)}, u32[]{:S(2)}) collective-permute-start(bf16[1,256,512]{2,1,0:T(8,128)(2,1)S(1)} %fusion.2), channel_id=1, source_target_pairs={{0,64},{16,80},{32,96},{48,112},{64,0},{80,16},{96,32},{112,48},{1... | collective-permute-start | bytes 786440 | tf_op jit(solution)/shard_map/ppermute | solution.py:288
  283.2 1.5 copy-start.3
  283.2 19.0 %collective-permute-start.15 = (bf16[2,256,512]{2,1,0:T(8,128)(2,1)}, bf16[2,256,512]{2,1,0:T(8,128)(2,1)}, u32[]{:S(2)}, u32[]{:S(2)}) collective-permute-start(bf16[2,256,512]{2,1,0:T(8,128)(2,1)} %get-tuple-element.84), channel_id=1, source_target_pairs={{0,64},{16,80},{32,96},{48,112},{64,0},{80,16},{96,32},{112,48},{1... | collective-permute-start | bytes 1572872 | tf_op jit(solution)/shard_map/ppermute | solution.py:288
  284.7 20.3 %copy-start.4 = (f32[2,256,512]{2,1,0:T(8,128)S(1)}, f32[2,256,512]{2,1,0:T(8,128)}, u32[]{:S(2)}) copy-start(f32[2,256,512]{2,1,0:T(8,128)} %get-tuple-element.79) | copy-start | bytes 3145732
  287.4 15.5 %copy-start.6 = (f32[1,256,512]{2,1,0:T(8,128)S(1)}, f32[1,256,512]{2,1,0:T(8,128)}, u32[]{:S(2)}) copy-start(f32[1,256,512]{2,1,0:T(8,128)} %get-tuple-element.91) | copy-start | bytes 1572868
  287.4 14.3 %collective-permute-start.17 = (bf16[1,256,512]{2,1,0:T(8,128)(2,1)}, bf16[1,256,512]{2,1,0:T(8,128)(2,1)}, u32[]{:S(2)}, u32[]{:S(2)}) collective-permute-start(bf16[1,256,512]{2,1,0:T(8,128)(2,1)} %get-tuple-element.87), channel_id=1, source_target_pairs={{0,16},{16,32},{32,48},{48,0},{64,80},{80,96},{96,112},{112,64},{1... | collective-permute-start | bytes 786440 | tf_op jit(solution)/shard_map/ppermute | solution.py:281
  287.5 14.2 %collective-permute-start.18 = (bf16[1,256,512]{2,1,0:T(8,128)(2,1)}, bf16[1,256,512]{2,1,0:T(8,128)(2,1)S(1)}, u32[]{:S(2)}, u32[]{:S(2)}) collective-permute-start(bf16[1,256,512]{2,1,0:T(8,128)(2,1)} %get-tuple-element.88), channel_id=1, source_target_pairs={{0,32},{16,48},{32,0},{48,16},{64,96},{80,112},{96,64},{112,80},{1... | collective-permute-start | bytes 786440 | tf_op jit(solution)/shard_map/ppermute | solution.py:281
  290.7 11.5 %collective-permute-start.19 = (bf16[1,256,512]{2,1,0:T(8,128)(2,1)}, bf16[1,256,512]{2,1,0:T(8,128)(2,1)S(1)}, u32[]{:S(2)}, u32[]{:S(2)}) collective-permute-start(bf16[1,256,512]{2,1,0:T(8,128)(2,1)} %get-tuple-element.89), channel_id=1, source_target_pairs={{0,48},{16,0},{32,16},{48,32},{64,112},{80,64},{96,80},{112,96},{1... | collective-permute-start | bytes 786440 | tf_op jit(solution)/shard_map/ppermute | solution.py:281
  295.1 14.3 %copy-start.5 = (f32[2,512,256]{2,1,0:T(8,128)S(1)}, f32[2,512,256]{2,1,0:T(8,128)}, u32[]{:S(2)}) copy-start(f32[2,512,256]{2,1,0:T(8,128)} %get-tuple-element.104) | copy-start | bytes 3145732
  295.1 14.3 %collective-permute-start.27 = (bf16[2,512,256]{2,1,0:T(8,128)(2,1)}, bf16[2,512,256]{2,1,0:T(8,128)(2,1)S(1)}, u32[]{:S(2)}, u32[]{:S(2)}) collective-permute-start(bf16[2,512,256]{2,1,0:T(8,128)(2,1)} %get-tuple-element.105), channel_id=1, source_target_pairs={{0,64},{16,80},{32,96},{48,112},{64,0},{80,16},{96,32},{112,48},{1... | collective-permute-start | bytes 1572872 | tf_op jit(solution)/shard_map/ppermute | solution.py:288
  302.2 0.7 copy-start.14
